TPU v7x, 256 devices: a whole 4x4x8 slice. The times are simulated.
256 devices in a mesh: depth: 64 (over z, x, core), lat: 4 (over y).
Axes of the slice: x: 4, y: 4, z: 8, core: 2. Of those that a mesh axis runs over, the one named last changes fastest.
Arguments:
- phase: float32 [2048, 256, 128], P('depth', 'lat'), may hold values from 0 to 1
- temper: float32 [2048, 256, 128], P('depth', 'lat'), may hold values from -3 to 3
- iface_count: int32 [64, 4], P('depth', 'lat'), may hold values from 1 to 32, as said below
Outputs:
- phase_next: float32 [2048, 256, 128], P('depth', 'lat')
- heat_next: float32 [2048, 256, 128], P('depth', 'lat')
- picture: float32 [4, 256, 512], P(None, 'lat', 'depth')
Inputs may be any that keep to these rules, and one draw needn't show every extreme that they name: `iface_count`: per brick a count of 1 to 32; some brick has exactly 32 and another exactly 1.
All inputs are finite; a program needn't handle non-finite values.
Results may differ from a plain program's by a relative error of at most 0.0003.
Values sent between devices are 32-bit elements; how exact they have to be, the bound alone decides.
No kernel may reach another device: no remote copies, remote signals or barrier semaphores. Data moves between devices by JAX's collectives and lax.ppermute only.
A program may use at most 64 MiB of HBM per device.

v0:
```python
import math

import jax
import jax.numpy as jnp
import numpy as np
from jax import lax
from jax.sharding import PartitionSpec as P

SWEEPS = 3


DIFFUSION = (0.5, 2.0)
TIME_STEP = 0.4
COUPLE = 0.6
LATENT = 0.5
SHEAR_Y = (1.6, -1.6, 0.8, -1.2)
SHEAR_Z = (0.9, -0.6, -0.9, 0.3)
CENTERS = (-0.8, 0.0, 0.8)


def with_halo(block, sides, width):
    for axis, dim in sides:
        count = lax.axis_size(axis)
        forward = [(i, i + 1) for i in range(count - 1)]
        backward = [(target, source) for source, target in forward]
        low = lax.ppermute(
            lax.slice_in_dim(block, block.shape[dim] - width, None, axis=dim), axis, forward
        )
        high = lax.ppermute(lax.slice_in_dim(block, 0, width, axis=dim), axis, backward)
        block = jnp.concatenate([low, block, high], axis=dim)
    return block


def from_partner(shard, axis, apart):
    return lax.ppermute(shard, axis, [(i, i ^ 1 << apart) for i in range(lax.axis_size(axis))])


def thetas(sweep_total):
    chebyshev = []
    for f in range(2):
        highest = 1.0 + 12.0 * DIFFUSION[f]
        entries = [
            0.5 * (highest + 1.0)
            + 0.5 * (highest - 1.0) * math.cos((2 * j + 1) * math.pi / (2 * sweep_total))
            for j in range(sweep_total)
        ]
        chebyshev.append(entries)
    return np.array(chebyshev)


def stencil(padded):
    summed = padded[:, 2:, 1:-1, 1:-1] + padded[:, :-2, 1:-1, 1:-1]
    summed = summed + padded[:, 1:-1, 2:, 1:-1] + padded[:, 1:-1, :-2, 1:-1]
    summed = summed + padded[:, 1:-1, 1:-1, 2:] + padded[:, 1:-1, 1:-1, :-2]
    return summed


def sources(phase, temper):
    reaction = phase * (1.0 - phase) * (phase - 0.5 + COUPLE * temper)
    return jnp.stack([phase + TIME_STEP * reaction, temper + LATENT * TIME_STEP * reaction])


def relax(current, source, diffusion, step_size, padded):
    applied = current + diffusion * (6.0 * current - stencil(padded))
    return current + (source - applied) / step_size


def tap_table(layers, shear, lowest, count):
    table = np.zeros((count, layers))
    for x in range(layers):
        offset = shear * x / layers
        whole_part = int(np.floor(offset))
        fraction = offset - whole_part
        table[whole_part - lowest, x] += 1.0 - fraction
        table[whole_part + 1 - lowest, x] += fraction
    return table


def footprint(rim, layer_mask, opacity_scale):
    layers = rim.shape[1]
    row_count = rim.shape[2] - 4
    zero_col = jnp.zeros(rim.shape[:3] + (1,), jnp.float32)
    ahead = jnp.concatenate([rim[..., 1:], zero_col], axis=3)
    behind = jnp.concatenate([zero_col, rim[..., :-1]], axis=3)
    shifted = (behind, rim, ahead)
    pictures = []
    for v in range(len(SHEAR_Y)):
        z_table = tap_table(layers, SHEAR_Z[v], -1, 3)
        y_table = tap_table(layers, SHEAR_Y[v], -2, 5)
        columns = None
        for t in range(3):
            if np.any(z_table[t] != 0.0):
                term = jnp.asarray(z_table[t], jnp.float32).reshape(1, layers, 1, 1) * shifted[t]
                columns = term if columns is None else columns + term
        sampled = None
        for t in range(5):
            if np.any(y_table[t] != 0.0):
                term = (
                    jnp.asarray(y_table[t], jnp.float32).reshape(1, layers, 1, 1)
                    * columns[:, :, t : t + row_count, :]
                )
                sampled = term if sampled is None else sampled + term
        thickness = opacity_scale * sampled[0] * sampled[0] * layer_mask[:, :, None]
        optical = jnp.cumsum(thickness, axis=0)
        weight = jnp.exp(-(optical - thickness)) * (1.0 - jnp.exp(-thickness))
        colours = []
        for centre in CENTERS:
            distance = sampled[1] - centre
            colours.append(jnp.sum(weight / (1.0 + distance * distance), axis=0))
        colours.append(jnp.exp(-optical[-1]))
        pictures.append(jnp.stack(colours))
    return jnp.concatenate(pictures, axis=2)


def over_blend(in_front, behind):
    return jnp.concatenate(
        [in_front[:3] + in_front[3:] * behind[:3], in_front[3:] * behind[3:]], axis=0
    )


def per_device(phase, temper, iface_count):
    layers = phase.shape[0]
    row_count = phase.shape[1]
    depth_size = lax.axis_size("depth")
    current = jnp.stack([phase, temper])
    chebyshev = thetas(SWEEPS)
    diffusion = jnp.asarray(np.array(DIFFUSION), jnp.float32).reshape(2, 1, 1, 1)
    source = sources(phase, temper)
    for k in range(SWEEPS):
        padded = with_halo(current, (("depth", 1), ("lat", 2)), 1)
        padded = jnp.pad(padded, ((0, 0), (0, 0), (0, 0), (1, 1)))
        step_size = jnp.asarray(chebyshev[:, k], jnp.float32).reshape(2, 1, 1, 1)
        current = relax(current, source, diffusion, step_size, padded)
    rim_fields = with_halo(current, (("lat", 2),), 2)
    layer_count = iface_count[0, 0]
    layer_mask = (jnp.arange(layers)[:, None] < layer_count).astype(jnp.float32)
    picture = footprint(rim_fields, layer_mask, 4.0 / (layers * depth_size))
    pixels = picture.shape[2]
    bit_count = depth_size.bit_length() - 1
    block_width = pixels >> bit_count
    shaped = picture.reshape((4, row_count) + (2,) * bit_count + (block_width,))
    permuted = (0, 1) + tuple(range(bit_count + 1, 1, -1)) + (bit_count + 2,)
    picture = jnp.transpose(shaped, permuted).reshape(4, row_count, pixels)
    my_index = lax.axis_index("depth")
    for b in range(bit_count):
        half_width = picture.shape[2] // 2
        front_half = picture[:, :, :half_width]
        second = picture[:, :, half_width:]
        upper_bit = my_index >> b & 1 == 1
        kept_half = jnp.where(upper_bit, second, front_half)
        sent_half = jnp.where(upper_bit, front_half, second)
        partner = from_partner(sent_half, "depth", b)
        in_front = jnp.where(upper_bit, partner, kept_half)
        behind = jnp.where(upper_bit, kept_half, partner)
        picture = over_blend(in_front, behind)
    return (current[0], current[1], picture)


def solution(mesh):
    return jax.shard_map(
        per_device,
        mesh=mesh,
        in_specs=(P("depth", "lat", None), P("depth", "lat", None), P("depth", "lat")),
        out_specs=(P("depth", "lat", None), P("depth", "lat", None), P(None, "lat", "depth")),
        check_vma=False,
    )
```

profile of v0, /device:TPU:8, one launch (start us, length us, event | category | flops | bytes accessed | tf_op | source)
XLA Modules:
  0.0 146.4 jit_solution(5661607904056935641)
XLA Ops:
  0.6 1.0 fusion.74
  1.6 1.7 %collective-permute-start.1 = (f32[2,1,64,128]{3,2,1,0:T(8,128)S(1)}, f32[2,1,64,128]{3,2,1,0:T(8,128)S(1)}, u32[]{:S(2)}, u32[]{:S(2)}) collective-permute-start(f32[2,1,64,128]{3,2,1,0:T(8,128)S(1)} %get-tuple-element.37), channel_id=1, source_target_pairs={{0,4},{4,8},{8,12},{12,16},{16,20},{20,24},{24,28},{28,32},{32,36}... | collective-permute-start | bytes 196616 | tf_op jit(solution)/shard_map/ppermute | solution.py:26
  3.4 1.3 collective-permute-start
  4.7 3.1 %collective-permute-done = f32[2,1,64,128]{3,2,1,0:T(8,128)S(1)} collective-permute-done((f32[2,1,64,128]{3,2,1,0:T(8,128)S(1)}, f32[2,1,64,128]{3,2,1,0:T(8,128)S(1)}, u32[]{:S(2)}, u32[]{:S(2)}) %collective-permute-start) | collective-permute-done | bytes 65568 | tf_op jit(solution)/shard_map/ppermute | solution.py:29
  7.9 3.5 %collective-permute-start.3 = (f32[2,34,1,128]{3,2,1,0:T(1,128)S(1)}, f32[2,34,1,128]{3,2,1,0:T(1,128)S(1)}, u32[]{:S(2)}, u32[]{:S(2)}) collective-permute-start(f32[2,34,1,128]{3,2,1,0:T(1,128)S(1)} %get-tuple-element.25), channel_id=1, source_target_pairs={{0,1},{1,2},{2,3},{4,5},{5,6},{6,7},{8,9},{9,10},{10,11},{12,13},{... | collective-permute-start | bytes 104456 | tf_op jit(solution)/shard_map/ppermute | solution.py:26
  11.3 2.4 %collective-permute-start.2 = (f32[2,34,1,128]{3,2,1,0:T(1,128)S(1)}, f32[2,34,1,128]{3,2,1,0:T(1,128)S(1)}, u32[]{:S(2)}, u32[]{:S(2)}) collective-permute-start(f32[2,34,1,128]{3,2,1,0:T(1,128)S(1)} %get-tuple-element.26), channel_id=1, source_target_pairs={{1,0},{2,1},{3,2},{5,4},{6,5},{7,6},{9,8},{10,9},{11,10},{13,12},{... | collective-permute-start | bytes 104456 | tf_op jit(solution)/shard_map/ppermute | solution.py:29
  14.1 3.1 %collective-permute-done.2 = f32[2,34,1,128]{3,2,1,0:T(1,128)S(1)} collective-permute-done((f32[2,34,1,128]{3,2,1,0:T(1,128)S(1)}, f32[2,34,1,128]{3,2,1,0:T(1,128)S(1)}, u32[]{:S(2)}, u32[]{:S(2)}) %collective-permute-start.2) | collective-permute-done | bytes 34848 | tf_op jit(solution)/shard_map/ppermute | solution.py:29
  17.2 4.1 %select_maximum_fusion.8 = f32[2,34,66,130]{3,2,1,0:T(8,128)S(1)} fusion(f32[2,34,1,128]{3,2,1,0:T(1,128)S(1)} %collective-permute-done.2, f32[2,34,1,128]{3,2,1,0:T(1,128)S(1)} %collective-permute-done.3, f32[2,1,64,128]{3,2,1,0:T(8,128)S(1)} %collective-permute-done, f32[2,1,64,128]{3,2,1,0:T(8,128)S(1)} %collective-permute-done.1, ...), kind=kLoop, calls=%fused_computation.10 | loop fusion | flops 8168160 | bytes 4631616 | tf_op jit(solution)/shard_map/concatenate | solution.py:30
  21.3 3.8 %fusion.31 = f32[2,32,64,128]{3,2,1,0:T(8,128)S(1)} fusion(f32[2,34,66,130]{3,2,1,0:T(8,128)S(1)} %select_maximum_fusion.8, f32[2,34,1,128]{3,2,1,0:T(1,128)S(1)} %collective-permute-done.3, f32[2,1,64,128]{3,2,1,0:T(8,128)S(1)} %collective-permute-done, f32[2,1,64,128]{3,2,1,0:T(8,128)S(1)} %collective-permute-done.1, f32[1,32,64,128]{3,2,1,0:T(8,128)S(1)} %bitcast.125, ...), kind=kLoop, calls=%fused_computation.88 | loop fusion | flops 13631488 | bytes 10686480 | tf_op jit(solution)/shard_map/add | solution.py:65
  25.1 3.4 %collective-permute-start.5 = (f32[2,1,64,128]{3,2,1,0:T(8,128)S(1)}, f32[2,1,64,128]{3,2,1,0:T(8,128)S(1)}, u32[]{:S(2)}, u32[]{:S(2)}) collective-permute-start(f32[2,1,64,128]{3,2,1,0:T(8,128)S(1)} %get-tuple-element.33), channel_id=1, source_target_pairs={{0,4},{4,8},{8,12},{12,16},{16,20},{20,24},{24,28},{28,32},{32,36}... | collective-permute-start | bytes 196616 | tf_op jit(solution)/shard_map/ppermute | solution.py:26
  28.6 1.3 collective-permute-start.4
  29.9 2.7 %collective-permute-done.4 = f32[2,1,64,128]{3,2,1,0:T(8,128)S(1)} collective-permute-done((f32[2,1,64,128]{3,2,1,0:T(8,128)S(1)}, f32[2,1,64,128]{3,2,1,0:T(8,128)S(1)}, u32[]{:S(2)}, u32[]{:S(2)}) %collective-permute-start.4) | collective-permute-done | bytes 65568 | tf_op jit(solution)/shard_map/ppermute | solution.py:29
  32.7 3.2 %collective-permute-start.7 = (f32[2,34,1,128]{3,2,1,0:T(1,128)S(1)}, f32[2,34,1,128]{3,2,1,0:T(1,128)S(1)}, u32[]{:S(2)}, u32[]{:S(2)}) collective-permute-start(f32[2,34,1,128]{3,2,1,0:T(1,128)S(1)} %get-tuple-element.23), channel_id=1, source_target_pairs={{0,1},{1,2},{2,3},{4,5},{5,6},{6,7},{8,9},{9,10},{10,11},{12,13},{... | collective-permute-start | bytes 104456 | tf_op jit(solution)/shard_map/ppermute | solution.py:26
  35.9 2.6 %collective-permute-start.6 = (f32[2,34,1,128]{3,2,1,0:T(1,128)S(1)}, f32[2,34,1,128]{3,2,1,0:T(1,128)S(1)}, u32[]{:S(2)}, u32[]{:S(2)}) collective-permute-start(f32[2,34,1,128]{3,2,1,0:T(1,128)S(1)} %get-tuple-element.24), channel_id=1, source_target_pairs={{1,0},{2,1},{3,2},{5,4},{6,5},{7,6},{9,8},{10,9},{11,10},{13,12},{... | collective-permute-start | bytes 104456 | tf_op jit(solution)/shard_map/ppermute | solution.py:29
  38.5 3.2 %collective-permute-done.6 = f32[2,34,1,128]{3,2,1,0:T(1,128)S(1)} collective-permute-done((f32[2,34,1,128]{3,2,1,0:T(1,128)S(1)}, f32[2,34,1,128]{3,2,1,0:T(1,128)S(1)}, u32[]{:S(2)}, u32[]{:S(2)}) %collective-permute-start.6) | collective-permute-done | bytes 34848 | tf_op jit(solution)/shard_map/ppermute | solution.py:29
  41.7 3.0 %select_maximum_fusion.4 = f32[2,34,66,130]{3,2,1,0:T(8,128)S(1)} fusion(f32[2,34,1,128]{3,2,1,0:T(1,128)S(1)} %collective-permute-done.6, f32[2,34,1,128]{3,2,1,0:T(1,128)S(1)} %collective-permute-done.7, f32[2,1,64,128]{3,2,1,0:T(8,128)S(1)} %collective-permute-done.4, f32[2,32,64,128]{3,2,1,0:T(8,128)S(1)} %fusion.31, ...), kind=kLoop, calls=%fused_computation.6 | loop fusion | flops 7001280 | bytes 4631616 | tf_op jit(solution)/shard_map/concatenate | solution.py:30
  44.7 4.0 %fusion.22 = f32[2,32,64,128]{3,2,1,0:T(8,128)S(1)} fusion(f32[2,32,64,128]{3,2,1,0:T(8,128)S(1)} %fusion.31, f32[2,34,66,130]{3,2,1,0:T(8,128)S(1)} %select_maximum_fusion.4, f32[2,34,1,128]{3,2,1,0:T(1,128)S(1)} %collective-permute-done.7, f32[2,1,64,128]{3,2,1,0:T(8,128)S(1)} %collective-permute-done.4, f32[2,1,64,128]{3,2,1,0:T(8,128)S(1)} %collective-permute-done.5, ...), kind=kLoop, calls=%fused_computation.69 | loop fusion | flops 11010048 | bytes 10686480 | tf_op jit(solution)/shard_map/add | solution.py:65
  48.7 3.4 %collective-permute-start.9 = (f32[2,1,64,128]{3,2,1,0:T(8,128)S(1)}, f32[2,1,64,128]{3,2,1,0:T(8,128)S(1)}, u32[]{:S(2)}, u32[]{:S(2)}) collective-permute-start(f32[2,1,64,128]{3,2,1,0:T(8,128)S(1)} %get-tuple-element.31), channel_id=1, source_target_pairs={{0,4},{4,8},{8,12},{12,16},{16,20},{20,24},{24,28},{28,32},{32,36}... | collective-permute-start | bytes 196616 | tf_op jit(solution)/shard_map/ppermute | solution.py:26
  52.1 1.3 collective-permute-start.8
  53.4 2.7 %collective-permute-done.8 = f32[2,1,64,128]{3,2,1,0:T(8,128)S(1)} collective-permute-done((f32[2,1,64,128]{3,2,1,0:T(8,128)S(1)}, f32[2,1,64,128]{3,2,1,0:T(8,128)S(1)}, u32[]{:S(2)}, u32[]{:S(2)}) %collective-permute-start.8) | collective-permute-done | bytes 65568 | tf_op jit(solution)/shard_map/ppermute | solution.py:29
  56.2 1.9 %collective-permute-start.11 = (f32[2,34,1,128]{3,2,1,0:T(1,128)S(1)}, f32[2,34,1,128]{3,2,1,0:T(1,128)S(1)}, u32[]{:S(2)}, u32[]{:S(2)}) collective-permute-start(f32[2,34,1,128]{3,2,1,0:T(1,128)S(1)} %get-tuple-element.21), channel_id=1, source_target_pairs={{0,1},{1,2},{2,3},{4,5},{5,6},{6,7},{8,9},{9,10},{10,11},{12,13},{... | collective-permute-start | bytes 104456 | tf_op jit(solution)/shard_map/ppermute | solution.py:26
  58.1 4.1 %collective-permute-start.10 = (f32[2,34,1,128]{3,2,1,0:T(1,128)S(1)}, f32[2,34,1,128]{3,2,1,0:T(1,128)S(1)}, u32[]{:S(2)}, u32[]{:S(2)}) collective-permute-start(f32[2,34,1,128]{3,2,1,0:T(1,128)S(1)} %get-tuple-element.22), channel_id=1, source_target_pairs={{1,0},{2,1},{3,2},{5,4},{6,5},{7,6},{9,8},{10,9},{11,10},{13,12},{... | collective-permute-start | bytes 104456 | tf_op jit(solution)/shard_map/ppermute | solution.py:29
  62.9 1.0 collective-permute-done.10
  64.0 3.0 %select_maximum_fusion = f32[2,34,66,130]{3,2,1,0:T(8,128)S(1)} fusion(f32[2,34,1,128]{3,2,1,0:T(1,128)S(1)} %collective-permute-done.10, f32[2,34,1,128]{3,2,1,0:T(1,128)S(1)} %collective-permute-done.11, f32[2,1,64,128]{3,2,1,0:T(8,128)S(1)} %collective-permute-done.8, f32[2,32,64,128]{3,2,1,0:T(8,128)S(1)} %fusion.22, ...), kind=kLoop, calls=%fused_computation.2 | loop fusion | flops 7001280 | bytes 4631616 | tf_op jit(solution)/shard_map/concatenate | solution.py:30
  67.0 6.7 %fusion.13 = f32[2,32,64,128]{3,2,1,0:T(8,128)S(1)} fusion(f32[2,32,64,128]{3,2,1,0:T(8,128)} %copy-done, f32[2,34,66,130]{3,2,1,0:T(8,128)S(1)} %select_maximum_fusion, f32[2,34,1,128]{3,2,1,0:T(1,128)S(1)} %collective-permute-done.11, f32[2,1,64,128]{3,2,1,0:T(8,128)S(1)} %collective-permute-done.8, f32[2,1,64,128]{3,2,1,0:T(8,128)S(1)} %collective-permute-done.9, ...), kind=kLoop, calls=%fused_computation.50 | loop fusion | flops 11010048 | bytes 10686480 | tf_op jit(solution)/shard_map/add | solution.py:65
  73.7 1.9 %collective-permute-start.12 = (f32[2,32,2,128]{3,2,1,0:T(2,128)S(1)}, f32[2,32,2,128]{3,2,1,0:T(2,128)S(1)}, u32[]{:S(2)}, u32[]{:S(2)}) collective-permute-start(f32[2,32,2,128]{3,2,1,0:T(2,128)S(1)} %get-tuple-element.27), channel_id=1, source_target_pairs={{0,1},{1,2},{2,3},{4,5},{5,6},{6,7},{8,9},{9,10},{10,11},{12,13},{... | collective-permute-start | bytes 196616 | tf_op jit(solution)/shard_map/ppermute | solution.py:26
  75.7 3.9 %collective-permute-start.13 = (f32[2,32,2,128]{3,2,1,0:T(2,128)S(1)}, f32[2,32,2,128]{3,2,1,0:T(2,128)S(1)}, u32[]{:S(2)}, u32[]{:S(2)}) collective-permute-start(f32[2,32,2,128]{3,2,1,0:T(2,128)S(1)} %get-tuple-element.28), channel_id=1, source_target_pairs={{1,0},{2,1},{3,2},{5,4},{6,5},{7,6},{9,8},{10,9},{11,10},{13,12},{... | collective-permute-start | bytes 196616 | tf_op jit(solution)/shard_map/ppermute | solution.py:29
  79.9 1.9 %collective-permute-done.13 = f32[2,32,2,128]{3,2,1,0:T(2,128)S(1)} collective-permute-done((f32[2,32,2,128]{3,2,1,0:T(2,128)S(1)}, f32[2,32,2,128]{3,2,1,0:T(2,128)S(1)}, u32[]{:S(2)}, u32[]{:S(2)}) %collective-permute-start.13) | collective-permute-done | bytes 65568 | tf_op jit(solution)/shard_map/ppermute | solution.py:29
  83.1 1.4 multiply_add_fusion.2
  84.5 0.9 multiply_add_fusion.3
  85.4 1.6 %fusion.6 = (f32[2,32,64,128]{3,2,1,0:T(8,128)S(1)}, f32[2,32,64,128]{3,2,1,0:T(8,128)S(1)}) fusion(f32[2,32,68,128]{3,2,1,0:T(8,128)S(1)} %get-tuple-element.15, f32[32]{0:T(128)S(1)} %copy-done.8, f32[32]{0:T(128)S(1)} %copy-done.9, f32[32]{0:T(128)S(1)} %copy-done.10, f32[2,32,68,128]{3,2,1,0:T(8,128)S(1)} %get-tuple-element.17), kind=kLoop, calls=%fused_computation.40 | loop fusion | flops 5242880 | bytes 16777600 | tf_op jit(solution)/shard_map/add | solution.py:102
  89.8 1.7 %subtract_multiply_fusion.4 = (f32[32,64,128]{2,1,0:T(8,128)S(1)}, f32[32,64,128]{2,1,0:T(8,128)S(1)}, f32[32,64,128]{2,1,0:T(8,128)S(1)}, f32[32,64,128]{2,1,0:T(8,128)S(1)}, f32[32,64,128]{2,1,0:T(8,128)S(1)}) fusion(f32[2,32,64,128]{3,2,1,0:T(8,128)S(1)} %get-tuple-element.63, f32[32]{0:T(128)S(1)} %compare_convert_fusion, ...), kind=kOutput, calls=%fused_computation.137 | output fusion | flops 17301504 | bytes 13632512 | tf_op jit(solution)/shard_map/jit(cumsum)/reduce_window_sum | solution.py:104
  91.5 1.2 fusion.48
  92.7 1.2 fusion.44
  93.9 1.3 copy.31
  95.2 1.4 copy.32
  98.0 1.9 %collective-permute-done.14 = f32[4,64,256]{1,2,0:T(8,128)} collective-permute-done((f32[4,64,256]{1,2,0:T(8,128)}, f32[4,64,256]{1,2,0:T(8,128)}, u32[]{:S(2)}, u32[]{:S(2)}) %collective-permute-start.14) | collective-permute-done | bytes 262176 | tf_op jit(solution)/shard_map/ppermute | solution.py:35
  99.9 1.1 broadcast_select_fusion.1
  101.2 3.1 %collective-permute-start.15 = (f32[4,64,128]{1,2,0:T(8,128)S(1)}, f32[4,64,128]{1,2,0:T(8,128)S(1)}, u32[]{:S(2)}, u32[]{:S(2)}) collective-permute-start(f32[4,64,128]{1,2,0:T(8,128)S(1)} %broadcast_select_fusion.5), channel_id=1, source_target_pairs={{0,8},{4,12},{8,0},{12,4},{16,24},{20,28},{24,16},{28,20},{32,40},... | collective-permute-start | bytes 393224 | tf_op jit(solution)/shard_map/ppermute | solution.py:35
  104.3 6.6 %collective-permute-done.15 = f32[4,64,128]{1,2,0:T(8,128)S(1)} collective-permute-done((f32[4,64,128]{1,2,0:T(8,128)S(1)}, f32[4,64,128]{1,2,0:T(8,128)S(1)}, u32[]{:S(2)}, u32[]{:S(2)}) %collective-permute-start.15) | collective-permute-done | bytes 131104 | tf_op jit(solution)/shard_map/ppermute | solution.py:35
  111.0 8.2 %collective-permute-start.16 = (f32[4,64,64]{1,2,0:T(8,128)S(1)}, f32[4,64,64]{1,2,0:T(8,128)S(1)}, u32[]{:S(2)}, u32[]{:S(2)}) collective-permute-start(f32[4,64,64]{1,2,0:T(8,128)S(1)} %broadcast_select_fusion.9), channel_id=1, source_target_pairs={{0,16},{4,20},{8,24},{12,28},{16,0},{20,4},{24,8},{28,12},{32,48},... | collective-permute-start | bytes 196616 | tf_op jit(solution)/shard_map/ppermute | solution.py:35
  119.2 3.5 %collective-permute-done.16 = f32[4,64,64]{1,2,0:T(8,128)S(1)} collective-permute-done((f32[4,64,64]{1,2,0:T(8,128)S(1)}, f32[4,64,64]{1,2,0:T(8,128)S(1)}, u32[]{:S(2)}, u32[]{:S(2)}) %collective-permute-start.16) | collective-permute-done | bytes 65568 | tf_op jit(solution)/shard_map/ppermute | solution.py:35
  122.8 3.0 %collective-permute-start.17 = (f32[4,64,32]{1,2,0:T(8,128)S(1)}, f32[4,64,32]{1,2,0:T(8,128)S(1)}, u32[]{:S(2)}, u32[]{:S(2)}) collective-permute-start(f32[4,64,32]{1,2,0:T(8,128)S(1)} %broadcast_select_fusion.13), channel_id=1, source_target_pairs={{0,32},{4,36},{8,40},{12,44},{16,48},{20,52},{24,56},{28,60},{32,0... | collective-permute-start | bytes 98312 | tf_op jit(solution)/shard_map/ppermute | solution.py:35
  125.8 2.2 %collective-permute-done.17 = f32[4,64,32]{1,2,0:T(8,128)S(1)} collective-permute-done((f32[4,64,32]{1,2,0:T(8,128)S(1)}, f32[4,64,32]{1,2,0:T(8,128)S(1)}, u32[]{:S(2)}, u32[]{:S(2)}) %collective-permute-start.17) | collective-permute-done | bytes 32800 | tf_op jit(solution)/shard_map/ppermute | solution.py:35
  128.1 7.2 %collective-permute-start.18 = (f32[4,64,16]{1,2,0:T(8,128)S(1)}, f32[4,64,16]{1,2,0:T(8,128)S(1)}, u32[]{:S(2)}, u32[]{:S(2)}) collective-permute-start(f32[4,64,16]{1,2,0:T(8,128)S(1)} %broadcast_select_fusion.17), channel_id=1, source_target_pairs={{0,64},{4,68},{8,72},{12,76},{16,80},{20,84},{24,88},{28,92},{32,9... | collective-permute-start | bytes 49160 | tf_op jit(solution)/shard_map/ppermute | solution.py:35
  135.3 1.9 %collective-permute-done.18 = f32[4,64,16]{1,2,0:T(8,128)S(1)} collective-permute-done((f32[4,64,16]{1,2,0:T(8,128)S(1)}, f32[4,64,16]{1,2,0:T(8,128)S(1)}, u32[]{:S(2)}, u32[]{:S(2)}) %collective-permute-start.18) | collective-permute-done | bytes 16416 | tf_op jit(solution)/shard_map/ppermute | solution.py:35
  137.2 6.8 %collective-permute-start.19 = (f32[4,64,8]{1,2,0:T(8,128)S(1)}, f32[4,64,8]{1,2,0:T(8,128)S(1)}, u32[]{:S(2)}, u32[]{:S(2)}) collective-permute-start(f32[4,64,8]{1,2,0:T(8,128)S(1)} %broadcast_select_fusion.21), channel_id=1, source_target_pairs={{0,128},{4,132},{8,136},{12,140},{16,144},{20,148},{24,152},{28,15... | collective-permute-start | bytes 24584 | tf_op jit(solution)/shard_map/ppermute | solution.py:35
  144.0 1.6 %slice_bitcast_fusion.4 = (f32[32,64,128]{2,1,0:T(8,128)}, f32[32,64,128]{2,1,0:T(8,128)}) fusion(f32[2,32,64,128]{3,2,1,0:T(8,128)S(1)} %fusion.13), kind=kLoop, calls=%fused_computation.120 | loop fusion | bytes 4194304 | tf_op jit(solution)/shard_map/squeeze | solution.py:156
  (97 shorter events, 7.4 us)
Async XLA Ops:
  0.6 7.2 %copy-start.2 = (f32[32,64,128]{2,1,0:T(8,128)S(1)}, f32[32,64,128]{2,1,0:T(8,128)}, u32[]{:S(2)}) copy-start(f32[32,64,128]{2,1,0:T(8,128)} %param.27) | copy-start | bytes 3145732
  0.6 7.2 %copy-start.1 = (f32[32,64,128]{2,1,0:T(8,128)S(1)}, f32[32,64,128]{2,1,0:T(8,128)}, u32[]{:S(2)}) copy-start(f32[32,64,128]{2,1,0:T(8,128)} %param.26) | copy-start | bytes 3145732
  1.6 3.1 %collective-permute-start.1 = (f32[2,1,64,128]{3,2,1,0:T(8,128)S(1)}, f32[2,1,64,128]{3,2,1,0:T(8,128)S(1)}, u32[]{:S(2)}, u32[]{:S(2)}) collective-permute-start(f32[2,1,64,128]{3,2,1,0:T(8,128)S(1)} %get-tuple-element.37), channel_id=1, source_target_pairs={{0,4},{4,8},{8,12},{12,16},{16,20},{20,24},{24,28},{28,32},{32,36}... | collective-permute-start | bytes 196616 | tf_op jit(solution)/shard_map/ppermute | solution.py:26
  3.4 4.4 %collective-permute-start = (f32[2,1,64,128]{3,2,1,0:T(8,128)S(1)}, f32[2,1,64,128]{3,2,1,0:T(8,128)S(1)}, u32[]{:S(2)}, u32[]{:S(2)}) collective-permute-start(f32[2,1,64,128]{3,2,1,0:T(8,128)S(1)} %get-tuple-element.38), channel_id=1, source_target_pairs={{4,0},{8,4},{12,8},{16,12},{20,16},{24,20},{28,24},{32,28},{36,32}... | collective-permute-start | bytes 196616 | tf_op jit(solution)/shard_map/ppermute | solution.py:29
  7.9 6.2 %collective-permute-start.3 = (f32[2,34,1,128]{3,2,1,0:T(1,128)S(1)}, f32[2,34,1,128]{3,2,1,0:T(1,128)S(1)}, u32[]{:S(2)}, u32[]{:S(2)}) collective-permute-start(f32[2,34,1,128]{3,2,1,0:T(1,128)S(1)} %get-tuple-element.25), channel_id=1, source_target_pairs={{0,1},{1,2},{2,3},{4,5},{5,6},{6,7},{8,9},{9,10},{10,11},{12,13},{... | collective-permute-start | bytes 104456 | tf_op jit(solution)/shard_map/ppermute | solution.py:26
  11.3 5.8 %collective-permute-start.2 = (f32[2,34,1,128]{3,2,1,0:T(1,128)S(1)}, f32[2,34,1,128]{3,2,1,0:T(1,128)S(1)}, u32[]{:S(2)}, u32[]{:S(2)}) collective-permute-start(f32[2,34,1,128]{3,2,1,0:T(1,128)S(1)} %get-tuple-element.26), channel_id=1, source_target_pairs={{1,0},{2,1},{3,2},{5,4},{6,5},{7,6},{9,8},{10,9},{11,10},{13,12},{... | collective-permute-start | bytes 104456 | tf_op jit(solution)/shard_map/ppermute | solution.py:29
  14.1 30.6 %copy-start.3 = (f32[1,32,64,128]{3,2,1,0:T(8,128)}, f32[1,32,64,128]{3,2,1,0:T(8,128)S(1)}, u32[]{:S(2)}) copy-start(f32[1,32,64,128]{3,2,1,0:T(8,128)S(1)} %get-tuple-element.36) | copy-start | bytes 3145732
  14.1 7.3 %copy-start.5 = (f32[2]{0:T(128)S(1)}, f32[2]{0:T(128)}, u32[]{:S(2)}) copy-start(f32[2]{0:T(128)} %constant.91.clone) | copy-start | bytes 28
  14.1 7.3 %copy-start.20 = (f32[2]{0:T(128)S(1)}, f32[2]{0:T(128)}, u32[]{:S(2)}) copy-start(f32[2]{0:T(128)} %constant.122) | copy-start | bytes 28
  25.1 4.7 %collective-permute-start.5 = (f32[2,1,64,128]{3,2,1,0:T(8,128)S(1)}, f32[2,1,64,128]{3,2,1,0:T(8,128)S(1)}, u32[]{:S(2)}, u32[]{:S(2)}) collective-permute-start(f32[2,1,64,128]{3,2,1,0:T(8,128)S(1)} %get-tuple-element.33), channel_id=1, source_target_pairs={{0,4},{4,8},{8,12},{12,16},{16,20},{20,24},{24,28},{28,32},{32,36}... | collective-permute-start | bytes 196616 | tf_op jit(solution)/shard_map/ppermute | solution.py:26
  28.6 4.0 %collective-permute-start.4 = (f32[2,1,64,128]{3,2,1,0:T(8,128)S(1)}, f32[2,1,64,128]{3,2,1,0:T(8,128)S(1)}, u32[]{:S(2)}, u32[]{:S(2)}) collective-permute-start(f32[2,1,64,128]{3,2,1,0:T(8,128)S(1)} %get-tuple-element.34), channel_id=1, source_target_pairs={{4,0},{8,4},{12,8},{16,12},{20,16},{24,20},{28,24},{32,28},{36,32}... | collective-permute-start | bytes 196616 | tf_op jit(solution)/shard_map/ppermute | solution.py:29
  32.7 5.9 %collective-permute-start.7 = (f32[2,34,1,128]{3,2,1,0:T(1,128)S(1)}, f32[2,34,1,128]{3,2,1,0:T(1,128)S(1)}, u32[]{:S(2)}, u32[]{:S(2)}) collective-permute-start(f32[2,34,1,128]{3,2,1,0:T(1,128)S(1)} %get-tuple-element.23), channel_id=1, source_target_pairs={{0,1},{1,2},{2,3},{4,5},{5,6},{6,7},{8,9},{9,10},{10,11},{12,13},{... | collective-permute-start | bytes 104456 | tf_op jit(solution)/shard_map/ppermute | solution.py:26
  35.9 8.8 %copy-start.19 = (f32[2]{0:T(128)S(1)}, f32[2]{0:T(128)}, u32[]{:S(2)}) copy-start(f32[2]{0:T(128)} %constant.123) | copy-start | bytes 28
  35.9 5.8 %collective-permute-start.6 = (f32[2,34,1,128]{3,2,1,0:T(1,128)S(1)}, f32[2,34,1,128]{3,2,1,0:T(1,128)S(1)}, u32[]{:S(2)}, u32[]{:S(2)}) collective-permute-start(f32[2,34,1,128]{3,2,1,0:T(1,128)S(1)} %get-tuple-element.24), channel_id=1, source_target_pairs={{1,0},{2,1},{3,2},{5,4},{6,5},{7,6},{9,8},{10,9},{11,10},{13,12},{... | collective-permute-start | bytes 104456 | tf_op jit(solution)/shard_map/ppermute | solution.py:29
  48.7 15.3 %copy-start = (f32[2,32,64,128]{3,2,1,0:T(8,128)}, f32[2,32,64,128]{3,2,1,0:T(8,128)S(1)}, u32[]{:S(2)}) copy-start(f32[2,32,64,128]{3,2,1,0:T(8,128)S(1)} %fusion.22) | copy-start | bytes 6291460
  48.7 4.7 %collective-permute-start.9 = (f32[2,1,64,128]{3,2,1,0:T(8,128)S(1)}, f32[2,1,64,128]{3,2,1,0:T(8,128)S(1)}, u32[]{:S(2)}, u32[]{:S(2)}) collective-permute-start(f32[2,1,64,128]{3,2,1,0:T(8,128)S(1)} %get-tuple-element.31), channel_id=1, source_target_pairs={{0,4},{4,8},{8,12},{12,16},{16,20},{20,24},{24,28},{28,32},{32,36}... | collective-permute-start | bytes 196616 | tf_op jit(solution)/shard_map/ppermute | solution.py:26
  52.1 4.0 %collective-permute-start.8 = (f32[2,1,64,128]{3,2,1,0:T(8,128)S(1)}, f32[2,1,64,128]{3,2,1,0:T(8,128)S(1)}, u32[]{:S(2)}, u32[]{:S(2)}) collective-permute-start(f32[2,1,64,128]{3,2,1,0:T(8,128)S(1)} %get-tuple-element.32), channel_id=1, source_target_pairs={{4,0},{8,4},{12,8},{16,12},{20,16},{24,20},{28,24},{32,28},{36,32}... | collective-permute-start | bytes 196616 | tf_op jit(solution)/shard_map/ppermute | solution.py:29
  56.2 6.7 %collective-permute-start.11 = (f32[2,34,1,128]{3,2,1,0:T(1,128)S(1)}, f32[2,34,1,128]{3,2,1,0:T(1,128)S(1)}, u32[]{:S(2)}, u32[]{:S(2)}) collective-permute-start(f32[2,34,1,128]{3,2,1,0:T(1,128)S(1)} %get-tuple-element.21), channel_id=1, source_target_pairs={{0,1},{1,2},{2,3},{4,5},{5,6},{6,7},{8,9},{9,10},{10,11},{12,13},{... | collective-permute-start | bytes 104456 | tf_op jit(solution)/shard_map/ppermute | solution.py:26
  58.1 5.8 %collective-permute-start.10 = (f32[2,34,1,128]{3,2,1,0:T(1,128)S(1)}, f32[2,34,1,128]{3,2,1,0:T(1,128)S(1)}, u32[]{:S(2)}, u32[]{:S(2)}) collective-permute-start(f32[2,34,1,128]{3,2,1,0:T(1,128)S(1)} %get-tuple-element.22), channel_id=1, source_target_pairs={{1,0},{2,1},{3,2},{5,4},{6,5},{7,6},{9,8},{10,9},{11,10},{13,12},{... | collective-permute-start | bytes 104456 | tf_op jit(solution)/shard_map/ppermute | solution.py:29
  62.9 4.1 %copy-start.4 = (f32[1,32,64,128]{3,2,1,0:T(8,128)S(1)}, f32[1,32,64,128]{3,2,1,0:T(8,128)}, u32[]{:S(2)}) copy-start(f32[1,32,64,128]{3,2,1,0:T(8,128)} %copy-done.3) | copy-start | bytes 3145732
  62.9 4.1 %copy-start.18 = (f32[2]{0:T(128)S(1)}, f32[2]{0:T(128)}, u32[]{:S(2)}) copy-start(f32[2]{0:T(128)} %constant.124) | copy-start | bytes 28
  73.7 6.2 %collective-permute-start.12 = (f32[2,32,2,128]{3,2,1,0:T(2,128)S(1)}, f32[2,32,2,128]{3,2,1,0:T(2,128)S(1)}, u32[]{:S(2)}, u32[]{:S(2)}) collective-permute-start(f32[2,32,2,128]{3,2,1,0:T(2,128)S(1)} %get-tuple-element.27), channel_id=1, source_target_pairs={{0,1},{1,2},{2,3},{4,5},{5,6},{6,7},{8,9},{9,10},{10,11},{12,13},{... | collective-permute-start | bytes 196616 | tf_op jit(solution)/shard_map/ppermute | solution.py:26
  75.7 6.2 %collective-permute-start.13 = (f32[2,32,2,128]{3,2,1,0:T(2,128)S(1)}, f32[2,32,2,128]{3,2,1,0:T(2,128)S(1)}, u32[]{:S(2)}, u32[]{:S(2)}) collective-permute-start(f32[2,32,2,128]{3,2,1,0:T(2,128)S(1)} %get-tuple-element.28), channel_id=1, source_target_pairs={{1,0},{2,1},{3,2},{5,4},{6,5},{7,6},{9,8},{10,9},{11,10},{13,12},{... | collective-permute-start | bytes 196616 | tf_op jit(solution)/shard_map/ppermute | solution.py:29
  82.2 0.8 copy-start.6
  82.2 0.8 copy-start.7
  82.2 0.8 copy-start.16
  82.2 0.8 copy-start.17
  83.0 1.4 copy-start.14
  83.1 1.4 copy-start.15
  84.5 0.9 copy-start.8
  84.5 0.9 copy-start.9
  84.5 0.9 copy-start.10
  87.0 0.7 copy-start.11
  87.1 0.7 copy-start.12
  87.1 0.7 copy-start.13
  88.4 0.7 copy-start.21
  88.4 0.7 copy-start.22
  97.4 2.5 %collective-permute-start.14 = (f32[4,64,256]{1,2,0:T(8,128)}, f32[4,64,256]{1,2,0:T(8,128)}, u32[]{:S(2)}, u32[]{:S(2)}) collective-permute-start(f32[4,64,256]{1,2,0:T(8,128)} %slice_select_fusion.1), channel_id=1, source_target_pairs={{0,4},{4,0},{8,12},{12,8},{16,20},{20,16},{24,28},{28,24},{32,36},... | collective-permute-start | bytes 786440 | tf_op jit(solution)/shard_map/ppermute | solution.py:35
  101.2 9.7 %collective-permute-start.15 = (f32[4,64,128]{1,2,0:T(8,128)S(1)}, f32[4,64,128]{1,2,0:T(8,128)S(1)}, u32[]{:S(2)}, u32[]{:S(2)}) collective-permute-start(f32[4,64,128]{1,2,0:T(8,128)S(1)} %broadcast_select_fusion.5), channel_id=1, source_target_pairs={{0,8},{4,12},{8,0},{12,4},{16,24},{20,28},{24,16},{28,20},{32,40},... | collective-permute-start | bytes 393224 | tf_op jit(solution)/shard_map/ppermute | solution.py:35
  111.0 11.7 %collective-permute-start.16 = (f32[4,64,64]{1,2,0:T(8,128)S(1)}, f32[4,64,64]{1,2,0:T(8,128)S(1)}, u32[]{:S(2)}, u32[]{:S(2)}) collective-permute-start(f32[4,64,64]{1,2,0:T(8,128)S(1)} %broadcast_select_fusion.9), channel_id=1, source_target_pairs={{0,16},{4,20},{8,24},{12,28},{16,0},{20,4},{24,8},{28,12},{32,48},... | collective-permute-start | bytes 196616 | tf_op jit(solution)/shard_map/ppermute | solution.py:35
  122.8 5.2 %collective-permute-start.17 = (f32[4,64,32]{1,2,0:T(8,128)S(1)}, f32[4,64,32]{1,2,0:T(8,128)S(1)}, u32[]{:S(2)}, u32[]{:S(2)}) collective-permute-start(f32[4,64,32]{1,2,0:T(8,128)S(1)} %broadcast_select_fusion.13), channel_id=1, source_target_pairs={{0,32},{4,36},{8,40},{12,44},{16,48},{20,52},{24,56},{28,60},{32,0... | collective-permute-start | bytes 98312 | tf_op jit(solution)/shard_map/ppermute | solution.py:35
  128.1 9.1 %collective-permute-start.18 = (f32[4,64,16]{1,2,0:T(8,128)S(1)}, f32[4,64,16]{1,2,0:T(8,128)S(1)}, u32[]{:S(2)}, u32[]{:S(2)}) collective-permute-start(f32[4,64,16]{1,2,0:T(8,128)S(1)} %broadcast_select_fusion.17), channel_id=1, source_target_pairs={{0,64},{4,68},{8,72},{12,76},{16,80},{20,84},{24,88},{28,92},{32,9... | collective-permute-start | bytes 49160 | tf_op jit(solution)/shard_map/ppermute | solution.py:35
  137.2 8.5 %collective-permute-start.19 = (f32[4,64,8]{1,2,0:T(8,128)S(1)}, f32[4,64,8]{1,2,0:T(8,128)S(1)}, u32[]{:S(2)}, u32[]{:S(2)}) collective-permute-start(f32[4,64,8]{1,2,0:T(8,128)S(1)} %broadcast_select_fusion.21), channel_id=1, source_target_pairs={{0,128},{4,132},{8,136},{12,140},{16,144},{20,148},{24,152},{28,15... | collective-permute-start | bytes 24584 | tf_op jit(solution)/shard_map/ppermute | solution.py:35
where the time goes:
time: 148 us; the launch traced here: 146 us
  starting transfers between devices  64.9 us (44%)
  other arithmetic  38.9 us (26%)
  waiting for transfers between devices  34.3 us (23%)
  local copies, waits for them, and re-layouts  6.16 us (4%)
  between operations  2.13 us (1%)
    ppermute x6, starting transfers between devices, from_partner(): lax.ppermute(shard, axis, [(i, i ^ 1 << apart) for i in range(lax.axis_si...  28.9 us
    ppermute x7, starting transfers between devices, with_halo(): lax.ppermute(lax.slice_in_dim(block, block.shape[dim] - width, None, axis...  19.1 us
    ppermute x7, waiting for transfers between devices, with_halo(): lax.ppermute(lax.slice_in_dim(block, 0, width, axis=dim), axis, backward)  17.8 us
    ppermute x7, starting transfers between devices, with_halo(): lax.ppermute(lax.slice_in_dim(block, 0, width, axis=dim), axis, backward)  16.9 us
    ppermute x6, waiting for transfers between devices, from_partner(): lax.ppermute(shard, axis, [(i, i ^ 1 << apart) for i in range(lax.axis_si...  16.2 us
    add x3, other arithmetic, relax(): return current + (source - applied) / step_size  14.4 us
    concatenate x7, other arithmetic, with_halo(): block = jnp.concatenate([low, block, high], axis=dim)  10.6 us
  transfers between devices with their start and end apart: 20, of which 14 were waited for; matrix products, arithmetic and copies ran while one was open for 1% of the time, Pallas kernels for 0%

commit v1 on v0

v1 whole, which is shorter than its diff:
```python
import functools
import math

import jax
import jax.numpy as jnp
import numpy as np
from jax import lax
from jax.experimental import pallas as pl
from jax.experimental.pallas import tpu as pltpu
from jax.sharding import PartitionSpec as P

SWEEPS = 3
DIFFUSION = (0.5, 2.0)
TIME_STEP = 0.4
COUPLE = 0.6
LATENT = 0.5
SHEAR_Y = (1.6, -1.6, 0.8, -1.2)
SHEAR_Z = (0.9, -0.6, -0.9, 0.3)
CX, CY, NZ = 32, 64, 128
NX = 2048
VIEWS = 4

HALO = 3
RIM = 5
EX = CX + 2 * HALO
ROW0 = 8
EY = CY + 2 * ROW0
CORNER = 4
RELATIVE = (0, 3, 1, 2)


def thetas(sweep_total):
    chebyshev = []
    for f in range(2):
        highest = 1.0 + 12.0 * DIFFUSION[f]
        entries = [
            0.5 * (highest + 1.0)
            + 0.5 * (highest - 1.0) * math.cos((2 * j + 1) * math.pi / (2 * sweep_total))
            for j in range(sweep_total)
        ]
        chebyshev.append(entries)
    return np.array(chebyshev)


VMEM = pl.BlockSpec(memory_space=pltpu.VMEM)
SMEM = pl.BlockSpec(memory_space=pltpu.SMEM)
ANY = pl.BlockSpec(memory_space=pl.ANY)


def pack_kernel(phase, temper, ext, depth_a, depth_b, lat_a, lat_b, aa, ab, ba, bb, sems):
    copies = []
    for f, field in enumerate((phase, temper)):
        copies.append(
            pltpu.make_async_copy(
                field, ext.at[f, pl.ds(HALO, CX), pl.ds(ROW0, CY), :], sems.at[f]
            )
        )
    for copy in copies:
        copy.start()
    d_odd = lax.rem(lax.axis_index("depth"), 2)
    l_odd = lax.rem(lax.axis_index("lat"), 2)
    layer_a = HALO + (1 - d_odd) * (CX - HALO)
    layer_b = HALO + d_odd * (CX - HALO)
    row_a = ROW0 + (1 - l_odd) * (CY - RIM)
    row_b = ROW0 + l_odd * (CY - RIM)
    corner_a = ROW0 + (1 - l_odd) * (CY - CORNER)
    corner_b = ROW0 + l_odd * (CY - CORNER)
    for f in range(2):
        copies[f].wait()

        def lat_rows(x, carry):
            at = (f * CX + x) * RIM
            lat_a[pl.ds(at, RIM), :] = ext[f, HALO + x, pl.ds(row_a, RIM), :]
            lat_b[pl.ds(at, RIM), :] = ext[f, HALO + x, pl.ds(row_b, RIM), :]
            return carry

        lax.fori_loop(0, CX, lat_rows, 0, unroll=4)
        for k in range(HALO):
            depth_a[f, k] = ext[f, layer_a + k, pl.ds(ROW0, CY), :]
            depth_b[f, k] = ext[f, layer_b + k, pl.ds(ROW0, CY), :]
            at = pl.ds((f * HALO + k) * CORNER, CORNER)
            aa[at, :] = ext[f, layer_a + k, pl.ds(corner_a, CORNER), :]
            ab[at, :] = ext[f, layer_a + k, pl.ds(corner_b, CORNER), :]
            ba[at, :] = ext[f, layer_b + k, pl.ds(corner_a, CORNER), :]
            bb[at, :] = ext[f, layer_b + k, pl.ds(corner_b, CORNER), :]


def pack(phase, temper):
    f32 = jnp.float32
    return pl.pallas_call(
        pack_kernel,
        out_shape=[
            jax.ShapeDtypeStruct((2, EX, EY, NZ), f32),
            jax.ShapeDtypeStruct((2, HALO, CY, NZ), f32),
            jax.ShapeDtypeStruct((2, HALO, CY, NZ), f32),
            jax.ShapeDtypeStruct((2 * CX * RIM, NZ), f32),
            jax.ShapeDtypeStruct((2 * CX * RIM, NZ), f32),
        ]
        + [jax.ShapeDtypeStruct((2 * HALO * CORNER, NZ), f32)] * 4,
        in_specs=[ANY, ANY],
        out_specs=[VMEM] * 9,
        scratch_shapes=[pltpu.SemaphoreType.DMA((2,))],
        compiler_params=pltpu.CompilerParams(vmem_limit_bytes=20 << 20),
    )(phase, temper)


def unpack(ext, depth_a, depth_b, lat_a, lat_b, aa, ab, ba, bb):
    d_odd = lax.rem(lax.axis_index("depth"), 2)
    l_odd = lax.rem(lax.axis_index("lat"), 2)
    layer_a = (1 - d_odd) * (HALO + CX)
    layer_b = d_odd * (HALO + CX)
    row_a = ROW0 - RIM + (1 - l_odd) * (RIM + CY)
    row_b = ROW0 - RIM + l_odd * (RIM + CY)
    corner_a = ROW0 - CORNER + (1 - l_odd) * (CORNER + CY)
    corner_b = ROW0 - CORNER + l_odd * (CORNER + CY)
    for f in range(2):

        def lat_rows(x, carry):
            at = (f * CX + x) * RIM
            ext[f, HALO + x, pl.ds(row_a, RIM), :] = lat_a[pl.ds(at, RIM), :]
            ext[f, HALO + x, pl.ds(row_b, RIM), :] = lat_b[pl.ds(at, RIM), :]
            return carry

        lax.fori_loop(0, CX, lat_rows, 0, unroll=4)
        for k in range(HALO):
            ext[f, layer_a + k, pl.ds(ROW0, CY), :] = depth_a[f, k]
            ext[f, layer_b + k, pl.ds(ROW0, CY), :] = depth_b[f, k]
            at = pl.ds((f * HALO + k) * CORNER, CORNER)
            ext[f, layer_a + k, pl.ds(corner_a, CORNER), :] = aa[at, :]
            ext[f, layer_a + k, pl.ds(corner_b, CORNER), :] = ab[at, :]
            ext[f, layer_b + k, pl.ds(corner_a, CORNER), :] = ba[at, :]
            ext[f, layer_b + k, pl.ds(corner_b, CORNER), :] = bb[at, :]


FIRST_ROW = ROW0 - CORNER
TILES = (CY + 2 * CORNER) // 8


def zero_outside(ref, first, last):
    depth = lax.axis_index("depth")
    lat = lax.axis_index("lat")

    @pl.when(depth == 0)
    def _():
        for f in range(2):
            for x in range(first, HALO):
                ref[f, x] = jnp.zeros((EY, NZ), jnp.float32)

    @pl.when(depth == lax.axis_size("depth") - 1)
    def _():
        for f in range(2):
            for x in range(HALO + CX, last):
                ref[f, x] = jnp.zeros((EY, NZ), jnp.float32)

    def zero_rows(row):
        def layer(x, carry):
            for f in range(2):
                ref[f, x, pl.ds(row, 8), :] = jnp.zeros((8, NZ), jnp.float32)
            return carry

        lax.fori_loop(first, last, layer, 0, unroll=4)

    @pl.when(lat == 0)
    def _():
        zero_rows(0)

    @pl.when(lat == lax.axis_size("lat") - 1)
    def _():
        zero_rows(ROW0 + CY)


def sweep(j, inp, out, source, first, last):
    theta = thetas(SWEEPS)
    lane = lax.broadcasted_iota(jnp.int32, (8, NZ), 1)
    low_edge = lane == 0
    high_edge = lane == NZ - 1

    def layer(x, carry):
        for t in range(TILES):
            row = FIRST_ROW + 8 * t
            centres = [inp[f, x, pl.ds(row, 8), :] for f in range(2)]
            if j == 0:
                p, h = centres
                reaction = TIME_STEP * (p * (1.0 - p) * ((p - 0.5) + COUPLE * h))
                sources = (p + reaction, h + LATENT * reaction)
                for f in range(2):
                    source[f, x, pl.ds(row, 8), :] = sources[f]
            else:
                sources = [source[f, x, pl.ds(row, 8), :] for f in range(2)]
            for f in range(2):
                u = centres[f]
                around = inp[f, x - 1, pl.ds(row, 8), :] + inp[f, x + 1, pl.ds(row, 8), :]
                sides = inp[f, x, pl.ds(row - 1, 8), :] + inp[f, x, pl.ds(row + 1, 8), :]
                below = jnp.where(low_edge, 0.0, pltpu.roll(u, 1, 1))
                above = jnp.where(high_edge, 0.0, pltpu.roll(u, NZ - 1, 1))
                total = (around + sides) + (below + above)
                k = DIFFUSION[f]
                inverse = 1.0 / theta[f, j]
                value = (
                    float(1.0 - (1.0 + 6.0 * k) * inverse) * u
                    + float(k * inverse) * total
                    + float(inverse) * sources[f]
                )
                out[f, x, pl.ds(row, 8), :] = value
        return carry

    lax.fori_loop(first, last, layer, 0)


def render_view(v, field, count, pic):
    lane = lax.broadcasted_iota(jnp.int32, (8, NZ), 1)
    positive = SHEAR_Z[v] > 0
    edge = (lane == NZ - 1) if positive else (lane == 0)
    inside = jnp.where(edge, 0.0, 1.0)
    shift = NZ - 1 if positive else 1
    tiles = CY // 8
    opacity = 4.0 / NX
    zeros = jnp.zeros((8, NZ), jnp.float32)
    ones = jnp.ones((8, NZ), jnp.float32)

    def whole(x):
        base = [math.floor(SHEAR_Y[v] * i / CX) for i in range(CX)]
        value = jnp.int32(base[0])
        for i in range(1, CX):
            if base[i] != base[i - 1]:
                value = value + jnp.where(x >= i, base[i] - base[i - 1], 0)
        return value

    def layer(x, state):
        trans, reds, greens, blues = state
        xf = x.astype(jnp.float32)
        base_y = whole(x)
        frac_y = xf * (SHEAR_Y[v] / CX) - base_y.astype(jnp.float32)
        frac_z = xf * (abs(SHEAR_Z[v]) / CX)
        near_z = 1.0 - frac_z
        far_z = inside * frac_z
        new = ([], [], [], [])
        for t in range(tiles):
            samples = []
            for f in range(2):
                row = ROW0 + 8 * t + base_y
                near = field[f, HALO + x, pl.ds(row, 8), :]
                far = field[f, HALO + x, pl.ds(row + 1, 8), :]
                mixed = near + frac_y * (far - near)
                samples.append(mixed * near_z + pltpu.roll(mixed, shift, 1) * far_z)
            s0, s1 = samples
            passed = trans[t] * jnp.exp(s0 * s0 * (-opacity))
            weight = trans[t] - passed
            square = s1 * s1
            middle = square + 1.0
            slope = 1.6 * s1
            outer = square + 1.64
            low = outer + slope
            high = outer - slope
            both = low * high
            share = weight / (middle * both)
            rest = share * middle
            new[0].append(passed)
            new[1].append(reds[t] + rest * high)
            new[2].append(greens[t] + share * both)
            new[3].append(blues[t] + rest * low)
        return tuple(tuple(n) for n in new)

    start = (ones,) * tiles, (zeros,) * tiles, (zeros,) * tiles, (zeros,) * tiles
    trans, reds, greens, blues = lax.fori_loop(0, count, layer, start)
    for c, channel in enumerate((reds, greens, blues, trans)):
        for t in range(tiles):
            pic[v, c, pl.ds(8 * t, 8), :] = channel[t]


def brick_kernel(
    ext, depth_a, depth_b, lat_a, lat_b, aa, ab, ba, bb, count,
    phase_next, heat_next, keep, send,
    other, source, pic, turned, sems,
):
    unpack(ext, depth_a, depth_b, lat_a, lat_b, aa, ab, ba, bb)
    sweep(0, ext, other, source, 1, EX - 1)
    zero_outside(other, 1, EX - 1)
    sweep(1, other, ext, source, 2, EX - 2)
    zero_outside(ext, 2, EX - 2)
    sweep(2, ext, other, source, HALO, HALO + CX)
    zero_outside(other, HALO, HALO + CX)
    copies = []
    for f, field in enumerate((phase_next, heat_next)):
        copies.append(
            pltpu.make_async_copy(
                other.at[f, pl.ds(HALO, CX), pl.ds(ROW0, CY), :], field, sems.at[f]
            )
        )
    for copy in copies:
        copy.start()
    layer_count = count[0, 0]
    for v in range(VIEWS):
        render_view(v, other, layer_count, pic)
    for v in range(2):
        for c in range(4):
            square = jnp.concatenate([pic[v, c], pltpu.roll(pic[3 - v, c], 64, 1)], axis=0)
            turned[v, c] = square.T
    depth = lax.axis_index("depth")
    my_core = lax.rem(depth, 2)
    my_x = lax.rem(lax.div(depth, 2), 4)
    my_z = lax.div(depth, 8)
    my_class = jnp.where(my_z < 4, my_z, 7 - my_z)
    for core_rel, target in ((0, keep), (1, send)):
        for i, x_rel in enumerate(RELATIVE):
            for j, z_rel in enumerate(RELATIVE):
                group = my_class ^ z_rel
                block = (group & 1) * 8 + (my_x ^ x_rel) * 2 + (my_core ^ core_rel)
                for c in range(4):
                    target[i * 4 + j, c] = turned[
                        group >> 1, c, pl.ds(pl.multiple_of(block * 8, 8), 8), :
                    ]
    for copy in copies:
        copy.wait()


def brick(ext, halos, iface_count):
    f32 = jnp.float32
    pieces = jax.ShapeDtypeStruct((16, 4, 8, NZ), f32)
    return pl.pallas_call(
        brick_kernel,
        out_shape=[
            jax.ShapeDtypeStruct((CX, CY, NZ), f32),
            jax.ShapeDtypeStruct((CX, CY, NZ), f32),
            pieces,
            pieces,
        ],
        in_specs=[VMEM] * 9 + [SMEM],
        out_specs=[ANY, ANY, VMEM, VMEM],
        scratch_shapes=[
            pltpu.VMEM((2, EX, EY, NZ), f32),
            pltpu.VMEM((2, EX, EY, NZ), f32),
            pltpu.VMEM((VIEWS, 4, CY, NZ), f32),
            pltpu.VMEM((2, 4, NZ, 2 * CY), f32),
            pltpu.SemaphoreType.DMA((2,)),
        ],
        compiler_params=pltpu.CompilerParams(vmem_limit_bytes=40 << 20),
    )(ext, *halos, iface_count)


def blend(front, back, write):
    clear = front[:, 3]
    for c in range(3):
        write(c, front[:, c] + clear * back[:, c])
    write(3, clear * back[:, 3])


def combine_kernel(bit, mine, theirs, keep, send):
    half = keep.shape[0]
    in_front = (lax.axis_index("depth") >> bit) & 1 == 0

    def write(c, value):
        keep[:, c] = value[:half]
        send[:, c] = value[half:]

    @pl.when(in_front)
    def _():
        blend(mine, theirs, write)

    @pl.when(jnp.logical_not(in_front))
    def _():
        blend(theirs, mine, write)


def combine(bit, mine, theirs):
    half = jax.ShapeDtypeStruct((mine.shape[0] // 2,) + mine.shape[1:], jnp.float32)
    return pl.pallas_call(
        functools.partial(combine_kernel, bit),
        out_shape=[half, half],
        in_specs=[VMEM] * 2,
        out_specs=[VMEM] * 2,
        compiler_params=pltpu.CompilerParams(vmem_limit_bytes=8 << 20),
    )(mine, theirs)


def last_kernel(bit, mine, theirs, out, mixed):
    low_half = (lax.axis_index("depth") >> bit) & 1 == 0

    def write(c, value):
        mixed[pl.ds(c * 8, 8), :] = value[0]

    @pl.when(low_half)
    def _():
        blend(mine, theirs, write)

    @pl.when(jnp.logical_not(low_half))
    def _():
        blend(theirs, mine, write)

    value = mixed[...]
    value = jnp.where(low_half, value, pltpu.roll(value, 64, 1))
    turned = value.T
    for c in range(4):
        out[c] = turned[:CY, c * 8 : c * 8 + 8]


def last(bit, mine, theirs):
    return pl.pallas_call(
        functools.partial(last_kernel, bit),
        out_shape=jax.ShapeDtypeStruct((4, CY, 8), jnp.float32),
        in_specs=[VMEM] * 2,
        out_specs=VMEM,
        scratch_shapes=[pltpu.VMEM((128, NZ), jnp.float32)],
        compiler_params=pltpu.CompilerParams(vmem_limit_bytes=8 << 20),
    )(mine, theirs)


def pairs(count, odd):
    result = []
    for i in range(odd, count - 1, 2):
        result += [(i, i + 1), (i + 1, i)]
    return result


def per_device(phase, temper, iface_count):
    depth_size = lax.axis_size("depth")
    lat_size = lax.axis_size("lat")
    ext, *sent = pack(phase, temper)
    depth_pairs = [pairs(depth_size, odd) for odd in range(2)]
    lat_pairs = [pairs(lat_size, odd) for odd in range(2)]
    lat_halo = [lax.ppermute(sent[2 + i], "lat", lat_pairs[i]) for i in range(2)]
    depth_halo = [lax.ppermute(sent[i], "depth", depth_pairs[i]) for i in range(2)]
    corners = []
    for i in range(2):
        for j in range(2):
            both = [
                (a * lat_size + m, b * lat_size + n)
                for a, b in depth_pairs[i]
                for m, n in lat_pairs[j]
            ]
            corners.append(lax.ppermute(sent[4 + 2 * i + j], ("depth", "lat"), both))
    phase_next, heat_next, mine, outgoing = brick(
        ext, (*depth_halo, *lat_halo, *corners), iface_count
    )
    for bit, distance in enumerate((1, 2, 6, 8, 24, 56)):
        hops = [(i, i ^ distance) for i in range(depth_size)]
        theirs = lax.ppermute(outgoing, "depth", hops)
        if bit < 4:
            mine, outgoing = combine(bit, mine, theirs)
        elif bit == 4:
            mine = outgoing = combine_all(bit, mine, theirs)
        else:
            picture = last(bit, mine, theirs)
    return phase_next, heat_next, picture


def all_kernel(bit, mine, theirs, out):
    in_front = (lax.axis_index("depth") >> bit) & 1 == 0

    def write(c, value):
        out[:, c] = value

    @pl.when(in_front)
    def _():
        blend(mine, theirs, write)

    @pl.when(jnp.logical_not(in_front))
    def _():
        blend(theirs, mine, write)


def combine_all(bit, mine, theirs):
    return pl.pallas_call(
        functools.partial(all_kernel, bit),
        out_shape=jax.ShapeDtypeStruct(mine.shape, jnp.float32),
        in_specs=[VMEM] * 2,
        out_specs=VMEM,
        compiler_params=pltpu.CompilerParams(vmem_limit_bytes=8 << 20),
    )(mine, theirs)


def solution(mesh):
    return jax.shard_map(
        per_device,
        mesh=mesh,
        in_specs=(P("depth", "lat", None), P("depth", "lat", None), P("depth", "lat")),
        out_specs=(P("depth", "lat", None), P("depth", "lat", None), P(None, "lat", "depth")),
        check_vma=False,
    )
```

time: 148 us -> 91.8 us (0.62); the launches traced: 146 us -> 92.5 us
  other arithmetic: 38.9 us -> 0 us
  Pallas kernels: 0 us -> 24 us
  starting transfers between devices: 64.9 us -> 42.9 us
  waiting for transfers between devices: 34.3 us -> 21.1 us
  local copies, waits for them, and re-layouts: 6.16 us -> 3.14 us
    pallas_call x0 -> x8, Pallas kernels: none -> 24 us  [the longest x1 23.3 us: brick(): pl.pallas_call(brick_kernel, out_shape=[jax.ShapeDtypeStruct((CX, CY, NZ)...]
    ppermute x20 -> x14, starting transfers between devices: 64.9 us -> 42.9 us  [the longest x6 31.8 us: per_device(): theirs = lax.ppermute(outgoing, 'depth', hops)]
    add x14 -> x0, other arithmetic: 19.6 us -> none  [the longest x3 14.4 us: relax(): return current + (source - applied) / step_size]
    ppermute x20 -> x14, waiting for transfers between devices: 34.3 us -> 21.1 us  [the longest x6 16.6 us: per_device(): theirs = lax.ppermute(outgoing, 'depth', hops)]
    concatenate x9 -> x0, other arithmetic: 11.3 us -> none  [the longest x7 10.6 us: with_halo(): block = jnp.concatenate([low, block, high], axis=dim)]
    another operation x6 -> x0, other arithmetic: 3.46 us -> none  [the longest x4 2.15 us: footprint(): optical = jnp.cumsum(thickness, axis=0)]
    reduce_sum x2 -> x0, other arithmetic: 2.3 us -> none  [footprint(): colours.append(jnp.sum(weight / (1.0 + distance * distance), axis=0))]
    select_n x12 -> x0, other arithmetic: 2.18 us -> none  [the longest x6 1.24 us: per_device(): in_front = jnp.where(upper_bit, partner, kept_half)]
  transfers between devices with their start and end apart: 20 -> 14, of which waited for: 14 -> 8; matrix products, arithmetic and copies ran while one was open for 1% -> 0% of each run, Pallas kernels for 0% -> 0%
where the time goes in v1:
time: 91.8 us; the launch traced here: 92.5 us
  starting transfers between devices  42.9 us (47%)
  Pallas kernels  24 us (26%)
  waiting for transfers between devices  21.1 us (23%)
  local copies, waits for them, and re-layouts  3.14 us (3%)
  between operations  1.44 us (2%)
    ppermute x6, starting transfers between devices, per_device(): theirs = lax.ppermute(outgoing, 'depth', hops)  31.8 us
    pallas_call x1, Pallas kernels, brick(): pl.pallas_call(brick_kernel, out_shape=[jax.ShapeDtypeStruct((CX, CY, NZ)...  23.3 us
    ppermute x6, waiting for transfers between devices, per_device(): theirs = lax.ppermute(outgoing, 'depth', hops)  16.6 us
    ppermute x4, starting transfers between devices, per_device(): corners.append(lax.ppermute(sent[4 + 2 * i + j], ('depth', 'lat'), both))  5.57 us
    ppermute x2, starting transfers between devices, per_device(): lax.ppermute(sent[2 + i], 'lat', lat_pairs[i])  4.84 us
    ppermute x4, waiting for transfers between devices, per_device(): corners.append(lax.ppermute(sent[4 + 2 * i + j], ('depth', 'lat'), both))  4.41 us
    unnamed x5, local copies, waits for them, and re-layouts  3.14 us
  transfers between devices with their start and end apart: 14, of which 8 were waited for; matrix products, arithmetic and copies ran while one was open for 0% of the time, Pallas kernels for 0%

profile of v1, /device:TPU:8, one launch (start us, length us, event | category | flops | bytes accessed | tf_op | source)
XLA Modules:
  0.0 92.5 jit_solution(16464050761795800368)
XLA Ops:
  0.6 0.0 copy-start
  0.6 1.2 %copy-done = f32[32,64,128]{2,1,0:T(8,128)S(1)} copy-done((f32[32,64,128]{2,1,0:T(8,128)S(1)}, f32[32,64,128]{2,1,0:T(8,128)}, u32[]{:S(2)}) %copy-start) | copy-done | bytes 1048600
  1.9 0.0 copy-start.1
  1.9 1.2 %copy-done.1 = f32[32,64,128]{2,1,0:T(8,128)S(1)} copy-done((f32[32,64,128]{2,1,0:T(8,128)S(1)}, f32[32,64,128]{2,1,0:T(8,128)}, u32[]{:S(2)}) %copy-start.1) | copy-done | bytes 1048600
  3.1 0.4 shard_map.58
  3.4 0.1 collective-permute-start
  3.5 0.7 collective-permute-start.1
  4.2 2.2 %collective-permute-start.2 = (f32[320,128]{1,0:T(8,128)S(1)}, f32[320,128]{1,0:T(8,128)S(1)}, u32[]{:S(2)}, u32[]{:S(2)}) collective-permute-start(f32[320,128]{1,0:T(8,128)S(1)} %get-tuple-element.27), channel_id=1, source_target_pairs={{0,1},{1,0},{2,3},{3,2},{4,5},{5,4},{6,7},{7,6},{8,9},{9,8},{10,11... | collective-permute-start | bytes 491528 | tf_op jit(solution)/shard_map/ppermute | solution.py:421
  6.5 2.6 %collective-permute-start.3 = (f32[320,128]{1,0:T(8,128)S(1)}, f32[320,128]{1,0:T(8,128)S(1)}, u32[]{:S(2)}, u32[]{:S(2)}) collective-permute-start(f32[320,128]{1,0:T(8,128)S(1)} %get-tuple-element.28), channel_id=1, source_target_pairs={{1,2},{2,1},{5,6},{6,5},{9,10},{10,9},{13,14},{14,13},{17,18},{18,... | collective-permute-start | bytes 491528 | tf_op jit(solution)/shard_map/ppermute | solution.py:421
  9.1 0.2 collective-permute-start.4
  9.3 3.0 %collective-permute-done.4.aa = f32[24,128]{1,0:T(8,128)S(1)} collective-permute-done((f32[24,128]{1,0:T(8,128)S(1)}, f32[24,128]{1,0:T(8,128)S(1)}, u32[]{:S(2)}, u32[]{:S(2)}) %collective-permute-start.4) | collective-permute-done | bytes 12320 | tf_op jit(solution)/shard_map/ppermute | solution.py:431
  12.3 4.1 %collective-permute-start.5 = (f32[24,128]{1,0:T(8,128)S(1)}, f32[24,128]{1,0:T(8,128)S(1)}, u32[]{:S(2)}, u32[]{:S(2)}) collective-permute-start(f32[24,128]{1,0:T(8,128)S(1)} %get-tuple-element.30), channel_id=1, source_target_pairs={{1,6},{2,5},{5,2},{6,1},{9,14},{10,13},{13,10},{14,9},{17,22},{18,... | collective-permute-start | bytes 36872 | tf_op jit(solution)/shard_map/ppermute | solution.py:431
  16.4 1.4 %collective-permute-done.5.ab = f32[24,128]{1,0:T(8,128)S(1)} collective-permute-done((f32[24,128]{1,0:T(8,128)S(1)}, f32[24,128]{1,0:T(8,128)S(1)}, u32[]{:S(2)}, u32[]{:S(2)}) %collective-permute-start.5) | collective-permute-done | bytes 12320 | tf_op jit(solution)/shard_map/ppermute | solution.py:431
  17.8 0.7 collective-permute-start.6
  18.4 0.0 collective-permute-done.6.ba
  18.4 0.7 collective-permute-start.7
  19.7 0.0 collective-permute-done.7.bb
  19.7 0.0 collective-permute-done.2.lat_a
  19.8 0.0 collective-permute-done.3.lat_b
  19.8 0.0 collective-permute-done.depth_a
  19.8 0.0 collective-permute-done.1.depth_b
  19.8 23.3 %shard_map.59 = (f32[32,64,128]{2,1,0:T(8,128)}, f32[32,64,128]{2,1,0:T(8,128)}, f32[16,4,8,128]{3,2,1,0:T(8,128)S(1)}, f32[16,4,8,128]{3,2,1,0:T(8,128)S(1)}) custom-call(f32[2,38,80,128]{3,2,1,0:T(8,128)S(1)} %get-tuple-element.24.ext, f32[2,3,64,128]{3,2,1,0:T(8,128)S(1)} %collective-permute-done.depth_a, ...), custom_call_target="tpu_custom_call" | custom-call | tf_op jit(solution)/shard_map/pallas_call | solution.py:320
  43.1 10.5 %collective-permute-start.8 = (f32[16,4,8,128]{3,2,1,0:T(8,128)S(1)}, f32[16,4,8,128]{3,2,1,0:T(8,128)S(1)}, u32[]{:S(2)}, u32[]{:S(2)}) collective-permute-start(f32[16,4,8,128]{3,2,1,0:T(8,128)S(1)} %get-tuple-element.36), channel_id=1, source_target_pairs={{0,4},{4,0},{8,12},{12,8},{16,20},{20,16},{24,28},{28,24},{32,36},... | collective-permute-start | bytes 786440 | tf_op jit(solution)/shard_map/ppermute | solution.py:437
  53.6 1.2 %collective-permute-done.8.theirs = f32[16,4,8,128]{3,2,1,0:T(8,128)S(1)} collective-permute-done((f32[16,4,8,128]{3,2,1,0:T(8,128)S(1)}, f32[16,4,8,128]{3,2,1,0:T(8,128)S(1)}, u32[]{:S(2)}, u32[]{:S(2)}) %collective-permute-start.8) | collective-permute-done | bytes 262176 | tf_op jit(solution)/shard_map/ppermute | solution.py:437
  54.8 0.1 collective-permute-start.9
  54.9 5.8 %collective-permute-done.9.theirs = f32[8,4,8,128]{3,2,1,0:T(8,128)S(1)} collective-permute-done((f32[8,4,8,128]{3,2,1,0:T(8,128)S(1)}, f32[8,4,8,128]{3,2,1,0:T(8,128)S(1)}, u32[]{:S(2)}, u32[]{:S(2)}) %collective-permute-start.9) | collective-permute-done | bytes 131104 | tf_op jit(solution)/shard_map/ppermute | solution.py:437
  60.7 2.6 %collective-permute-start.10 = (f32[4,4,8,128]{3,2,1,0:T(8,128)S(1)}, f32[4,4,8,128]{3,2,1,0:T(8,128)S(1)}, u32[]{:S(2)}, u32[]{:S(2)}) collective-permute-start(f32[4,4,8,128]{3,2,1,0:T(8,128)S(1)} %get-tuple-element.40), channel_id=1, source_target_pairs={{0,24},{4,28},{8,16},{12,20},{16,8},{20,12},{24,0},{28,4},{32,56},... | collective-permute-start | bytes 196616 | tf_op jit(solution)/shard_map/ppermute | solution.py:437
  63.3 3.0 %collective-permute-done.10.theirs = f32[4,4,8,128]{3,2,1,0:T(8,128)S(1)} collective-permute-done((f32[4,4,8,128]{3,2,1,0:T(8,128)S(1)}, f32[4,4,8,128]{3,2,1,0:T(8,128)S(1)}, u32[]{:S(2)}, u32[]{:S(2)}) %collective-permute-start.10) | collective-permute-done | bytes 65568 | tf_op jit(solution)/shard_map/ppermute | solution.py:437
  66.3 6.9 %collective-permute-start.11 = (f32[2,4,8,128]{3,2,1,0:T(8,128)S(1)}, f32[2,4,8,128]{3,2,1,0:T(8,128)S(1)}, u32[]{:S(2)}, u32[]{:S(2)}) collective-permute-start(f32[2,4,8,128]{3,2,1,0:T(8,128)S(1)} %get-tuple-element.42), channel_id=1, source_target_pairs={{0,32},{4,36},{8,40},{12,44},{16,48},{20,52},{24,56},{28,60},{32,0... | collective-permute-start | bytes 98312 | tf_op jit(solution)/shard_map/ppermute | solution.py:437
  73.2 1.9 %collective-permute-done.11.theirs = f32[2,4,8,128]{3,2,1,0:T(8,128)S(1)} collective-permute-done((f32[2,4,8,128]{3,2,1,0:T(8,128)S(1)}, f32[2,4,8,128]{3,2,1,0:T(8,128)S(1)}, u32[]{:S(2)}, u32[]{:S(2)}) %collective-permute-start.11) | collective-permute-done | bytes 32800 | tf_op jit(solution)/shard_map/ppermute | solution.py:437
  75.1 2.4 %collective-permute-start.12 = (f32[1,4,8,128]{3,2,1,0:T(8,128)S(1)}, f32[1,4,8,128]{3,2,1,0:T(8,128)S(1)}, u32[]{:S(2)}, u32[]{:S(2)}) collective-permute-start(f32[1,4,8,128]{3,2,1,0:T(8,128)S(1)} %get-tuple-element.44), channel_id=1, source_target_pairs={{0,96},{4,100},{8,104},{12,108},{16,112},{20,116},{24,120},{28,124... | collective-permute-start | bytes 49160 | tf_op jit(solution)/shard_map/ppermute | solution.py:437
  77.5 3.1 %collective-permute-done.12.theirs = f32[1,4,8,128]{3,2,1,0:T(8,128)S(1)} collective-permute-done((f32[1,4,8,128]{3,2,1,0:T(8,128)S(1)}, f32[1,4,8,128]{3,2,1,0:T(8,128)S(1)}, u32[]{:S(2)}, u32[]{:S(2)}) %collective-permute-start.12) | collective-permute-done | bytes 16416 | tf_op jit(solution)/shard_map/ppermute | solution.py:437
  80.7 9.2 %collective-permute-start.13 = (f32[1,4,8,128]{3,2,1,0:T(8,128)S(1)}, f32[1,4,8,128]{3,2,1,0:T(8,128)S(1)}, u32[]{:S(2)}, u32[]{:S(2)}) collective-permute-start(f32[1,4,8,128]{3,2,1,0:T(8,128)S(1)} %shard_map.64.mine), channel_id=1, source_target_pairs={{0,224},{4,228},{8,232},{12,236},{16,240},{20,244},{24,248},{28,25... | collective-permute-start | bytes 49160 | tf_op jit(solution)/shard_map/ppermute | solution.py:437
  89.9 1.7 %collective-permute-done.13.theirs = f32[1,4,8,128]{3,2,1,0:T(8,128)S(1)} collective-permute-done((f32[1,4,8,128]{3,2,1,0:T(8,128)S(1)}, f32[1,4,8,128]{3,2,1,0:T(8,128)S(1)}, u32[]{:S(2)}, u32[]{:S(2)}) %collective-permute-start.13) | collective-permute-done | bytes 16416 | tf_op jit(solution)/shard_map/ppermute | solution.py:437
  91.6 0.2 shard_map.65
  91.9 0.7 copy.6
  (5 shorter events, 0.1 us)
Async XLA Ops:
  0.6 1.2 %copy-start = (f32[32,64,128]{2,1,0:T(8,128)S(1)}, f32[32,64,128]{2,1,0:T(8,128)}, u32[]{:S(2)}) copy-start(f32[32,64,128]{2,1,0:T(8,128)} %phase.1) | copy-start | bytes 3145732
  1.9 1.2 %copy-start.1 = (f32[32,64,128]{2,1,0:T(8,128)S(1)}, f32[32,64,128]{2,1,0:T(8,128)}, u32[]{:S(2)}) copy-start(f32[32,64,128]{2,1,0:T(8,128)} %temper.1) | copy-start | bytes 3145732
  3.4 16.3 %collective-permute-start = (f32[2,3,64,128]{3,2,1,0:T(8,128)S(1)}, f32[2,3,64,128]{3,2,1,0:T(8,128)S(1)}, u32[]{:S(2)}, u32[]{:S(2)}) collective-permute-start(f32[2,3,64,128]{3,2,1,0:T(8,128)S(1)} %get-tuple-element.25), channel_id=1, source_target_pairs={{0,4},{4,0},{8,12},{12,8},{16,20},{20,16},{24,28},{28,24},{32,36},... | collective-permute-start | bytes 589832 | tf_op jit(solution)/shard_map/ppermute | solution.py:422
  3.5 16.2 %collective-permute-start.1 = (f32[2,3,64,128]{3,2,1,0:T(8,128)S(1)}, f32[2,3,64,128]{3,2,1,0:T(8,128)S(1)}, u32[]{:S(2)}, u32[]{:S(2)}) collective-permute-start(f32[2,3,64,128]{3,2,1,0:T(8,128)S(1)} %get-tuple-element.26), channel_id=1, source_target_pairs={{4,8},{8,4},{12,16},{16,12},{20,24},{24,20},{28,32},{32,28},{36,40... | collective-permute-start | bytes 589832 | tf_op jit(solution)/shard_map/ppermute | solution.py:422
  4.2 15.5 %collective-permute-start.2 = (f32[320,128]{1,0:T(8,128)S(1)}, f32[320,128]{1,0:T(8,128)S(1)}, u32[]{:S(2)}, u32[]{:S(2)}) collective-permute-start(f32[320,128]{1,0:T(8,128)S(1)} %get-tuple-element.27), channel_id=1, source_target_pairs={{0,1},{1,0},{2,3},{3,2},{4,5},{5,4},{6,7},{7,6},{8,9},{9,8},{10,11... | collective-permute-start | bytes 491528 | tf_op jit(solution)/shard_map/ppermute | solution.py:421
  6.5 13.3 %collective-permute-start.3 = (f32[320,128]{1,0:T(8,128)S(1)}, f32[320,128]{1,0:T(8,128)S(1)}, u32[]{:S(2)}, u32[]{:S(2)}) collective-permute-start(f32[320,128]{1,0:T(8,128)S(1)} %get-tuple-element.28), channel_id=1, source_target_pairs={{1,2},{2,1},{5,6},{6,5},{9,10},{10,9},{13,14},{14,13},{17,18},{18,... | collective-permute-start | bytes 491528 | tf_op jit(solution)/shard_map/ppermute | solution.py:421
  9.1 3.2 %collective-permute-start.4 = (f32[24,128]{1,0:T(8,128)S(1)}, f32[24,128]{1,0:T(8,128)S(1)}, u32[]{:S(2)}, u32[]{:S(2)}) collective-permute-start(f32[24,128]{1,0:T(8,128)S(1)} %get-tuple-element.29), channel_id=1, source_target_pairs={{0,5},{1,4},{2,7},{3,6},{4,1},{5,0},{6,3},{7,2},{8,13},{9,12},{10,... | collective-permute-start | bytes 36872 | tf_op jit(solution)/shard_map/ppermute | solution.py:431
  12.3 5.5 %collective-permute-start.5 = (f32[24,128]{1,0:T(8,128)S(1)}, f32[24,128]{1,0:T(8,128)S(1)}, u32[]{:S(2)}, u32[]{:S(2)}) collective-permute-start(f32[24,128]{1,0:T(8,128)S(1)} %get-tuple-element.30), channel_id=1, source_target_pairs={{1,6},{2,5},{5,2},{6,1},{9,14},{10,13},{13,10},{14,9},{17,22},{18,... | collective-permute-start | bytes 36872 | tf_op jit(solution)/shard_map/ppermute | solution.py:431
  17.8 0.7 collective-permute-start.6
  18.4 1.3 %collective-permute-start.7 = (f32[24,128]{1,0:T(8,128)S(1)}, f32[24,128]{1,0:T(8,128)S(1)}, u32[]{:S(2)}, u32[]{:S(2)}) collective-permute-start(f32[24,128]{1,0:T(8,128)S(1)} %get-tuple-element.32), channel_id=1, source_target_pairs={{5,10},{6,9},{9,6},{10,5},{13,18},{14,17},{17,14},{18,13},{21,26},... | collective-permute-start | bytes 36872 | tf_op jit(solution)/shard_map/ppermute | solution.py:431
  43.1 11.7 %collective-permute-start.8 = (f32[16,4,8,128]{3,2,1,0:T(8,128)S(1)}, f32[16,4,8,128]{3,2,1,0:T(8,128)S(1)}, u32[]{:S(2)}, u32[]{:S(2)}) collective-permute-start(f32[16,4,8,128]{3,2,1,0:T(8,128)S(1)} %get-tuple-element.36), channel_id=1, source_target_pairs={{0,4},{4,0},{8,12},{12,8},{16,20},{20,16},{24,28},{28,24},{32,36},... | collective-permute-start | bytes 786440 | tf_op jit(solution)/shard_map/ppermute | solution.py:437
  54.8 5.9 %collective-permute-start.9 = (f32[8,4,8,128]{3,2,1,0:T(8,128)S(1)}, f32[8,4,8,128]{3,2,1,0:T(8,128)S(1)}, u32[]{:S(2)}, u32[]{:S(2)}) collective-permute-start(f32[8,4,8,128]{3,2,1,0:T(8,128)S(1)} %get-tuple-element.38), channel_id=1, source_target_pairs={{0,8},{4,12},{8,0},{12,4},{16,24},{20,28},{24,16},{28,20},{32,40},... | collective-permute-start | bytes 393224 | tf_op jit(solution)/shard_map/ppermute | solution.py:437
  60.7 5.6 %collective-permute-start.10 = (f32[4,4,8,128]{3,2,1,0:T(8,128)S(1)}, f32[4,4,8,128]{3,2,1,0:T(8,128)S(1)}, u32[]{:S(2)}, u32[]{:S(2)}) collective-permute-start(f32[4,4,8,128]{3,2,1,0:T(8,128)S(1)} %get-tuple-element.40), channel_id=1, source_target_pairs={{0,24},{4,28},{8,16},{12,20},{16,8},{20,12},{24,0},{28,4},{32,56},... | collective-permute-start | bytes 196616 | tf_op jit(solution)/shard_map/ppermute | solution.py:437
  66.3 8.8 %collective-permute-start.11 = (f32[2,4,8,128]{3,2,1,0:T(8,128)S(1)}, f32[2,4,8,128]{3,2,1,0:T(8,128)S(1)}, u32[]{:S(2)}, u32[]{:S(2)}) collective-permute-start(f32[2,4,8,128]{3,2,1,0:T(8,128)S(1)} %get-tuple-element.42), channel_id=1, source_target_pairs={{0,32},{4,36},{8,40},{12,44},{16,48},{20,52},{24,56},{28,60},{32,0... | collective-permute-start | bytes 98312 | tf_op jit(solution)/shard_map/ppermute | solution.py:437
  75.1 5.5 %collective-permute-start.12 = (f32[1,4,8,128]{3,2,1,0:T(8,128)S(1)}, f32[1,4,8,128]{3,2,1,0:T(8,128)S(1)}, u32[]{:S(2)}, u32[]{:S(2)}) collective-permute-start(f32[1,4,8,128]{3,2,1,0:T(8,128)S(1)} %get-tuple-element.44), channel_id=1, source_target_pairs={{0,96},{4,100},{8,104},{12,108},{16,112},{20,116},{24,120},{28,124... | collective-permute-start | bytes 49160 | tf_op jit(solution)/shard_map/ppermute | solution.py:437
  80.7 10.9 %collective-permute-start.13 = (f32[1,4,8,128]{3,2,1,0:T(8,128)S(1)}, f32[1,4,8,128]{3,2,1,0:T(8,128)S(1)}, u32[]{:S(2)}, u32[]{:S(2)}) collective-permute-start(f32[1,4,8,128]{3,2,1,0:T(8,128)S(1)} %shard_map.64.mine), channel_id=1, source_target_pairs={{0,224},{4,228},{8,232},{12,236},{16,240},{20,244},{24,248},{28,25... | collective-permute-start | bytes 49160 | tf_op jit(solution)/shard_map/ppermute | solution.py:437

commit v2 on v1

v2 whole, which is shorter than its diff:
```python
import functools
import math

import jax
import jax.numpy as jnp
import numpy as np
from jax import lax
from jax.experimental import pallas as pl
from jax.experimental.pallas import tpu as pltpu
from jax.sharding import PartitionSpec as P

SWEEPS = 3
DIFFUSION = (0.5, 2.0)
TIME_STEP = 0.4
COUPLE = 0.6
LATENT = 0.5
SHEAR_Y = (1.6, -1.6, 0.8, -1.2)
SHEAR_Z = (0.9, -0.6, -0.9, 0.3)
CX, CY, NZ = 32, 64, 128
NX = 2048
VIEWS = 4

HALO = 3
RIM = 5
EX = CX + 2 * HALO
ROW0 = 8
EY = CY + 2 * ROW0
CORNER = 4
RELATIVE = (0, 3, 1, 2)


def thetas(sweep_total):
    chebyshev = []
    for f in range(2):
        highest = 1.0 + 12.0 * DIFFUSION[f]
        entries = [
            0.5 * (highest + 1.0)
            + 0.5 * (highest - 1.0) * math.cos((2 * j + 1) * math.pi / (2 * sweep_total))
            for j in range(sweep_total)
        ]
        chebyshev.append(entries)
    return np.array(chebyshev)


VMEM = pl.BlockSpec(memory_space=pltpu.VMEM)
SMEM = pl.BlockSpec(memory_space=pltpu.SMEM)
ANY = pl.BlockSpec(memory_space=pl.ANY)


HBM = pl.BlockSpec(memory_space=pltpu.HBM)
FIELD = jax.ShapeDtypeStruct((2, EX, EY, NZ), jnp.float32)
INNER = tuple(range(ROW0, ROW0 + CY, 8))
STRIPS = (ROW0 - CORNER, ROW0 + CY - CORNER)


def params(mib):
    return pltpu.CompilerParams(vmem_limit_bytes=mib << 20)


def odd(axis):
    return lax.rem(lax.axis_index(axis), 2)


def depth_pack(phase, temper):
    low = jnp.stack([phase[:HALO], temper[:HALO]])
    high = jnp.stack([phase[-HALO:], temper[-HALO:]])
    is_odd = odd("depth") == 1
    return jnp.where(is_odd, low, high), jnp.where(is_odd, high, low)


def lat_pack_kernel(ext, depth_a, depth_b, lat_a, lat_b):
    layer_a = (1 - odd("depth")) * (HALO + CX)
    layer_b = odd("depth") * (HALO + CX)
    row_a = (1 - odd("lat")) * (CY - RIM)
    row_b = odd("lat") * (CY - RIM)
    for f in range(2):
        for row, target in ((row_a, lat_a), (row_b, lat_b)):
            for x in range(CX):
                at = pl.ds((f * EX + HALO + x) * RIM, RIM)
                target[at, :] = ext[f, HALO + x, pl.ds(ROW0 + row, RIM), :]
            for k in range(HALO):
                for layer, halo in ((layer_a, depth_a), (layer_b, depth_b)):
                    at = pl.ds((f * EX + layer + k) * RIM, RIM)
                    target[at, :] = halo[f, k, pl.ds(row, RIM), :]


def lat_pack(ext, depth_a, depth_b):
    rows = jax.ShapeDtypeStruct((2 * EX * RIM, NZ), jnp.float32)
    return pl.pallas_call(
        lat_pack_kernel,
        out_shape=[rows, rows],
        in_specs=[VMEM] * 3,
        out_specs=[VMEM] * 2,
        compiler_params=params(4),
    )(ext, depth_a, depth_b)


def lat_unpack(ext, lat_a, lat_b):
    row_a = ROW0 - RIM + (1 - odd("lat")) * (RIM + CY)
    row_b = ROW0 - RIM + odd("lat") * (RIM + CY)
    for f in range(2):
        for x in range(EX):
            at = pl.ds((f * EX + x) * RIM, RIM)
            ext[f, x, pl.ds(row_a, RIM), :] = lat_a[at, :]
            ext[f, x, pl.ds(row_b, RIM), :] = lat_b[at, :]


def zero_layers(ref, first, last):
    depth = lax.axis_index("depth")

    @pl.when(depth == 0)
    def _():
        for f in range(2):
            for x in range(first, HALO):
                ref[f, x] = jnp.zeros((EY, NZ), jnp.float32)

    @pl.when(depth == lax.axis_size("depth") - 1)
    def _():
        for f in range(2):
            for x in range(HALO + CX, last):
                ref[f, x] = jnp.zeros((EY, NZ), jnp.float32)


def zero_rows(ref, first, last):
    lat = lax.axis_index("lat")

    def rows(row):
        def layer(x, carry):
            for f in range(2):
                ref[f, x, pl.ds(row, 8), :] = jnp.zeros((8, NZ), jnp.float32)
            return carry

        lax.fori_loop(first, last, layer, 0, unroll=2)

    @pl.when(lat == 0)
    def _():
        rows(0)

    @pl.when(lat == lax.axis_size("lat") - 1)
    def _():
        rows(ROW0 + CY)


def sweep(j, inp, out, source, first, last, rows, unroll):
    theta = thetas(SWEEPS)
    lane = lax.broadcasted_iota(jnp.int32, (8, NZ), 1)
    low_edge = lane == 0
    high_edge = lane == NZ - 1

    def layer(x, carry):
        for row in rows:
            centres = [inp[f, x, pl.ds(row, 8), :] for f in range(2)]
            if j == 0:
                p, h = centres
                reaction = TIME_STEP * (p * (1.0 - p) * ((p - 0.5) + COUPLE * h))
                sources = (
                    (p + reaction) * (1.0 / DIFFUSION[0]),
                    (h + LATENT * reaction) * (1.0 / DIFFUSION[1]),
                )
                for f in range(2):
                    source[f, x, pl.ds(row, 8), :] = sources[f]
            else:
                sources = [source[f, x, pl.ds(row, 8), :] for f in range(2)]
            for f in range(2):
                u = centres[f]
                around = inp[f, x - 1, pl.ds(row, 8), :] + inp[f, x + 1, pl.ds(row, 8), :]
                sides = inp[f, x, pl.ds(row - 1, 8), :] + inp[f, x, pl.ds(row + 1, 8), :]
                below = jnp.where(low_edge, 0.0, pltpu.roll(u, 1, 1))
                above = jnp.where(high_edge, 0.0, pltpu.roll(u, NZ - 1, 1))
                total = (around + sides) + ((below + above) + sources[f])
                k = DIFFUSION[f]
                inverse = 1.0 / theta[f, j]
                value = float(k * inverse) * total
                own = float(1.0 - (1.0 + 6.0 * k) * inverse)
                if 2 * j + 1 != SWEEPS:
                    value = value + own * u
                out[f, x, pl.ds(row, 8), :] = value
        return carry

    lax.fori_loop(first, last, layer, 0, unroll=unroll)


def first_kernel(phase, temper, ext, once, source):
    for f, field in enumerate((phase, temper)):

        def layer(x, carry):
            ext[f, HALO + x, pl.ds(ROW0, CY), :] = field[x]
            return carry

        lax.fori_loop(0, CX, layer, 0, unroll=4)
    sweep(0, ext, once, source, HALO + 1, HALO + CX - 1, INNER, 3)


def first(phase, temper):
    return pl.pallas_call(
        first_kernel,
        out_shape=[FIELD] * 3,
        in_specs=[VMEM] * 2,
        out_specs=[VMEM] * 3,
        compiler_params=params(4),
    )(phase, temper)


def inner_kernel(
    ext_in, once_in, source_in, depth_a, depth_b, lat_a, ext, once, source, twice, thrice
):
    del ext_in, once_in, source_in, lat_a
    layer_a = (1 - odd("depth")) * (HALO + CX)
    layer_b = odd("depth") * (HALO + CX)
    for f in range(2):
        for k in range(HALO):
            ext[f, layer_a + k, pl.ds(ROW0, CY), :] = depth_a[f, k]
            ext[f, layer_b + k, pl.ds(ROW0, CY), :] = depth_b[f, k]
    sweep(0, ext, once, source, 1, HALO + 1, INNER, 3)
    sweep(0, ext, once, source, HALO + CX - 1, EX - 1, INNER, 3)
    zero_layers(once, 1, EX - 1)
    sweep(1, once, twice, source, 2, EX - 2, INNER, 2)
    zero_layers(twice, 2, EX - 2)
    sweep(2, twice, thrice, source, HALO, HALO + CX, INNER, 4)


def inner(fields, halos, lat_a):
    return pl.pallas_call(
        inner_kernel,
        out_shape=[FIELD] * 5,
        in_specs=[VMEM] * 6,
        out_specs=[VMEM] * 5,
        input_output_aliases={0: 0, 1: 1, 2: 2},
        compiler_params=params(4),
    )(*fields, *halos, lat_a)


def whole_part(v, x):
    base = [math.floor(SHEAR_Y[v] * i / CX) for i in range(CX)]
    value = jnp.int32(base[0])
    for i in range(1, CX):
        if base[i] != base[i - 1]:
            value = value + jnp.where(x >= i, base[i] - base[i - 1], 0)
    return value


AT_ONCE = 2


def render(views, field, count, pic):
    lane = lax.broadcasted_iota(jnp.int32, (8, NZ), 1)
    scale = -4.0 / NX * math.log2(math.e)
    tiles = tuple(range(0, CY, 8))
    for v in views:
        for c in range(4):
            pic[v, c] = jnp.full((CY, NZ), 1.0 if c == 3 else 0.0, jnp.float32)

    def layers(i, carry):
        for v in views:
            positive = SHEAR_Z[v] > 0
            shift = NZ - 1 if positive else 1
            edge = (lane == NZ - 1) if positive else (lane == 0)
            places = []
            for q in range(AT_ONCE):
                x = i * AT_ONCE + q
                xf = x.astype(jnp.float32)
                base_y = whole_part(v, x)
                frac_y = xf * (SHEAR_Y[v] / CX) - base_y.astype(jnp.float32)
                frac_z = xf * (abs(SHEAR_Z[v]) / CX)
                far_z = jnp.where(edge, 0.0, frac_z)
                live = jnp.where(x < count, scale, 0.0)
                places.append((x, base_y, frac_y, 1.0 - frac_z, far_z, live))
            for t in tiles:
                at = pl.ds(t, 8)
                colours = [pic[v, c, at, :] for c in range(3)]
                trans = pic[v, 3, at, :]
                for x, base_y, frac_y, near_z, far_z, live in places:
                    samples = []
                    for f in range(2):
                        row = ROW0 + t + base_y
                        near = field[f, HALO + x, pl.ds(row, 8), :]
                        far = field[f, HALO + x, pl.ds(row + 1, 8), :]
                        mixed = near + frac_y * (far - near)
                        samples.append(mixed * near_z + pltpu.roll(mixed, shift, 1) * far_z)
                    s0, s1 = samples
                    passed = trans * jnp.exp2(s0 * s0 * live)
                    weight = trans - passed
                    trans = passed
                    square = s1 * s1
                    outer = square + 1.64
                    slope = 1.6 * s1
                    colours[0] = colours[0] + weight / (outer + slope)
                    colours[1] = colours[1] + weight / (square + 1.0)
                    colours[2] = colours[2] + weight / (outer - slope)
                for c in range(3):
                    pic[v, c, at, :] = colours[c]
                pic[v, 3, at, :] = trans
        return carry

    lax.fori_loop(0, lax.div(count + (AT_ONCE - 1), AT_ONCE), layers, 0)


def brick_kernel(
    ext_in, once_in, source_in, twice_in, thrice_in, lat_a, lat_b, count,
    phase_next, heat_next, keep, send, ext, once, source, twice, thrice,
    pic, turned, sems,
):
    del ext_in, once_in, source_in, twice_in, thrice_in
    lat_unpack(ext, lat_a, lat_b)
    sweep(0, ext, once, source, 1, EX - 1, STRIPS, 6)
    zero_layers(once, 1, EX - 1)
    zero_rows(once, 1, EX - 1)
    sweep(1, once, twice, source, 2, EX - 2, STRIPS, 2)
    zero_layers(twice, 2, EX - 2)
    zero_rows(twice, 2, EX - 2)
    sweep(2, twice, thrice, source, HALO, HALO + CX, STRIPS, 8)
    zero_rows(thrice, HALO, HALO + CX)
    copies = []
    for f, field in enumerate((phase_next, heat_next)):
        copies.append(
            pltpu.make_async_copy(
                thrice.at[f, pl.ds(HALO, CX), pl.ds(ROW0, CY), :], field, sems.at[f]
            )
        )
    for copy in copies:
        copy.start()
    render(range(VIEWS), thrice, count[0, 0], pic)
    for v in range(2):
        for c in range(4):
            square = jnp.concatenate([pic[v, c], pltpu.roll(pic[3 - v, c], 64, 1)], axis=0)
            turned[v, c] = square.T
    depth = lax.axis_index("depth")
    my_core = lax.rem(depth, 2)
    my_x = lax.rem(lax.div(depth, 2), 4)
    my_z = lax.div(depth, 8)
    my_class = jnp.where(my_z < 4, my_z, 7 - my_z)
    for core_rel, target in ((0, keep), (1, send)):
        for i, x_rel in enumerate(RELATIVE):
            for j, z_rel in enumerate(RELATIVE):
                group = my_class ^ z_rel
                block = (group & 1) * 8 + (my_x ^ x_rel) * 2 + (my_core ^ core_rel)
                for c in range(4):
                    target[i * 4 + j, c] = turned[
                        group >> 1, c, pl.ds(pl.multiple_of(block * 8, 8), 8), :
                    ]
    for copy in copies:
        copy.wait()


def brick(fields, lat_a, lat_b, iface_count):
    f32 = jnp.float32
    pieces = jax.ShapeDtypeStruct((16, 4, 8, NZ), f32)
    block = jax.ShapeDtypeStruct((CX, CY, NZ), f32)
    return pl.pallas_call(
        brick_kernel,
        out_shape=[block, block, pieces, pieces] + [FIELD] * 5,
        in_specs=[VMEM] * 7 + [SMEM],
        out_specs=[HBM, HBM] + [VMEM] * 7,
        input_output_aliases={i: 4 + i for i in range(5)},
        scratch_shapes=[
            pltpu.VMEM((VIEWS, 4, CY, NZ), f32),
            pltpu.VMEM((2, 4, NZ, 2 * CY), f32),
            pltpu.SemaphoreType.DMA((2,)),
        ],
        compiler_params=params(8),
    )(*fields, lat_a, lat_b, iface_count)[:4]


def blend(front, back, write):
    clear = front[:, 3]
    for c in range(3):
        write(c, front[:, c] + clear * back[:, c])
    write(3, clear * back[:, 3])


def combine_kernel(bit, mine, theirs, keep, send):
    half = keep.shape[0]
    in_front = (lax.axis_index("depth") >> bit) & 1 == 0

    def write(c, value):
        keep[:, c] = value[:half]
        send[:, c] = value[half:]

    @pl.when(in_front)
    def _():
        blend(mine, theirs, write)

    @pl.when(jnp.logical_not(in_front))
    def _():
        blend(theirs, mine, write)


def combine(bit, mine, theirs):
    half = jax.ShapeDtypeStruct((mine.shape[0] // 2,) + mine.shape[1:], jnp.float32)
    return pl.pallas_call(
        functools.partial(combine_kernel, bit),
        out_shape=[half, half],
        in_specs=[VMEM] * 2,
        out_specs=[VMEM] * 2,
        compiler_params=pltpu.CompilerParams(vmem_limit_bytes=4 << 20),
    )(mine, theirs)


def last_kernel(bit, mine, theirs, out, mixed):
    low_half = (lax.axis_index("depth") >> bit) & 1 == 0

    def write(c, value):
        mixed[pl.ds(c * 8, 8), :] = value[0]

    @pl.when(low_half)
    def _():
        blend(mine, theirs, write)

    @pl.when(jnp.logical_not(low_half))
    def _():
        blend(theirs, mine, write)

    value = mixed[...]
    value = jnp.where(low_half, value, pltpu.roll(value, 64, 1))
    for c in range(4):
        out[c] = value[c * 8 : c * 8 + 8, :CY]


def last(bit, mine, theirs):
    return pl.pallas_call(
        functools.partial(last_kernel, bit),
        out_shape=jax.ShapeDtypeStruct((4, 8, CY), jnp.float32),
        in_specs=[VMEM] * 2,
        out_specs=VMEM,
        scratch_shapes=[pltpu.VMEM((32, NZ), jnp.float32)],
        compiler_params=pltpu.CompilerParams(vmem_limit_bytes=4 << 20),
    )(mine, theirs).transpose(0, 2, 1)


def pairs(count, start):
    result = []
    for i in range(start, count - 1, 2):
        result += [(i, i + 1), (i + 1, i)]
    return result


def per_device(phase, temper, iface_count):
    depth_size = lax.axis_size("depth")
    lat_size = lax.axis_size("lat")
    depth_pairs = [pairs(depth_size, start) for start in range(2)]
    lat_pairs = [pairs(lat_size, start) for start in range(2)]
    halos = depth_pack(phase, temper)
    halos = [lax.ppermute(h, "depth", p) for h, p in zip(halos, depth_pairs)]
    fields = first(phase, temper)
    packed = lat_pack(fields[0], *halos)
    rims = [lax.ppermute(h, "lat", p) for h, p in zip(packed, lat_pairs)]
    fields = inner(fields, halos, packed[0])
    phase_next, heat_next, mine, outgoing = brick(fields, *rims, iface_count)
    for bit, distance in enumerate((1, 2, 6, 8, 24, 56)):
        hops = [(i, i ^ distance) for i in range(depth_size)]
        theirs = lax.ppermute(outgoing, "depth", hops)
        if bit < 4:
            mine, outgoing = combine(bit, mine, theirs)
        elif bit == 4:
            mine = outgoing = combine_all(bit, mine, theirs)
        else:
            picture = last(bit, mine, theirs)
    return phase_next, heat_next, picture


def all_kernel(bit, mine, theirs, out):
    in_front = (lax.axis_index("depth") >> bit) & 1 == 0

    def write(c, value):
        out[:, c] = value

    @pl.when(in_front)
    def _():
        blend(mine, theirs, write)

    @pl.when(jnp.logical_not(in_front))
    def _():
        blend(theirs, mine, write)


def combine_all(bit, mine, theirs):
    return pl.pallas_call(
        functools.partial(all_kernel, bit),
        out_shape=jax.ShapeDtypeStruct(mine.shape, jnp.float32),
        in_specs=[VMEM] * 2,
        out_specs=VMEM,
        compiler_params=pltpu.CompilerParams(vmem_limit_bytes=4 << 20),
    )(mine, theirs)


def solution(mesh):
    return jax.shard_map(
        per_device,
        mesh=mesh,
        in_specs=(P("depth", "lat", None), P("depth", "lat", None), P("depth", "lat")),
        out_specs=(P("depth", "lat", None), P("depth", "lat", None), P(None, "lat", "depth")),
        check_vma=False,
    )
```

time: 91.8 us -> 57.9 us (0.63)
  starting transfers between devices: 42.9 us -> 25.4 us
  Pallas kernels: 24 us -> 12.1 us
  waiting for transfers between devices: 21.1 us -> 15.5 us
    ppermute x6, starting transfers between devices: 31.8 us -> 18.2 us  [per_device(): theirs = lax.ppermute(outgoing, 'depth', hops)]
    pallas_call x2 -> x4, Pallas kernels: 23.6 us -> 11.4 us  [the longest x1 4.9 us: brick(): pl.pallas_call(brick_kernel, out_shape=[block, block, pieces, pieces] + [...]
    ppermute x8 -> x4, starting transfers between devices: 11.2 us -> 7.18 us  [the longest x2 3.6 us: per_device(): halos = [lax.ppermute(h, 'depth', p) for h, p in zip(halos, depth_pairs)]]
    ppermute x8 -> x4, waiting for transfers between devices: 4.42 us -> 1.42 us  [the longest x2 1.42 us: per_device(): rims = [lax.ppermute(h, 'lat', p) for h, p in zip(packed, lat_pairs)]]
    ppermute x6, waiting for transfers between devices: 16.6 us -> 14.1 us  [per_device(): theirs = lax.ppermute(outgoing, 'depth', hops)]
    another operation x0 -> x1, local copies, waits for them, and re-layouts: none -> 1.07 us  [depth_pack(): low = jnp.stack([phase[:HALO], temper[:HALO]])]
    unnamed x5 -> x4, local copies, waits for them, and re-layouts: 3.14 us -> 2.45 us
  transfers between devices with their start and end apart: 14 -> 10, of which waited for: 8 -> 7; matrix products, arithmetic and copies ran while one was open for 0% -> 0% of each run, Pallas kernels for 0% -> 11%
where the time goes in v2:
time: 57.9 us; the launch traced here: 58 us
  starting transfers between devices  25.4 us (44%)
  waiting for transfers between devices  15.5 us (27%)
  Pallas kernels  12.1 us (21%)
  local copies, waits for them, and re-layouts  3.52 us (6%)
  between operations  1.4 us (2%)
    ppermute x6, starting transfers between devices, per_device(): theirs = lax.ppermute(outgoing, 'depth', hops)  18.2 us
    ppermute x6, waiting for transfers between devices, per_device(): theirs = lax.ppermute(outgoing, 'depth', hops)  14.1 us
    pallas_call x1, Pallas kernels, brick(): pl.pallas_call(brick_kernel, out_shape=[block, block, pieces, pieces] + [...  4.9 us
    pallas_call x1, Pallas kernels, inner(): pl.pallas_call(inner_kernel, out_shape=[FIELD] * 5, in_specs=[VMEM] * 6,...  4.46 us
    ppermute x2, starting transfers between devices, per_device(): halos = [lax.ppermute(h, 'depth', p) for h, p in zip(halos, depth_pairs)]  3.6 us
    ppermute x2, starting transfers between devices, per_device(): rims = [lax.ppermute(h, 'lat', p) for h, p in zip(packed, lat_pairs)]  3.58 us
    unnamed x4, local copies, waits for them, and re-layouts  2.45 us
    pallas_call x1, Pallas kernels, first(): pl.pallas_call(first_kernel, out_shape=[FIELD] * 3, in_specs=[VMEM] * 2,...  1.94 us
  transfers between devices with their start and end apart: 10, of which 7 were waited for; matrix products, arithmetic and copies ran while one was open for 0% of the time, Pallas kernels for 11%

profile of v2, /device:TPU:8, one launch (start us, length us, event | category | flops | bytes accessed | tf_op | source)
XLA Modules:
  0.0 58.0 jit_solution(12822868263656263060)
XLA Ops:
  0.6 1.1 %slice_bitcast_fusion.2 = (f32[1,3,64,128]{3,2,1,0:T(8,128)S(1)}, f32[1,3,64,128]{3,2,1,0:T(8,128)S(1)}, f32[1,3,64,128]{3,2,1,0:T(8,128)S(1)}, f32[1,3,64,128]{3,2,1,0:T(8,128)S(1)}) fusion(f32[32,64,128]{2,1,0:T(8,128)} %temper.1, f32[32,64,128]{2,1,0:T(8,128)} %phase.1), kind=kLoop, calls=%fused_computation.6 | loop fusion | bytes 786432 | tf_op jit(solution)/shard_map/stack | solution.py:65
  1.7 0.7 %collective-permute-start.1 = (f32[2,3,64,128]{3,2,1,0:T(8,128)S(1)}, f32[2,3,64,128]{3,2,1,0:T(8,128)S(1)}, u32[]{:S(2)}, u32[]{:S(2)}) collective-permute-start(f32[2,3,64,128]{3,2,1,0:T(8,128)S(1)} %get-tuple-element.51), channel_id=1, source_target_pairs={{4,8},{8,4},{12,16},{16,12},{20,24},{24,20},{28,32},{32,28},{36,40... | collective-permute-start | bytes 589832 | tf_op jit(solution)/shard_map/ppermute | solution.py:443
  2.4 2.9 %collective-permute-start = (f32[2,3,64,128]{3,2,1,0:T(8,128)S(1)}, f32[2,3,64,128]{3,2,1,0:T(8,128)S(1)}, u32[]{:S(2)}, u32[]{:S(2)}) collective-permute-start(f32[2,3,64,128]{3,2,1,0:T(8,128)S(1)} %get-tuple-element.52), channel_id=1, source_target_pairs={{0,4},{4,0},{8,12},{12,8},{16,20},{20,16},{24,28},{28,24},{32,36},... | collective-permute-start | bytes 589832 | tf_op jit(solution)/shard_map/ppermute | solution.py:443
  5.4 0.0 copy-start
  5.4 1.2 %copy-done = f32[32,64,128]{2,1,0:T(8,128)S(1)} copy-done((f32[32,64,128]{2,1,0:T(8,128)S(1)}, f32[32,64,128]{2,1,0:T(8,128)}, u32[]{:S(2)}) %copy-start) | copy-done | bytes 1048600
  6.6 0.0 copy-start.1
  6.6 1.2 %copy-done.1 = f32[32,64,128]{2,1,0:T(8,128)S(1)} copy-done((f32[32,64,128]{2,1,0:T(8,128)S(1)}, f32[32,64,128]{2,1,0:T(8,128)}, u32[]{:S(2)}) %copy-start.1) | copy-done | bytes 1048600
  7.8 1.9 %shard_map.58 = (f32[2,38,80,128]{3,2,1,0:T(8,128)S(1)}, f32[2,38,80,128]{3,2,1,0:T(8,128)S(1)}, f32[2,38,80,128]{3,2,1,0:T(8,128)S(1)}) custom-call(f32[32,64,128]{2,1,0:T(8,128)S(1)} %copy-done, f32[32,64,128]{2,1,0:T(8,128)S(1)} %copy-done.1), custom_call_target="tpu_custom_call" | custom-call | tf_op jit(solution)/shard_map/pallas_call | solution.py:195
  9.8 0.0 collective-permute-done.1.depth_b
  9.8 0.0 collective-permute-done.depth_a
  9.8 0.1 shard_map.59
  9.9 3.5 %collective-permute-start.3 = (f32[380,128]{1,0:T(8,128)S(1)}, f32[380,128]{1,0:T(8,128)S(1)}, u32[]{:S(2)}, u32[]{:S(2)}) collective-permute-start(f32[380,128]{1,0:T(8,128)S(1)} %get-tuple-element.34), channel_id=1, source_target_pairs={{1,2},{2,1},{5,6},{6,5},{9,10},{10,9},{13,14},{14,13},{17,18},{18,... | collective-permute-start | bytes 583688 | tf_op jit(solution)/shard_map/ppermute | solution.py:446
  13.3 0.1 collective-permute-start.2
  14.1 4.5 %shard_map.60 = (f32[2,38,80,128]{3,2,1,0:T(8,128)S(1)}, f32[2,38,80,128]{3,2,1,0:T(8,128)S(1)}, f32[2,38,80,128]{3,2,1,0:T(8,128)S(1)}, f32[2,38,80,128]{3,2,1,0:T(8,128)S(1)}, f32[2,38,80,128]{3,2,1,0:T(8,128)S(1)}) custom-call(f32[2,38,80,128]{3,2,1,0:T(8,128)S(1)} %get-tuple-element.25.ext.ext_in, ...), custom_call_target="tpu_custom_call", output_to_operand_aliasing={{0}: (0, {}), {1}: (1, {}), {2}: (2, {})} | custom-call | tf_op jit(solution)/shard_map/pallas_call | solution.py:223
  18.6 0.0 collective-permute-done.3.lat_b
  18.6 1.4 %collective-permute-done.2.lat_a = f32[380,128]{1,0:T(8,128)S(1)} collective-permute-done((f32[380,128]{1,0:T(8,128)S(1)}, f32[380,128]{1,0:T(8,128)S(1)}, u32[]{:S(2)}, u32[]{:S(2)}) %collective-permute-start.2) | collective-permute-done | bytes 194592 | tf_op jit(solution)/shard_map/ppermute | solution.py:446
  20.0 4.9 %shard_map.61 = (f32[32,64,128]{2,1,0:T(8,128)}, f32[32,64,128]{2,1,0:T(8,128)}, f32[16,4,8,128]{3,2,1,0:T(8,128)S(1)}, f32[16,4,8,128]{3,2,1,0:T(8,128)S(1)}, f...) custom-call(f32[2,38,80,128]{3,2,1,0:T(8,128)S(1)} %get-tuple-elemen, ...), custom_call_target="tpu_custom_call", output_to_operand_aliasing={{4}: (0, {}), {5}: (1, {}), {6}: (2, {}), {7}: (3, {}), {8}... | custom-call | tf_op jit(solution)/shard_map/pallas_call | solution.py:349
  24.9 0.1 collective-permute-start.4
  25.0 1.5 %collective-permute-done.4.theirs = f32[16,4,8,128]{3,2,1,0:T(8,128)S(1)} collective-permute-done((f32[16,4,8,128]{3,2,1,0:T(8,128)S(1)}, f32[16,4,8,128]{3,2,1,0:T(8,128)S(1)}, u32[]{:S(2)}, u32[]{:S(2)}) %collective-permute-start.4) | collective-permute-done | bytes 262176 | tf_op jit(solution)/shard_map/ppermute | solution.py:451
  26.5 0.9 %collective-permute-start.5 = (f32[8,4,8,128]{3,2,1,0:T(8,128)S(1)}, f32[8,4,8,128]{3,2,1,0:T(8,128)S(1)}, u32[]{:S(2)}, u32[]{:S(2)}) collective-permute-start(f32[8,4,8,128]{3,2,1,0:T(8,128)S(1)} %get-tuple-element.40), channel_id=1, source_target_pairs={{0,8},{4,12},{8,0},{12,4},{16,24},{20,28},{24,16},{28,20},{32,40},... | collective-permute-start | bytes 393224 | tf_op jit(solution)/shard_map/ppermute | solution.py:451
  27.5 4.7 %collective-permute-done.5.theirs = f32[8,4,8,128]{3,2,1,0:T(8,128)S(1)} collective-permute-done((f32[8,4,8,128]{3,2,1,0:T(8,128)S(1)}, f32[8,4,8,128]{3,2,1,0:T(8,128)S(1)}, u32[]{:S(2)}, u32[]{:S(2)}) %collective-permute-start.5) | collective-permute-done | bytes 131104 | tf_op jit(solution)/shard_map/ppermute | solution.py:451
  32.2 4.0 %collective-permute-start.6 = (f32[4,4,8,128]{3,2,1,0:T(8,128)S(1)}, f32[4,4,8,128]{3,2,1,0:T(8,128)S(1)}, u32[]{:S(2)}, u32[]{:S(2)}) collective-permute-start(f32[4,4,8,128]{3,2,1,0:T(8,128)S(1)} %get-tuple-element.42), channel_id=1, source_target_pairs={{0,24},{4,28},{8,16},{12,20},{16,8},{20,12},{24,0},{28,4},{32,56},... | collective-permute-start | bytes 196616 | tf_op jit(solution)/shard_map/ppermute | solution.py:451
  36.2 2.2 %collective-permute-done.6.theirs = f32[4,4,8,128]{3,2,1,0:T(8,128)S(1)} collective-permute-done((f32[4,4,8,128]{3,2,1,0:T(8,128)S(1)}, f32[4,4,8,128]{3,2,1,0:T(8,128)S(1)}, u32[]{:S(2)}, u32[]{:S(2)}) %collective-permute-start.6) | collective-permute-done | bytes 65568 | tf_op jit(solution)/shard_map/ppermute | solution.py:451
  38.5 1.8 %collective-permute-start.7 = (f32[2,4,8,128]{3,2,1,0:T(8,128)S(1)}, f32[2,4,8,128]{3,2,1,0:T(8,128)S(1)}, u32[]{:S(2)}, u32[]{:S(2)}) collective-permute-start(f32[2,4,8,128]{3,2,1,0:T(8,128)S(1)} %get-tuple-element.44), channel_id=1, source_target_pairs={{0,32},{4,36},{8,40},{12,44},{16,48},{20,52},{24,56},{28,60},{32,0... | collective-permute-start | bytes 98312 | tf_op jit(solution)/shard_map/ppermute | solution.py:451
  40.2 2.2 %collective-permute-done.7.theirs = f32[2,4,8,128]{3,2,1,0:T(8,128)S(1)} collective-permute-done((f32[2,4,8,128]{3,2,1,0:T(8,128)S(1)}, f32[2,4,8,128]{3,2,1,0:T(8,128)S(1)}, u32[]{:S(2)}, u32[]{:S(2)}) %collective-permute-start.7) | collective-permute-done | bytes 32800 | tf_op jit(solution)/shard_map/ppermute | solution.py:451
  42.5 7.6 %collective-permute-start.8 = (f32[1,4,8,128]{3,2,1,0:T(8,128)S(1)}, f32[1,4,8,128]{3,2,1,0:T(8,128)S(1)}, u32[]{:S(2)}, u32[]{:S(2)}) collective-permute-start(f32[1,4,8,128]{3,2,1,0:T(8,128)S(1)} %get-tuple-element.46), channel_id=1, source_target_pairs={{0,96},{4,100},{8,104},{12,108},{16,112},{20,116},{24,120},{28,124... | collective-permute-start | bytes 49160 | tf_op jit(solution)/shard_map/ppermute | solution.py:451
  50.1 1.7 %collective-permute-done.8.theirs = f32[1,4,8,128]{3,2,1,0:T(8,128)S(1)} collective-permute-done((f32[1,4,8,128]{3,2,1,0:T(8,128)S(1)}, f32[1,4,8,128]{3,2,1,0:T(8,128)S(1)}, u32[]{:S(2)}, u32[]{:S(2)}) %collective-permute-start.8) | collective-permute-done | bytes 16416 | tf_op jit(solution)/shard_map/ppermute | solution.py:451
  51.8 3.8 %collective-permute-start.9 = (f32[1,4,8,128]{3,2,1,0:T(8,128)S(1)}, f32[1,4,8,128]{3,2,1,0:T(8,128)S(1)}, u32[]{:S(2)}, u32[]{:S(2)}) collective-permute-start(f32[1,4,8,128]{3,2,1,0:T(8,128)S(1)} %shard_map.66.mine), channel_id=1, source_target_pairs={{0,224},{4,228},{8,232},{12,236},{16,240},{20,244},{24,248},{28,25... | collective-permute-start | bytes 49160 | tf_op jit(solution)/shard_map/ppermute | solution.py:451
  55.6 1.7 %collective-permute-done.9.theirs = f32[1,4,8,128]{3,2,1,0:T(8,128)S(1)} collective-permute-done((f32[1,4,8,128]{3,2,1,0:T(8,128)S(1)}, f32[1,4,8,128]{3,2,1,0:T(8,128)S(1)}, u32[]{:S(2)}, u32[]{:S(2)}) %collective-permute-start.9) | collective-permute-done | bytes 16416 | tf_op jit(solution)/shard_map/ppermute | solution.py:451
  57.3 0.7 %shard_map.67 = f32[4,8,64]{2,1,0:T(8,128)} custom-call(f32[1,4,8,128]{3,2,1,0:T(8,128)S(1)} %shard_map.66.mine, f32[1,4,8,128]{3,2,1,0:T(8,128)S(1)} %collective-permute-done.9.theirs), custom_call_target="tpu_custom_call" | custom-call | tf_op jit(solution)/shard_map/pallas_call | solution.py:420
  (6 shorter events, 0.1 us)
Async XLA Ops:
  1.7 8.0 %collective-permute-start.1 = (f32[2,3,64,128]{3,2,1,0:T(8,128)S(1)}, f32[2,3,64,128]{3,2,1,0:T(8,128)S(1)}, u32[]{:S(2)}, u32[]{:S(2)}) collective-permute-start(f32[2,3,64,128]{3,2,1,0:T(8,128)S(1)} %get-tuple-element.51), channel_id=1, source_target_pairs={{4,8},{8,4},{12,16},{16,12},{20,24},{24,20},{28,32},{32,28},{36,40... | collective-permute-start | bytes 589832 | tf_op jit(solution)/shard_map/ppermute | solution.py:443
  2.4 7.3 %collective-permute-start = (f32[2,3,64,128]{3,2,1,0:T(8,128)S(1)}, f32[2,3,64,128]{3,2,1,0:T(8,128)S(1)}, u32[]{:S(2)}, u32[]{:S(2)}) collective-permute-start(f32[2,3,64,128]{3,2,1,0:T(8,128)S(1)} %get-tuple-element.52), channel_id=1, source_target_pairs={{0,4},{4,0},{8,12},{12,8},{16,20},{20,16},{24,28},{28,24},{32,36},... | collective-permute-start | bytes 589832 | tf_op jit(solution)/shard_map/ppermute | solution.py:443
  5.4 1.2 %copy-start = (f32[32,64,128]{2,1,0:T(8,128)S(1)}, f32[32,64,128]{2,1,0:T(8,128)}, u32[]{:S(2)}) copy-start(f32[32,64,128]{2,1,0:T(8,128)} %phase.1) | copy-start | bytes 3145732
  6.6 1.2 %copy-start.1 = (f32[32,64,128]{2,1,0:T(8,128)S(1)}, f32[32,64,128]{2,1,0:T(8,128)}, u32[]{:S(2)}) copy-start(f32[32,64,128]{2,1,0:T(8,128)} %temper.1) | copy-start | bytes 3145732
  9.9 8.7 %collective-permute-start.3 = (f32[380,128]{1,0:T(8,128)S(1)}, f32[380,128]{1,0:T(8,128)S(1)}, u32[]{:S(2)}, u32[]{:S(2)}) collective-permute-start(f32[380,128]{1,0:T(8,128)S(1)} %get-tuple-element.34), channel_id=1, source_target_pairs={{1,2},{2,1},{5,6},{6,5},{9,10},{10,9},{13,14},{14,13},{17,18},{18,... | collective-permute-start | bytes 583688 | tf_op jit(solution)/shard_map/ppermute | solution.py:446
  13.3 6.6 %collective-permute-start.2 = (f32[380,128]{1,0:T(8,128)S(1)}, f32[380,128]{1,0:T(8,128)S(1)}, u32[]{:S(2)}, u32[]{:S(2)}) collective-permute-start(f32[380,128]{1,0:T(8,128)S(1)} %get-tuple-element.28.lat_a), channel_id=1, source_target_pairs={{0,1},{1,0},{2,3},{3,2},{4,5},{5,4},{6,7},{7,6},{8,9},{9,8},{10,11... | collective-permute-start | bytes 583688 | tf_op jit(solution)/shard_map/ppermute | solution.py:446
  24.9 1.6 %collective-permute-start.4 = (f32[16,4,8,128]{3,2,1,0:T(8,128)S(1)}, f32[16,4,8,128]{3,2,1,0:T(8,128)S(1)}, u32[]{:S(2)}, u32[]{:S(2)}) collective-permute-start(f32[16,4,8,128]{3,2,1,0:T(8,128)S(1)} %get-tuple-element.38), channel_id=1, source_target_pairs={{0,4},{4,0},{8,12},{12,8},{16,20},{20,16},{24,28},{28,24},{32,36},... | collective-permute-start | bytes 786440 | tf_op jit(solution)/shard_map/ppermute | solution.py:451
  26.5 5.6 %collective-permute-start.5 = (f32[8,4,8,128]{3,2,1,0:T(8,128)S(1)}, f32[8,4,8,128]{3,2,1,0:T(8,128)S(1)}, u32[]{:S(2)}, u32[]{:S(2)}) collective-permute-start(f32[8,4,8,128]{3,2,1,0:T(8,128)S(1)} %get-tuple-element.40), channel_id=1, source_target_pairs={{0,8},{4,12},{8,0},{12,4},{16,24},{20,28},{24,16},{28,20},{32,40},... | collective-permute-start | bytes 393224 | tf_op jit(solution)/shard_map/ppermute | solution.py:451
  32.2 6.3 %collective-permute-start.6 = (f32[4,4,8,128]{3,2,1,0:T(8,128)S(1)}, f32[4,4,8,128]{3,2,1,0:T(8,128)S(1)}, u32[]{:S(2)}, u32[]{:S(2)}) collective-permute-start(f32[4,4,8,128]{3,2,1,0:T(8,128)S(1)} %get-tuple-element.42), channel_id=1, source_target_pairs={{0,24},{4,28},{8,16},{12,20},{16,8},{20,12},{24,0},{28,4},{32,56},... | collective-permute-start | bytes 196616 | tf_op jit(solution)/shard_map/ppermute | solution.py:451
  38.5 4.0 %collective-permute-start.7 = (f32[2,4,8,128]{3,2,1,0:T(8,128)S(1)}, f32[2,4,8,128]{3,2,1,0:T(8,128)S(1)}, u32[]{:S(2)}, u32[]{:S(2)}) collective-permute-start(f32[2,4,8,128]{3,2,1,0:T(8,128)S(1)} %get-tuple-element.44), channel_id=1, source_target_pairs={{0,32},{4,36},{8,40},{12,44},{16,48},{20,52},{24,56},{28,60},{32,0... | collective-permute-start | bytes 98312 | tf_op jit(solution)/shard_map/ppermute | solution.py:451
  42.5 9.3 %collective-permute-start.8 = (f32[1,4,8,128]{3,2,1,0:T(8,128)S(1)}, f32[1,4,8,128]{3,2,1,0:T(8,128)S(1)}, u32[]{:S(2)}, u32[]{:S(2)}) collective-permute-start(f32[1,4,8,128]{3,2,1,0:T(8,128)S(1)} %get-tuple-element.46), channel_id=1, source_target_pairs={{0,96},{4,100},{8,104},{12,108},{16,112},{20,116},{24,120},{28,124... | collective-permute-start | bytes 49160 | tf_op jit(solution)/shard_map/ppermute | solution.py:451
  51.8 5.6 %collective-permute-start.9 = (f32[1,4,8,128]{3,2,1,0:T(8,128)S(1)}, f32[1,4,8,128]{3,2,1,0:T(8,128)S(1)}, u32[]{:S(2)}, u32[]{:S(2)}) collective-permute-start(f32[1,4,8,128]{3,2,1,0:T(8,128)S(1)} %shard_map.66.mine), channel_id=1, source_target_pairs={{0,224},{4,228},{8,232},{12,236},{16,240},{20,244},{24,248},{28,25... | collective-permute-start | bytes 49160 | tf_op jit(solution)/shard_map/ppermute | solution.py:451

commit v3 on v2

--- a/solution.py
+++ b/solution.py
@@ -26,7 +26,6 @@
 ROW0 = 8
 EY = CY + 2 * ROW0
 CORNER = 4
-RELATIVE = (0, 3, 1, 2)
 
 
 def thetas(sweep_total):
@@ -61,9 +60,9 @@
     return lax.rem(lax.axis_index(axis), 2)
 
 
-def depth_pack(phase, temper):
-    low = jnp.stack([phase[:HALO], temper[:HALO]])
-    high = jnp.stack([phase[-HALO:], temper[-HALO:]])
+def depth_pack(fields):
+    low = fields[:, :HALO]
+    high = fields[:, -HALO:]
     is_odd = odd("depth") == 1
     return jnp.where(is_odd, low, high), jnp.where(is_odd, high, low)
 
@@ -180,25 +179,25 @@
     lax.fori_loop(first, last, layer, 0, unroll=unroll)
 
 
-def first_kernel(phase, temper, ext, once, source):
-    for f, field in enumerate((phase, temper)):
+def first_kernel(fields, ext, once, source):
+    for f in range(2):
 
         def layer(x, carry):
-            ext[f, HALO + x, pl.ds(ROW0, CY), :] = field[x]
+            ext[f, HALO + x, pl.ds(ROW0, CY), :] = fields[f, x]
             return carry
 
-        lax.fori_loop(0, CX, layer, 0, unroll=4)
-    sweep(0, ext, once, source, HALO + 1, HALO + CX - 1, INNER, 3)
-
-
-def first(phase, temper):
+        lax.fori_loop(0, CX, layer, 0, unroll=8)
+    sweep(0, ext, once, source, HALO + 1, HALO + CX - 1, INNER, 5)
+
+
+def first(fields):
     return pl.pallas_call(
         first_kernel,
         out_shape=[FIELD] * 3,
-        in_specs=[VMEM] * 2,
+        in_specs=[VMEM],
         out_specs=[VMEM] * 3,
         compiler_params=params(4),
-    )(phase, temper)
+    )(fields)
 
 
 def inner_kernel(
@@ -214,9 +213,9 @@
     sweep(0, ext, once, source, 1, HALO + 1, INNER, 3)
     sweep(0, ext, once, source, HALO + CX - 1, EX - 1, INNER, 3)
     zero_layers(once, 1, EX - 1)
-    sweep(1, once, twice, source, 2, EX - 2, INNER, 2)
+    sweep(1, once, twice, source, 2, EX - 2, INNER, 17)
     zero_layers(twice, 2, EX - 2)
-    sweep(2, twice, thrice, source, HALO, HALO + CX, INNER, 4)
+    sweep(2, twice, thrice, source, HALO, HALO + CX, INNER, 8)
 
 
 def inner(fields, halos, lat_a):
@@ -262,21 +261,23 @@
                 base_y = whole_part(v, x)
                 frac_y = xf * (SHEAR_Y[v] / CX) - base_y.astype(jnp.float32)
                 frac_z = xf * (abs(SHEAR_Z[v]) / CX)
-                far_z = jnp.where(edge, 0.0, frac_z)
+                near_w = (1.0 - frac_y) * (1.0 - frac_z)
+                far_w = frac_y * (1.0 - frac_z)
+                side = jnp.where(edge, 0.0, jnp.full((8, NZ), frac_z) / (1.0 - frac_z))
                 live = jnp.where(x < count, scale, 0.0)
-                places.append((x, base_y, frac_y, 1.0 - frac_z, far_z, live))
+                places.append((x, base_y, near_w, far_w, side, live))
             for t in tiles:
                 at = pl.ds(t, 8)
                 colours = [pic[v, c, at, :] for c in range(3)]
                 trans = pic[v, 3, at, :]
-                for x, base_y, frac_y, near_z, far_z, live in places:
+                for x, base_y, near_w, far_w, side, live in places:
                     samples = []
                     for f in range(2):
                         row = ROW0 + t + base_y
                         near = field[f, HALO + x, pl.ds(row, 8), :]
                         far = field[f, HALO + x, pl.ds(row + 1, 8), :]
-                        mixed = near + frac_y * (far - near)
-                        samples.append(mixed * near_z + pltpu.roll(mixed, shift, 1) * far_z)
+                        mixed = near * near_w + far * far_w
+                        samples.append(mixed + pltpu.roll(mixed, shift, 1) * side)
                     s0, s1 = samples
                     passed = trans * jnp.exp2(s0 * s0 * live)
                     weight = trans - passed
@@ -302,13 +303,13 @@
 ):
     del ext_in, once_in, source_in, twice_in, thrice_in
     lat_unpack(ext, lat_a, lat_b)
-    sweep(0, ext, once, source, 1, EX - 1, STRIPS, 6)
+    sweep(0, ext, once, source, 1, EX - 1, STRIPS, 12)
     zero_layers(once, 1, EX - 1)
     zero_rows(once, 1, EX - 1)
-    sweep(1, once, twice, source, 2, EX - 2, STRIPS, 2)
+    sweep(1, once, twice, source, 2, EX - 2, STRIPS, 17)
     zero_layers(twice, 2, EX - 2)
     zero_rows(twice, 2, EX - 2)
-    sweep(2, twice, thrice, source, HALO, HALO + CX, STRIPS, 8)
+    sweep(2, twice, thrice, source, HALO, HALO + CX, STRIPS, 16)
     zero_rows(thrice, HALO, HALO + CX)
     copies = []
     for f, field in enumerate((phase_next, heat_next)):
@@ -327,17 +328,13 @@
     depth = lax.axis_index("depth")
     my_core = lax.rem(depth, 2)
     my_x = lax.rem(lax.div(depth, 2), 4)
-    my_z = lax.div(depth, 8)
-    my_class = jnp.where(my_z < 4, my_z, 7 - my_z)
     for core_rel, target in ((0, keep), (1, send)):
-        for i, x_rel in enumerate(RELATIVE):
-            for j, z_rel in enumerate(RELATIVE):
-                group = my_class ^ z_rel
-                block = (group & 1) * 8 + (my_x ^ x_rel) * 2 + (my_core ^ core_rel)
+        for x_rel in range(4):
+            block = (my_x ^ x_rel) * 2 + (my_core ^ core_rel)
+            for z in range(4):
+                at = pl.ds(pl.multiple_of((block + (z & 1) * 8) * 8, 8), 8)
                 for c in range(4):
-                    target[i * 4 + j, c] = turned[
-                        group >> 1, c, pl.ds(pl.multiple_of(block * 8, 8), 8), :
-                    ]
+                    target[x_rel * 4 + z, c] = turned[z >> 1, c, at, :]
     for copy in copies:
         copy.wait()
 
@@ -368,13 +365,12 @@
     write(3, clear * back[:, 3])
 
 
-def combine_kernel(bit, mine, theirs, keep, send):
-    half = keep.shape[0]
-    in_front = (lax.axis_index("depth") >> bit) & 1 == 0
+def core_kernel(mine, theirs, *parts):
+    in_front = lax.rem(lax.axis_index("depth"), 2) == 0
 
     def write(c, value):
-        keep[:, c] = value[:half]
-        send[:, c] = value[half:]
+        for i, part in enumerate(parts):
+            part[:, c] = value[4 * i : 4 * i + 4]
 
     @pl.when(in_front)
     def _():
@@ -385,46 +381,71 @@
         blend(theirs, mine, write)
 
 
-def combine(bit, mine, theirs):
-    half = jax.ShapeDtypeStruct((mine.shape[0] // 2,) + mine.shape[1:], jnp.float32)
-    return pl.pallas_call(
-        functools.partial(combine_kernel, bit),
-        out_shape=[half, half],
+def core_combine(mine, theirs):
+    part = jax.ShapeDtypeStruct((4,) + mine.shape[1:], jnp.float32)
+    return pl.pallas_call(
+        core_kernel,
+        out_shape=[part] * 4,
         in_specs=[VMEM] * 2,
-        out_specs=[VMEM] * 2,
-        compiler_params=pltpu.CompilerParams(vmem_limit_bytes=4 << 20),
+        out_specs=[VMEM] * 4,
+        compiler_params=params(4),
     )(mine, theirs)
 
 
-def last_kernel(bit, mine, theirs, out, mixed):
-    low_half = (lax.axis_index("depth") >> bit) & 1 == 0
-
-    def write(c, value):
-        mixed[pl.ds(c * 8, 8), :] = value[0]
-
-    @pl.when(low_half)
-    def _():
-        blend(mine, theirs, write)
-
-    @pl.when(jnp.logical_not(low_half))
-    def _():
-        blend(theirs, mine, write)
-
-    value = mixed[...]
-    value = jnp.where(low_half, value, pltpu.roll(value, 64, 1))
-    for c in range(4):
-        out[c] = value[c * 8 : c * 8 + 8, :CY]
-
-
-def last(bit, mine, theirs):
-    return pl.pallas_call(
-        functools.partial(last_kernel, bit),
+def x_kernel(*refs):
+    parts, out = refs[:4], refs[4]
+    my_x = lax.rem(lax.div(lax.axis_index("depth"), 2), 4)
+    low = lax.broadcasted_iota(jnp.int32, (8, NZ), 1) < CY
+
+    def ordered(place):
+        for z in range(4):
+            back = parts[3 ^ place]
+            total = [back[z, c] for c in range(4)]
+            for x in (2, 1, 0):
+                front = parts[x ^ place]
+                clear = front[z, 3]
+                total = [front[z, c] + clear * total[c] for c in range(3)] + [clear * total[3]]
+            for pair in range(2):
+                a, b = total[2 * pair], total[2 * pair + 1]
+                out[z, pair] = jnp.where(low, a, pltpu.roll(b, CY, 1))
+                out[7 - z, pair] = jnp.where(low, pltpu.roll(a, CY, 1), b)
+
+    for place in range(4):
+        pl.when(my_x == place)(functools.partial(ordered, place))
+
+
+def x_combine(parts):
+    return pl.pallas_call(
+        x_kernel,
+        out_shape=jax.ShapeDtypeStruct((8, 2, 8, NZ), jnp.float32),
+        in_specs=[VMEM] * 4,
+        out_specs=VMEM,
+        compiler_params=params(4),
+    )(*parts)
+
+
+def z_kernel(slabs, out):
+    low = lax.broadcasted_iota(jnp.int32, (8, NZ), 1) < CY
+    first_pair, second_pair = slabs[7, 0], slabs[7, 1]
+    for z in range(6, -1, -1):
+        ahead = slabs[z, 1]
+        clear = jnp.where(low, pltpu.roll(ahead, CY, 1), ahead)
+        first_pair = slabs[z, 0] + clear * first_pair
+        second_pair = jnp.where(low, ahead, 0.0) + clear * second_pair
+    out[0] = first_pair[:, :CY]
+    out[1] = first_pair[:, CY:]
+    out[2] = second_pair[:, :CY]
+    out[3] = second_pair[:, CY:]
+
+
+def z_combine(slabs):
+    return pl.pallas_call(
+        z_kernel,
         out_shape=jax.ShapeDtypeStruct((4, 8, CY), jnp.float32),
-        in_specs=[VMEM] * 2,
+        in_specs=[VMEM],
         out_specs=VMEM,
-        scratch_shapes=[pltpu.VMEM((32, NZ), jnp.float32)],
-        compiler_params=pltpu.CompilerParams(vmem_limit_bytes=4 << 20),
-    )(mine, theirs).transpose(0, 2, 1)
+        compiler_params=params(4),
+    )(slabs).transpose(0, 2, 1)
 
 
 def pairs(count, start):
@@ -439,48 +460,25 @@
     lat_size = lax.axis_size("lat")
     depth_pairs = [pairs(depth_size, start) for start in range(2)]
     lat_pairs = [pairs(lat_size, start) for start in range(2)]
-    halos = depth_pack(phase, temper)
+    fields = jnp.stack([phase, temper])
+    halos = depth_pack(fields)
     halos = [lax.ppermute(h, "depth", p) for h, p in zip(halos, depth_pairs)]
-    fields = first(phase, temper)
+    fields = first(fields)
     packed = lat_pack(fields[0], *halos)
     rims = [lax.ppermute(h, "lat", p) for h, p in zip(packed, lat_pairs)]
     fields = inner(fields, halos, packed[0])
     phase_next, heat_next, mine, outgoing = brick(fields, *rims, iface_count)
-    for bit, distance in enumerate((1, 2, 6, 8, 24, 56)):
-        hops = [(i, i ^ distance) for i in range(depth_size)]
-        theirs = lax.ppermute(outgoing, "depth", hops)
-        if bit < 4:
-            mine, outgoing = combine(bit, mine, theirs)
-        elif bit == 4:
-            mine = outgoing = combine_all(bit, mine, theirs)
-        else:
-            picture = last(bit, mine, theirs)
-    return phase_next, heat_next, picture
-
-
-def all_kernel(bit, mine, theirs, out):
-    in_front = (lax.axis_index("depth") >> bit) & 1 == 0
-
-    def write(c, value):
-        out[:, c] = value
-
-    @pl.when(in_front)
-    def _():
-        blend(mine, theirs, write)
-
-    @pl.when(jnp.logical_not(in_front))
-    def _():
-        blend(theirs, mine, write)
-
-
-def combine_all(bit, mine, theirs):
-    return pl.pallas_call(
-        functools.partial(all_kernel, bit),
-        out_shape=jax.ShapeDtypeStruct(mine.shape, jnp.float32),
-        in_specs=[VMEM] * 2,
-        out_specs=VMEM,
-        compiler_params=pltpu.CompilerParams(vmem_limit_bytes=4 << 20),
-    )(mine, theirs)
+
+    def partner(value, distance):
+        return lax.ppermute(value, "depth", [(i, i ^ distance) for i in range(depth_size)])
+
+    parts = core_combine(mine, partner(outgoing, 1))
+    parts = [parts[0]] + [partner(parts[k], 2 * k) for k in (1, 2, 3)]
+    groups = [[z * 8 + i for z in range(depth_size // 8)] for i in range(8)]
+    slabs = lax.all_to_all(
+        x_combine(parts), "depth", 0, 0, tiled=True, axis_index_groups=groups
+    )
+    return phase_next, heat_next, z_combine(slabs)
 
 
 def solution(mesh):

time: 57.9 us -> 53.8 us (0.929); the launches traced: 58 us -> 53.3 us
  blocking collectives: 0 us -> 17.8 us
  starting transfers between devices: 25.4 us -> 12.5 us
  waiting for transfers between devices: 15.5 us -> 8.89 us
  local copies, waits for them, and re-layouts: 3.52 us -> 0.01 us
  other arithmetic: 0.03 us -> 1.64 us
  Pallas kernels: 12.1 us -> 11.1 us
    all_to_all x0 -> x1, blocking collectives: none -> 17.8 us  [per_device(): lax.all_to_all(x_combine(parts), 'depth', 0, 0, tiled=True, axis_index_gr...]
    ppermute x6 -> x4, starting transfers between devices: 18.2 us -> 5.28 us  [partner(): lax.ppermute(value, 'depth', [(i, i ^ distance) for i in range(depth_size)])]
    ppermute x6 -> x4, waiting for transfers between devices: 14.1 us -> 4.83 us  [partner(): lax.ppermute(value, 'depth', [(i, i ^ distance) for i in range(depth_size)])]
    ppermute x2, waiting for transfers between devices: 1.42 us -> 4.05 us  [per_device(): rims = [lax.ppermute(h, 'lat', p) for h, p in zip(packed, lat_pairs)]]
    unnamed x4, local copies, waits for them, and re-layouts: 2.45 us -> 0.01 us
    pallas_call x1, Pallas kernels: 4.46 us -> 3.01 us  [inner(): pl.pallas_call(inner_kernel, out_shape=[FIELD] * 5, in_specs=[VMEM] * 6,...]
    select_n x1, other arithmetic: 0.03 us -> 1.4 us  [depth_pack(): return (jnp.where(is_odd, low, high), jnp.where(is_odd, high, low))]
    another operation x1 -> x0, local copies, waits for them, and re-layouts: 1.07 us -> none  [depth_pack(): low = jnp.stack([phase[:HALO], temper[:HALO]])]
  transfers between devices with their start and end apart: 10 -> 8, of which waited for: 7 -> 6; matrix products, arithmetic and copies ran while one was open for 0% -> 0% of each run, Pallas kernels for 11% -> 9%
where the time goes in v3:
time: 53.8 us; the launch traced here: 53.3 us
  blocking collectives  17.8 us (33%)
  starting transfers between devices  12.5 us (23%)
  Pallas kernels  11.1 us (21%)
  waiting for transfers between devices  8.89 us (17%)
  other arithmetic  1.64 us (3%)
  between operations  1.4 us (3%)
    all_to_all x1, blocking collectives, per_device(): lax.all_to_all(x_combine(parts), 'depth', 0, 0, tiled=True, axis_index_gr...  17.8 us
    pallas_call x1, Pallas kernels, brick(): pl.pallas_call(brick_kernel, out_shape=[block, block, pieces, pieces] + [...  5.49 us
    ppermute x4, starting transfers between devices, partner(): lax.ppermute(value, 'depth', [(i, i ^ distance) for i in range(depth_size)])  5.28 us
    ppermute x4, waiting for transfers between devices, partner(): lax.ppermute(value, 'depth', [(i, i ^ distance) for i in range(depth_size)])  4.83 us
    ppermute x2, waiting for transfers between devices, per_device(): rims = [lax.ppermute(h, 'lat', p) for h, p in zip(packed, lat_pairs)]  4.05 us
    ppermute x2, starting transfers between devices, per_device(): halos = [lax.ppermute(h, 'depth', p) for h, p in zip(halos, depth_pairs)]  3.6 us
    ppermute x2, starting transfers between devices, per_device(): rims = [lax.ppermute(h, 'lat', p) for h, p in zip(packed, lat_pairs)]  3.58 us
    pallas_call x1, Pallas kernels, inner(): pl.pallas_call(inner_kernel, out_shape=[FIELD] * 5, in_specs=[VMEM] * 6,...  3.01 us
  transfers between devices with their start and end apart: 8, of which 6 were waited for; matrix products, arithmetic and copies ran while one was open for 0% of the time, Pallas kernels for 9%

profile of v3, /device:TPU:8, one launch (start us, length us, event | category | flops | bytes accessed | tf_op | source)
XLA Modules:
  0.0 53.3 jit_solution(10405727921006683956)
XLA Ops:
  0.6 0.0 copy-start
  0.6 0.0 copy-start.1
  0.7 1.4 %broadcast_select_fusion = (f32[2,3,64,128]{3,2,1,0:T(8,128)S(1)}, f32[2,3,64,128]{3,2,1,0:T(8,128)S(1)}) fusion(pred[]{:T(512)S(6)} %eq.3, f32[1,32,64,128]{3,2,1,0:T(8,128)} %bitcast.3, f32[1,32,64,128]{3,2,1,0:T(8,128)} %bitcast.5), kind=kLoop, calls=%fused_computation.7 | loop fusion | flops 294912 | bytes 2490369 | tf_op jit(solution)/shard_map/jit(_where)/select_n | solution.py:67
  2.1 0.7 %collective-permute-start.1 = (f32[2,3,64,128]{3,2,1,0:T(8,128)S(1)}, f32[2,3,64,128]{3,2,1,0:T(8,128)S(1)}, u32[]{:S(2)}, u32[]{:S(2)}) collective-permute-start(f32[2,3,64,128]{3,2,1,0:T(8,128)S(1)} %get-tuple-element.39), channel_id=1, source_target_pairs={{4,8},{8,4},{12,16},{16,12},{20,24},{24,20},{28,32},{32,28},{36,40... | collective-permute-start | bytes 589832 | tf_op jit(solution)/shard_map/ppermute | solution.py:465
  2.7 2.9 %collective-permute-start = (f32[2,3,64,128]{3,2,1,0:T(8,128)S(1)}, f32[2,3,64,128]{3,2,1,0:T(8,128)S(1)}, u32[]{:S(2)}, u32[]{:S(2)}) collective-permute-start(f32[2,3,64,128]{3,2,1,0:T(8,128)S(1)} %get-tuple-element.40), channel_id=1, source_target_pairs={{0,4},{4,0},{8,12},{12,8},{16,20},{20,16},{24,28},{28,24},{32,36},... | collective-permute-start | bytes 589832 | tf_op jit(solution)/shard_map/ppermute | solution.py:465
  5.7 0.0 copy-done
  5.7 0.0 copy-done.1
  5.7 0.2 pad_maximum_fusion.fields
  5.9 1.7 %shard_map.58 = (f32[2,38,80,128]{3,2,1,0:T(8,128)S(1)}, f32[2,38,80,128]{3,2,1,0:T(8,128)S(1)}, f32[2,38,80,128]{3,2,1,0:T(8,128)S(1)}) custom-call(f32[2,32,64,128]{3,2,1,0:T(8,128)S(1)} %pad_maximum_fusion.fields), custom_call_target="tpu_custom_call" | custom-call | tf_op jit(solution)/shard_map/pallas_call | solution.py:194
  7.6 0.0 collective-permute-done.1.depth_b
  7.6 0.0 collective-permute-done.depth_a
  7.6 0.1 shard_map.59
  7.7 3.5 %collective-permute-start.3 = (f32[380,128]{1,0:T(8,128)S(1)}, f32[380,128]{1,0:T(8,128)S(1)}, u32[]{:S(2)}, u32[]{:S(2)}) collective-permute-start(f32[380,128]{1,0:T(8,128)S(1)} %get-tuple-element.30), channel_id=1, source_target_pairs={{1,2},{2,1},{5,6},{6,5},{9,10},{10,9},{13,14},{14,13},{17,18},{18,... | collective-permute-start | bytes 583688 | tf_op jit(solution)/shard_map/ppermute | solution.py:468
  11.2 0.1 collective-permute-start.2
  11.9 3.0 %shard_map.60 = (f32[2,38,80,128]{3,2,1,0:T(8,128)S(1)}, f32[2,38,80,128]{3,2,1,0:T(8,128)S(1)}, f32[2,38,80,128]{3,2,1,0:T(8,128)S(1)}, f32[2,38,80,128]{3,2,1,0:T(8,128)S(1)}, f32[2,38,80,128]{3,2,1,0:T(8,128)S(1)}) custom-call(f32[2,38,80,128]{3,2,1,0:T(8,128)S(1)} %get-tuple-element.21.ext.ext_in, ...), custom_call_target="tpu_custom_call", output_to_operand_aliasing={{0}: (0, {}), {1}: (1, {}), {2}: (2, {})} | custom-call | tf_op jit(solution)/shard_map/pallas_call | solution.py:222
  14.9 2.1 %collective-permute-done.3.lat_b = f32[380,128]{1,0:T(8,128)S(1)} collective-permute-done((f32[380,128]{1,0:T(8,128)S(1)}, f32[380,128]{1,0:T(8,128)S(1)}, u32[]{:S(2)}, u32[]{:S(2)}) %collective-permute-start.3) | collective-permute-done | bytes 194592 | tf_op jit(solution)/shard_map/ppermute | solution.py:468
  17.0 2.0 %collective-permute-done.2.lat_a = f32[380,128]{1,0:T(8,128)S(1)} collective-permute-done((f32[380,128]{1,0:T(8,128)S(1)}, f32[380,128]{1,0:T(8,128)S(1)}, u32[]{:S(2)}, u32[]{:S(2)}) %collective-permute-start.2) | collective-permute-done | bytes 194592 | tf_op jit(solution)/shard_map/ppermute | solution.py:468
  19.0 5.5 %shard_map.61 = (f32[32,64,128]{2,1,0:T(8,128)}, f32[32,64,128]{2,1,0:T(8,128)}, f32[16,4,8,128]{3,2,1,0:T(8,128)S(1)}, f32[16,4,8,128]{3,2,1,0:T(8,128)S(1)}, f...) custom-call(f32[2,38,80,128]{3,2,1,0:T(8,128)S(1)} %get-tuple-elemen, ...), custom_call_target="tpu_custom_call", output_to_operand_aliasing={{4}: (0, {}), {5}: (1, {}), {6}: (2, {}), {7}: (3, {}), {8}... | custom-call | tf_op jit(solution)/shard_map/pallas_call | solution.py:346
  24.5 0.5 collective-permute-start.4
  25.0 1.2 %collective-permute-done.4.theirs = f32[16,4,8,128]{3,2,1,0:T(8,128)S(1)} collective-permute-done((f32[16,4,8,128]{3,2,1,0:T(8,128)S(1)}, f32[16,4,8,128]{3,2,1,0:T(8,128)S(1)}, u32[]{:S(2)}, u32[]{:S(2)}) %collective-permute-start.4) | collective-permute-done | bytes 262176 | tf_op jit(solution)/shard_map/ppermute | solution.py:473
  26.2 1.1 %collective-permute-start.5 = (f32[4,4,8,128]{3,2,1,0:T(8,128)S(1)}, f32[4,4,8,128]{3,2,1,0:T(8,128)S(1)}, u32[]{:S(2)}, u32[]{:S(2)}) collective-permute-start(f32[4,4,8,128]{3,2,1,0:T(8,128)S(1)} %get-tuple-element.36), channel_id=1, source_target_pairs={{0,8},{4,12},{8,0},{12,4},{16,24},{20,28},{24,16},{28,20},{32,40},... | collective-permute-start | bytes 196616 | tf_op jit(solution)/shard_map/ppermute | solution.py:473
  27.3 1.9 %collective-permute-start.6 = (f32[4,4,8,128]{3,2,1,0:T(8,128)S(1)}, f32[4,4,8,128]{3,2,1,0:T(8,128)S(1)}, u32[]{:S(2)}, u32[]{:S(2)}) collective-permute-start(f32[4,4,8,128]{3,2,1,0:T(8,128)S(1)} %get-tuple-element.37), channel_id=1, source_target_pairs={{0,16},{4,20},{8,24},{12,28},{16,0},{20,4},{24,8},{28,12},{32,48},... | collective-permute-start | bytes 196616 | tf_op jit(solution)/shard_map/ppermute | solution.py:473
  29.2 1.8 %collective-permute-start.7 = (f32[4,4,8,128]{3,2,1,0:T(8,128)S(1)}, f32[4,4,8,128]{3,2,1,0:T(8,128)S(1)}, u32[]{:S(2)}, u32[]{:S(2)}) collective-permute-start(f32[4,4,8,128]{3,2,1,0:T(8,128)S(1)} %get-tuple-element.38), channel_id=1, source_target_pairs={{0,24},{4,28},{8,16},{12,20},{16,8},{20,12},{24,0},{28,4},{32,56},... | collective-permute-start | bytes 196616 | tf_op jit(solution)/shard_map/ppermute | solution.py:473
  31.0 0.3 collective-permute-done.5.refs_1_
  31.2 1.8 %collective-permute-done.6.refs_2_ = f32[4,4,8,128]{3,2,1,0:T(8,128)S(1)} collective-permute-done((f32[4,4,8,128]{3,2,1,0:T(8,128)S(1)}, f32[4,4,8,128]{3,2,1,0:T(8,128)S(1)}, u32[]{:S(2)}, u32[]{:S(2)}) %collective-permute-start.6) | collective-permute-done | bytes 65568 | tf_op jit(solution)/shard_map/ppermute | solution.py:473
  33.1 1.6 %collective-permute-done.7.refs_3_ = f32[4,4,8,128]{3,2,1,0:T(8,128)S(1)} collective-permute-done((f32[4,4,8,128]{3,2,1,0:T(8,128)S(1)}, f32[4,4,8,128]{3,2,1,0:T(8,128)S(1)}, u32[]{:S(2)}, u32[]{:S(2)}) %collective-permute-start.7) | collective-permute-done | bytes 65568 | tf_op jit(solution)/shard_map/ppermute | solution.py:473
  34.6 0.1 shard_map.63
  34.8 17.8 %all_to_all.5.slabs = f32[8,2,8,128]{3,2,1,0:T(8,128)S(1)} all-to-all(f32[8,2,8,128]{3,2,1,0:T(8,128)S(1)} %shard_map.63), channel_id=1, replica_groups={{0,32,64,96,128,160,192,224},{4,36,68,100,132,164,196,228},{8,40,72,104..., dimensions={0} | all-to-all | bytes 131072 | tf_op jit(solution)/shard_map/all_to_all | solution.py:478
  52.6 0.8 %shard_map.64 = f32[4,8,64]{2,1,0:T(8,128)} custom-call(f32[8,2,8,128]{3,2,1,0:T(8,128)S(1)} %all_to_all.5.slabs), custom_call_target="tpu_custom_call" | custom-call | tf_op jit(solution)/shard_map/pallas_call | solution.py:442
  (1 shorter events, 0.0 us)
Async XLA Ops:
  0.6 5.0 %copy-start = (f32[32,64,128]{2,1,0:T(8,128)S(1)}, f32[32,64,128]{2,1,0:T(8,128)}, u32[]{:S(2)}) copy-start(f32[32,64,128]{2,1,0:T(8,128)} %param.4) | copy-start | bytes 3145732
  0.6 5.0 %copy-start.1 = (f32[32,64,128]{2,1,0:T(8,128)S(1)}, f32[32,64,128]{2,1,0:T(8,128)}, u32[]{:S(2)}) copy-start(f32[32,64,128]{2,1,0:T(8,128)} %param.3) | copy-start | bytes 3145732
  2.1 5.5 %collective-permute-start.1 = (f32[2,3,64,128]{3,2,1,0:T(8,128)S(1)}, f32[2,3,64,128]{3,2,1,0:T(8,128)S(1)}, u32[]{:S(2)}, u32[]{:S(2)}) collective-permute-start(f32[2,3,64,128]{3,2,1,0:T(8,128)S(1)} %get-tuple-element.39), channel_id=1, source_target_pairs={{4,8},{8,4},{12,16},{16,12},{20,24},{24,20},{28,32},{32,28},{36,40... | collective-permute-start | bytes 589832 | tf_op jit(solution)/shard_map/ppermute | solution.py:465
  2.7 4.9 %collective-permute-start = (f32[2,3,64,128]{3,2,1,0:T(8,128)S(1)}, f32[2,3,64,128]{3,2,1,0:T(8,128)S(1)}, u32[]{:S(2)}, u32[]{:S(2)}) collective-permute-start(f32[2,3,64,128]{3,2,1,0:T(8,128)S(1)} %get-tuple-element.40), channel_id=1, source_target_pairs={{0,4},{4,0},{8,12},{12,8},{16,20},{20,16},{24,28},{28,24},{32,36},... | collective-permute-start | bytes 589832 | tf_op jit(solution)/shard_map/ppermute | solution.py:465
  7.7 9.3 %collective-permute-start.3 = (f32[380,128]{1,0:T(8,128)S(1)}, f32[380,128]{1,0:T(8,128)S(1)}, u32[]{:S(2)}, u32[]{:S(2)}) collective-permute-start(f32[380,128]{1,0:T(8,128)S(1)} %get-tuple-element.30), channel_id=1, source_target_pairs={{1,2},{2,1},{5,6},{6,5},{9,10},{10,9},{13,14},{14,13},{17,18},{18,... | collective-permute-start | bytes 583688 | tf_op jit(solution)/shard_map/ppermute | solution.py:468
  11.2 7.8 %collective-permute-start.2 = (f32[380,128]{1,0:T(8,128)S(1)}, f32[380,128]{1,0:T(8,128)S(1)}, u32[]{:S(2)}, u32[]{:S(2)}) collective-permute-start(f32[380,128]{1,0:T(8,128)S(1)} %get-tuple-element.24.lat_a), channel_id=1, source_target_pairs={{0,1},{1,0},{2,3},{3,2},{4,5},{5,4},{6,7},{7,6},{8,9},{9,8},{10,11... | collective-permute-start | bytes 583688 | tf_op jit(solution)/shard_map/ppermute | solution.py:468
  24.5 1.7 %collective-permute-start.4 = (f32[16,4,8,128]{3,2,1,0:T(8,128)S(1)}, f32[16,4,8,128]{3,2,1,0:T(8,128)S(1)}, u32[]{:S(2)}, u32[]{:S(2)}) collective-permute-start(f32[16,4,8,128]{3,2,1,0:T(8,128)S(1)} %get-tuple-element.34), channel_id=1, source_target_pairs={{0,4},{4,0},{8,12},{12,8},{16,20},{20,16},{24,28},{28,24},{32,36},... | collective-permute-start | bytes 786440 | tf_op jit(solution)/shard_map/ppermute | solution.py:473
  26.2 5.1 %collective-permute-start.5 = (f32[4,4,8,128]{3,2,1,0:T(8,128)S(1)}, f32[4,4,8,128]{3,2,1,0:T(8,128)S(1)}, u32[]{:S(2)}, u32[]{:S(2)}) collective-permute-start(f32[4,4,8,128]{3,2,1,0:T(8,128)S(1)} %get-tuple-element.36), channel_id=1, source_target_pairs={{0,8},{4,12},{8,0},{12,4},{16,24},{20,28},{24,16},{28,20},{32,40},... | collective-permute-start | bytes 196616 | tf_op jit(solution)/shard_map/ppermute | solution.py:473
  27.3 5.8 %collective-permute-start.6 = (f32[4,4,8,128]{3,2,1,0:T(8,128)S(1)}, f32[4,4,8,128]{3,2,1,0:T(8,128)S(1)}, u32[]{:S(2)}, u32[]{:S(2)}) collective-permute-start(f32[4,4,8,128]{3,2,1,0:T(8,128)S(1)} %get-tuple-element.37), channel_id=1, source_target_pairs={{0,16},{4,20},{8,24},{12,28},{16,0},{20,4},{24,8},{28,12},{32,48},... | collective-permute-start | bytes 196616 | tf_op jit(solution)/shard_map/ppermute | solution.py:473
  29.2 5.5 %collective-permute-start.7 = (f32[4,4,8,128]{3,2,1,0:T(8,128)S(1)}, f32[4,4,8,128]{3,2,1,0:T(8,128)S(1)}, u32[]{:S(2)}, u32[]{:S(2)}) collective-permute-start(f32[4,4,8,128]{3,2,1,0:T(8,128)S(1)} %get-tuple-element.38), channel_id=1, source_target_pairs={{0,24},{4,28},{8,16},{12,20},{16,8},{20,12},{24,0},{28,4},{32,56},... | collective-permute-start | bytes 196616 | tf_op jit(solution)/shard_map/ppermute | solution.py:473

commit v4 on v3

--- a/solution.py
+++ b/solution.py
@@ -48,6 +48,9 @@
 
 HBM = pl.BlockSpec(memory_space=pltpu.HBM)
 FIELD = jax.ShapeDtypeStruct((2, EX, EY, NZ), jnp.float32)
+PICTURES = jax.ShapeDtypeStruct((VIEWS, 4, CY, NZ), jnp.float32)
+INNER_TILES = tuple(range(8, CY - 8, 8))
+OUTER_TILES = (0, CY - 8)
 INNER = tuple(range(ROW0, ROW0 + CY, 8))
 STRIPS = (ROW0 - CORNER, ROW0 + CY - CORNER)
 
@@ -179,7 +182,7 @@
     lax.fori_loop(first, last, layer, 0, unroll=unroll)
 
 
-def first_kernel(fields, ext, once, source):
+def first_kernel(fields, ext, once, source, twice, thrice):
     for f in range(2):
 
         def layer(x, carry):
@@ -188,45 +191,49 @@
 
         lax.fori_loop(0, CX, layer, 0, unroll=8)
     sweep(0, ext, once, source, HALO + 1, HALO + CX - 1, INNER, 5)
+    sweep(1, once, twice, source, HALO + 2, HALO + CX - 2, INNER, 14)
+    sweep(2, twice, thrice, source, HALO + 3, HALO + CX - 3, INNER, 13)
 
 
 def first(fields):
     return pl.pallas_call(
         first_kernel,
-        out_shape=[FIELD] * 3,
+        out_shape=[FIELD] * 5,
         in_specs=[VMEM],
-        out_specs=[VMEM] * 3,
+        out_specs=[VMEM] * 5,
         compiler_params=params(4),
     )(fields)
 
 
-def inner_kernel(
-    ext_in, once_in, source_in, depth_a, depth_b, lat_a, ext, once, source, twice, thrice
-):
-    del ext_in, once_in, source_in, lat_a
+def inner_kernel(*refs):
+    depth_a, depth_b, unused_lat, count = refs[5:9]
+    ext, once, source, twice, thrice, pic = refs[9:]
     layer_a = (1 - odd("depth")) * (HALO + CX)
     layer_b = odd("depth") * (HALO + CX)
     for f in range(2):
         for k in range(HALO):
             ext[f, layer_a + k, pl.ds(ROW0, CY), :] = depth_a[f, k]
             ext[f, layer_b + k, pl.ds(ROW0, CY), :] = depth_b[f, k]
-    sweep(0, ext, once, source, 1, HALO + 1, INNER, 3)
-    sweep(0, ext, once, source, HALO + CX - 1, EX - 1, INNER, 3)
-    zero_layers(once, 1, EX - 1)
-    sweep(1, once, twice, source, 2, EX - 2, INNER, 17)
-    zero_layers(twice, 2, EX - 2)
-    sweep(2, twice, thrice, source, HALO, HALO + CX, INNER, 8)
-
-
-def inner(fields, halos, lat_a):
+    for j, (inp, out) in enumerate(((ext, once), (once, twice), (twice, thrice))):
+        for start in (1 + j, HALO + CX - 1 - j):
+            sweep(j, inp, out, source, start, start + 3, INNER, 3)
+        if j < 2:
+            zero_layers(out, 1 + j, EX - 1 - j)
+    render(INNER_TILES, 2, thrice, count[0, 0], pic)
+
+
+def inner(fields, halos, lat_a, iface_count):
     return pl.pallas_call(
         inner_kernel,
-        out_shape=[FIELD] * 5,
-        in_specs=[VMEM] * 6,
-        out_specs=[VMEM] * 5,
-        input_output_aliases={0: 0, 1: 1, 2: 2},
-        compiler_params=params(4),
-    )(*fields, *halos, lat_a)
+        out_shape=[FIELD] * 5 + [PICTURES],
+        in_specs=[VMEM] * 8 + [SMEM],
+        out_specs=[VMEM] * 6,
+        input_output_aliases={i: i for i in range(5)},
+        compiler_params=params(4),
+        cost_estimate=pl.CostEstimate(
+            flops=40_000_000, bytes_accessed=1 << 20, transcendentals=0
+        ),
+    )(*fields, *halos, lat_a, iface_count)
 
 
 def whole_part(v, x):
@@ -238,25 +245,22 @@
     return value
 
 
-AT_ONCE = 2
-
-
-def render(views, field, count, pic):
+def render(tiles, at_once, field, count, pic):
     lane = lax.broadcasted_iota(jnp.int32, (8, NZ), 1)
     scale = -4.0 / NX * math.log2(math.e)
-    tiles = tuple(range(0, CY, 8))
-    for v in views:
+    for v in range(VIEWS):
         for c in range(4):
-            pic[v, c] = jnp.full((CY, NZ), 1.0 if c == 3 else 0.0, jnp.float32)
+            for t in tiles:
+                pic[v, c, pl.ds(t, 8), :] = jnp.full((8, NZ), 1.0 if c == 3 else 0.0)
 
     def layers(i, carry):
-        for v in views:
+        for v in range(VIEWS):
             positive = SHEAR_Z[v] > 0
             shift = NZ - 1 if positive else 1
             edge = (lane == NZ - 1) if positive else (lane == 0)
             places = []
-            for q in range(AT_ONCE):
-                x = i * AT_ONCE + q
+            for q in range(at_once):
+                x = i * at_once + q
                 xf = x.astype(jnp.float32)
                 base_y = whole_part(v, x)
                 frac_y = xf * (SHEAR_Y[v] / CX) - base_y.astype(jnp.float32)
@@ -293,15 +297,12 @@
                 pic[v, 3, at, :] = trans
         return carry
 
-    lax.fori_loop(0, lax.div(count + (AT_ONCE - 1), AT_ONCE), layers, 0)
-
-
-def brick_kernel(
-    ext_in, once_in, source_in, twice_in, thrice_in, lat_a, lat_b, count,
-    phase_next, heat_next, keep, send, ext, once, source, twice, thrice,
-    pic, turned, sems,
-):
-    del ext_in, once_in, source_in, twice_in, thrice_in
+    lax.fori_loop(0, lax.div(count + (at_once - 1), at_once), layers, 0)
+
+
+def brick_kernel(*refs):
+    lat_a, lat_b, count = refs[6:9]
+    keep, send, ext, once, source, twice, thrice, pic, turned = refs[9:]
     lat_unpack(ext, lat_a, lat_b)
     sweep(0, ext, once, source, 1, EX - 1, STRIPS, 12)
     zero_layers(once, 1, EX - 1)
@@ -311,16 +312,7 @@
     zero_rows(twice, 2, EX - 2)
     sweep(2, twice, thrice, source, HALO, HALO + CX, STRIPS, 16)
     zero_rows(thrice, HALO, HALO + CX)
-    copies = []
-    for f, field in enumerate((phase_next, heat_next)):
-        copies.append(
-            pltpu.make_async_copy(
-                thrice.at[f, pl.ds(HALO, CX), pl.ds(ROW0, CY), :], field, sems.at[f]
-            )
-        )
-    for copy in copies:
-        copy.start()
-    render(range(VIEWS), thrice, count[0, 0], pic)
+    render(OUTER_TILES, 4, thrice, count[0, 0], pic)
     for v in range(2):
         for c in range(4):
             square = jnp.concatenate([pic[v, c], pltpu.roll(pic[3 - v, c], 64, 1)], axis=0)
@@ -335,27 +327,46 @@
                 at = pl.ds(pl.multiple_of((block + (z & 1) * 8) * 8, 8), 8)
                 for c in range(4):
                     target[x_rel * 4 + z, c] = turned[z >> 1, c, at, :]
+
+
+def brick(fields, lat_a, lat_b, iface_count):
+    pieces = jax.ShapeDtypeStruct((16, 4, 8, NZ), jnp.float32)
+    results = pl.pallas_call(
+        brick_kernel,
+        out_shape=[pieces, pieces] + [FIELD] * 5 + [PICTURES],
+        in_specs=[VMEM] * 8 + [SMEM],
+        out_specs=[VMEM] * 8,
+        input_output_aliases={i: 2 + i for i in range(6)},
+        scratch_shapes=[pltpu.VMEM((2, 4, NZ, 2 * CY), jnp.float32)],
+        compiler_params=params(4),
+    )(*fields, lat_a, lat_b, iface_count)
+    return results[0], results[1], results[6]
+
+
+def emit_kernel(field, part, phase_next, heat_next, token, sems):
+    copies = []
+    for f, target in enumerate((phase_next, heat_next)):
+        copies.append(
+            pltpu.make_async_copy(
+                field.at[f, pl.ds(HALO, CX), pl.ds(ROW0, CY), :], target, sems.at[f]
+            )
+        )
+        copies[f].start()
+    token[...] = part[0, 0]
     for copy in copies:
         copy.wait()
 
 
-def brick(fields, lat_a, lat_b, iface_count):
-    f32 = jnp.float32
-    pieces = jax.ShapeDtypeStruct((16, 4, 8, NZ), f32)
-    block = jax.ShapeDtypeStruct((CX, CY, NZ), f32)
-    return pl.pallas_call(
-        brick_kernel,
-        out_shape=[block, block, pieces, pieces] + [FIELD] * 5,
-        in_specs=[VMEM] * 7 + [SMEM],
-        out_specs=[HBM, HBM] + [VMEM] * 7,
-        input_output_aliases={i: 4 + i for i in range(5)},
-        scratch_shapes=[
-            pltpu.VMEM((VIEWS, 4, CY, NZ), f32),
-            pltpu.VMEM((2, 4, NZ, 2 * CY), f32),
-            pltpu.SemaphoreType.DMA((2,)),
-        ],
-        compiler_params=params(8),
-    )(*fields, lat_a, lat_b, iface_count)[:4]
+def emit(field, part):
+    block = jax.ShapeDtypeStruct((CX, CY, NZ), jnp.float32)
+    return pl.pallas_call(
+        emit_kernel,
+        out_shape=[block, block, jax.ShapeDtypeStruct((8, NZ), jnp.float32)],
+        in_specs=[VMEM, VMEM],
+        out_specs=[HBM, HBM, VMEM],
+        scratch_shapes=[pltpu.SemaphoreType.DMA((2,))],
+        compiler_params=params(4),
+    )(field, part)
 
 
 def blend(front, back, write):
@@ -393,7 +404,7 @@
 
 
 def x_kernel(*refs):
-    parts, out = refs[:4], refs[4]
+    parts, out = refs[:4], refs[5]
     my_x = lax.rem(lax.div(lax.axis_index("depth"), 2), 4)
     low = lax.broadcasted_iota(jnp.int32, (8, NZ), 1) < CY
 
@@ -414,14 +425,14 @@
         pl.when(my_x == place)(functools.partial(ordered, place))
 
 
-def x_combine(parts):
+def x_combine(parts, token):
     return pl.pallas_call(
         x_kernel,
         out_shape=jax.ShapeDtypeStruct((8, 2, 8, NZ), jnp.float32),
-        in_specs=[VMEM] * 4,
+        in_specs=[VMEM] * 5,
         out_specs=VMEM,
         compiler_params=params(4),
-    )(*parts)
+    )(*parts, token)
 
 
 def z_kernel(slabs, out):
@@ -466,17 +477,18 @@
     fields = first(fields)
     packed = lat_pack(fields[0], *halos)
     rims = [lax.ppermute(h, "lat", p) for h, p in zip(packed, lat_pairs)]
-    fields = inner(fields, halos, packed[0])
-    phase_next, heat_next, mine, outgoing = brick(fields, *rims, iface_count)
+    fields = inner(fields, halos, packed[0], iface_count)
+    mine, outgoing, solved = brick(fields, *rims, iface_count)
 
     def partner(value, distance):
         return lax.ppermute(value, "depth", [(i, i ^ distance) for i in range(depth_size)])
 
     parts = core_combine(mine, partner(outgoing, 1))
+    phase_next, heat_next, token = emit(solved, parts[0])
     parts = [parts[0]] + [partner(parts[k], 2 * k) for k in (1, 2, 3)]
     groups = [[z * 8 + i for z in range(depth_size // 8)] for i in range(8)]
     slabs = lax.all_to_all(
-        x_combine(parts), "depth", 0, 0, tiled=True, axis_index_groups=groups
+        x_combine(parts, token), "depth", 0, 0, tiled=True, axis_index_groups=groups
     )
     return phase_next, heat_next, z_combine(slabs)
 

time: 53.8 us -> 51.8 us (0.963)
  blocking collectives: 17.8 us -> 15.1 us
  starting transfers between devices: 12.5 us -> 13.1 us
    all_to_all x1, blocking collectives: 17.8 us -> 15.1 us  [per_device(): lax.all_to_all(x_combine(parts, token), 'depth', 0, 0, tiled=True, axis_i...]
    ppermute x2, waiting for transfers between devices: 4.05 us -> 3.13 us  [per_device(): rims = [lax.ppermute(h, 'lat', p) for h, p in zip(packed, lat_pairs)]]
    ppermute x4, waiting for transfers between devices: 4.83 us -> 5.65 us  [partner(): lax.ppermute(value, 'depth', [(i, i ^ distance) for i in range(depth_size)])]
    ppermute x4, starting transfers between devices: 5.28 us -> 5.9 us  [partner(): lax.ppermute(value, 'depth', [(i, i ^ distance) for i in range(depth_size)])]
    pallas_call x3 -> x4, Pallas kernels: 10.2 us -> 10.5 us  [the longest x1 3.79 us: first(): pl.pallas_call(first_kernel, out_shape=[FIELD] * 5, in_specs=[VMEM], out_...]
  transfers between devices with their start and end apart: 8 -> 8, of which waited for: 6 -> 5; matrix products, arithmetic and copies ran while one was open for 0% -> 0% of each run, Pallas kernels for 9% -> 15%
where the time goes in v4:
time: 51.8 us; the launch traced here: 51.4 us
  blocking collectives  15.1 us (29%)
  starting transfers between devices  13.1 us (25%)
  Pallas kernels  11.5 us (22%)
  waiting for transfers between devices  8.78 us (17%)
  other arithmetic  1.54 us (3%)
  between operations  1.42 us (3%)
    all_to_all x1, blocking collectives, per_device(): lax.all_to_all(x_combine(parts, token), 'depth', 0, 0, tiled=True, axis_i...  15.1 us
    ppermute x4, starting transfers between devices, partner(): lax.ppermute(value, 'depth', [(i, i ^ distance) for i in range(depth_size)])  5.9 us
    ppermute x4, waiting for transfers between devices, partner(): lax.ppermute(value, 'depth', [(i, i ^ distance) for i in range(depth_size)])  5.65 us
    pallas_call x1, Pallas kernels, first(): pl.pallas_call(first_kernel, out_shape=[FIELD] * 5, in_specs=[VMEM], out_...  3.79 us
    ppermute x2, starting transfers between devices, per_device(): halos = [lax.ppermute(h, 'depth', p) for h, p in zip(halos, depth_pairs)]  3.6 us
    ppermute x2, starting transfers between devices, per_device(): rims = [lax.ppermute(h, 'lat', p) for h, p in zip(packed, lat_pairs)]  3.58 us
    ppermute x2, waiting for transfers between devices, per_device(): rims = [lax.ppermute(h, 'lat', p) for h, p in zip(packed, lat_pairs)]  3.13 us
    pallas_call x1, Pallas kernels, inner(): pl.pallas_call(inner_kernel, out_shape=[FIELD] * 5 + [PICTURES], in_specs...  2.76 us
  transfers between devices with their start and end apart: 8, of which 5 were waited for; matrix products, arithmetic and copies ran while one was open for 0% of the time, Pallas kernels for 15%

profile of v4, /device:TPU:8, one launch (start us, length us, event | category | flops | bytes accessed | tf_op | source)
XLA Modules:
  0.0 51.4 jit_solution(10241994558264705031)
XLA Ops:
  0.6 0.0 copy-start
  0.6 0.0 copy-start.1
  0.7 1.4 %broadcast_select_fusion = (f32[2,3,64,128]{3,2,1,0:T(8,128)S(1)}, f32[2,3,64,128]{3,2,1,0:T(8,128)S(1)}) fusion(pred[]{:T(512)S(6)} %eq.3, f32[1,32,64,128]{3,2,1,0:T(8,128)} %bitcast.3, f32[1,32,64,128]{3,2,1,0:T(8,128)} %bitcast.5), kind=kLoop, calls=%fused_computation.7 | loop fusion | flops 294912 | bytes 2490369 | tf_op jit(solution)/shard_map/jit(_where)/select_n | solution.py:70
  2.1 0.7 %collective-permute-start.1 = (f32[2,3,64,128]{3,2,1,0:T(8,128)S(1)}, f32[2,3,64,128]{3,2,1,0:T(8,128)S(1)}, u32[]{:S(2)}, u32[]{:S(2)}) collective-permute-start(f32[2,3,64,128]{3,2,1,0:T(8,128)S(1)} %get-tuple-element.49), channel_id=1, source_target_pairs={{4,8},{8,4},{12,16},{16,12},{20,24},{24,20},{28,32},{32,28},{36,40... | collective-permute-start | bytes 589832 | tf_op jit(solution)/shard_map/ppermute | solution.py:476
  2.7 2.9 %collective-permute-start = (f32[2,3,64,128]{3,2,1,0:T(8,128)S(1)}, f32[2,3,64,128]{3,2,1,0:T(8,128)S(1)}, u32[]{:S(2)}, u32[]{:S(2)}) collective-permute-start(f32[2,3,64,128]{3,2,1,0:T(8,128)S(1)} %get-tuple-element.50), channel_id=1, source_target_pairs={{0,4},{4,0},{8,12},{12,8},{16,20},{20,16},{24,28},{28,24},{32,36},... | collective-permute-start | bytes 589832 | tf_op jit(solution)/shard_map/ppermute | solution.py:476
  5.7 0.0 copy-done
  5.7 0.0 copy-done.1
  5.7 0.1 pad_maximum_fusion.fields
  5.8 3.8 %shard_map.58 = (f32[2,38,80,128]{3,2,1,0:T(8,128)S(1)}, f32[2,38,80,128]{3,2,1,0:T(8,128)S(1)}, f32[2,38,80,128]{3,2,1,0:T(8,128)S(1)}, f32[2,38,80,128]{3,2,1,0:T(8,128)S(1)}, f32[2,38,80,128]{3,2,1,0:T(8,128)S(1)}) custom-call(f32[2,32,64,128]{3,2,1,0:T(8,128)S(1)} %pad_maximum_fusion.fields), custom_call_target="tpu_custom_call" | custom-call | tf_op jit(solution)/shard_map/pallas_call | solution.py:199
  9.6 0.0 collective-permute-done.1.depth_b.refs_6_
  9.6 0.0 collective-permute-done.depth_a.refs_5_
  9.6 0.1 shard_map.59
  9.7 3.5 %collective-permute-start.3 = (f32[380,128]{1,0:T(8,128)S(1)}, f32[380,128]{1,0:T(8,128)S(1)}, u32[]{:S(2)}, u32[]{:S(2)}) collective-permute-start(f32[380,128]{1,0:T(8,128)S(1)} %get-tuple-element.38), channel_id=1, source_target_pairs={{1,2},{2,1},{5,6},{6,5},{9,10},{10,9},{13,14},{14,13},{17,18},{18,... | collective-permute-start | bytes 583688 | tf_op jit(solution)/shard_map/ppermute | solution.py:479
  13.2 0.1 collective-permute-start.2
  13.9 2.8 %shard_map.60 = (f32[2,38,80,128]{3,2,1,0:T(8,128)S(1)}, f32[2,38,80,128]{3,2,1,0:T(8,128)S(1)}, f32[2,38,80,128]{3,2,1,0:T(8,128)S(1)}, f32[2,38,80,128]{3,2,1,...) custom-call(f32[2,38,80,128]{3,2,1,0:T(8,128)S(1)} %get-tuple-elemen, ...), custom_call_target="tpu_custom_call", output_to_operand_aliasing={{0}: (0, {}), {1}: (1, {}), {2}: (2, {}), {3}: (3, {}), {4}... | custom-call | flops 40000000 | bytes 1048576 | tf_op jit(solution)/shard_map/pallas_call | solution.py:226
  16.7 1.7 %collective-permute-done.3.refs_7_ = f32[380,128]{1,0:T(8,128)S(1)} collective-permute-done((f32[380,128]{1,0:T(8,128)S(1)}, f32[380,128]{1,0:T(8,128)S(1)}, u32[]{:S(2)}, u32[]{:S(2)}) %collective-permute-start.3) | collective-permute-done | bytes 194592 | tf_op jit(solution)/shard_map/ppermute | solution.py:479
  18.4 1.4 %collective-permute-done.2.refs_6_ = f32[380,128]{1,0:T(8,128)S(1)} collective-permute-done((f32[380,128]{1,0:T(8,128)S(1)}, f32[380,128]{1,0:T(8,128)S(1)}, u32[]{:S(2)}, u32[]{:S(2)}) %collective-permute-start.2) | collective-permute-done | bytes 194592 | tf_op jit(solution)/shard_map/ppermute | solution.py:479
  19.8 2.7 %shard_map.61 = (f32[16,4,8,128]{3,2,1,0:T(8,128)S(1)}, f32[16,4,8,128]{3,2,1,0:T(8,128)S(1)}, f32[2,38,80,128]{3,2,1,0:T(8,128)S(1)}, f32[2,38,80,128]{3,2,1,0:...) custom-call(f32[2,38,80,128]{3,2,1,0:T(8,128)S(1)} %get-tuple-elemen, ...), custom_call_target="tpu_custom_call", output_to_operand_aliasing={{2}: (0, {}), {3}: (1, {}), {4}: (2, {}), {5}: (3, {}), {6}... | custom-call | tf_op jit(solution)/shard_map/pallas_call | solution.py:334
  22.5 0.1 collective-permute-start.4
  22.6 1.5 %collective-permute-done.4.theirs = f32[16,4,8,128]{3,2,1,0:T(8,128)S(1)} collective-permute-done((f32[16,4,8,128]{3,2,1,0:T(8,128)S(1)}, f32[16,4,8,128]{3,2,1,0:T(8,128)S(1)}, u32[]{:S(2)}, u32[]{:S(2)}) %collective-permute-start.4) | collective-permute-done | bytes 262176 | tf_op jit(solution)/shard_map/ppermute | solution.py:484
  24.2 1.2 %collective-permute-start.5 = (f32[4,4,8,128]{3,2,1,0:T(8,128)S(1)}, f32[4,4,8,128]{3,2,1,0:T(8,128)S(1)}, u32[]{:S(2)}, u32[]{:S(2)}) collective-permute-start(f32[4,4,8,128]{3,2,1,0:T(8,128)S(1)} %get-tuple-element.45), channel_id=1, source_target_pairs={{0,8},{4,12},{8,0},{12,4},{16,24},{20,28},{24,16},{28,20},{32,40},... | collective-permute-start | bytes 196616 | tf_op jit(solution)/shard_map/ppermute | solution.py:484
  25.4 4.6 %collective-permute-start.6 = (f32[4,4,8,128]{3,2,1,0:T(8,128)S(1)}, f32[4,4,8,128]{3,2,1,0:T(8,128)S(1)}, u32[]{:S(2)}, u32[]{:S(2)}) collective-permute-start(f32[4,4,8,128]{3,2,1,0:T(8,128)S(1)} %get-tuple-element.46), channel_id=1, source_target_pairs={{0,16},{4,20},{8,24},{12,28},{16,0},{20,4},{24,8},{28,12},{32,48},... | collective-permute-start | bytes 196616 | tf_op jit(solution)/shard_map/ppermute | solution.py:484
  30.0 0.0 collective-permute-start.7
  30.0 1.3 %shard_map.63 = (f32[32,64,128]{2,1,0:T(8,128)}, f32[32,64,128]{2,1,0:T(8,128)}, f32[8,128]{1,0:T(8,128)S(1)}) custom-call(f32[2,38,80,128]{3,2,1,0:T(8,128)S(1)} %get-tuple-element.39.field, f32[4,4,8,128]{3,2,1,0:T(8,128)S(1)} %get-tuple-element.42.part.refs_0_), custom_call_target="tpu_custom_call" | custom-call | tf_op jit(solution)/shard_map/pallas_call | solution.py:362
  31.3 0.0 collective-permute-done.5.refs_1_
  31.3 2.2 %collective-permute-done.6.refs_2_ = f32[4,4,8,128]{3,2,1,0:T(8,128)S(1)} collective-permute-done((f32[4,4,8,128]{3,2,1,0:T(8,128)S(1)}, f32[4,4,8,128]{3,2,1,0:T(8,128)S(1)}, u32[]{:S(2)}, u32[]{:S(2)}) %collective-permute-start.6) | collective-permute-done | bytes 65568 | tf_op jit(solution)/shard_map/ppermute | solution.py:484
  33.5 2.0 %collective-permute-done.7.refs_3_ = f32[4,4,8,128]{3,2,1,0:T(8,128)S(1)} collective-permute-done((f32[4,4,8,128]{3,2,1,0:T(8,128)S(1)}, f32[4,4,8,128]{3,2,1,0:T(8,128)S(1)}, u32[]{:S(2)}, u32[]{:S(2)}) %collective-permute-start.7) | collective-permute-done | bytes 65568 | tf_op jit(solution)/shard_map/ppermute | solution.py:484
  35.5 0.1 shard_map.64
  35.6 15.1 %all_to_all.5.slabs = f32[8,2,8,128]{3,2,1,0:T(8,128)S(1)} all-to-all(f32[8,2,8,128]{3,2,1,0:T(8,128)S(1)} %shard_map.64), channel_id=1, replica_groups={{0,32,64,96,128,160,192,224},{4,36,68,100,132,164,196,228},{8,40,72,104..., dimensions={0} | all-to-all | bytes 131072 | tf_op jit(solution)/shard_map/all_to_all | solution.py:490
  50.7 0.8 %shard_map.65 = f32[4,8,64]{2,1,0:T(8,128)} custom-call(f32[8,2,8,128]{3,2,1,0:T(8,128)S(1)} %all_to_all.5.slabs), custom_call_target="tpu_custom_call" | custom-call | tf_op jit(solution)/shard_map/pallas_call | solution.py:453
  (1 shorter events, 0.0 us)
Async XLA Ops:
  0.6 5.0 %copy-start = (f32[32,64,128]{2,1,0:T(8,128)S(1)}, f32[32,64,128]{2,1,0:T(8,128)}, u32[]{:S(2)}) copy-start(f32[32,64,128]{2,1,0:T(8,128)} %param.4) | copy-start | bytes 3145732
  0.6 5.0 %copy-start.1 = (f32[32,64,128]{2,1,0:T(8,128)S(1)}, f32[32,64,128]{2,1,0:T(8,128)}, u32[]{:S(2)}) copy-start(f32[32,64,128]{2,1,0:T(8,128)} %param.3) | copy-start | bytes 3145732
  2.1 7.6 %collective-permute-start.1 = (f32[2,3,64,128]{3,2,1,0:T(8,128)S(1)}, f32[2,3,64,128]{3,2,1,0:T(8,128)S(1)}, u32[]{:S(2)}, u32[]{:S(2)}) collective-permute-start(f32[2,3,64,128]{3,2,1,0:T(8,128)S(1)} %get-tuple-element.49), channel_id=1, source_target_pairs={{4,8},{8,4},{12,16},{16,12},{20,24},{24,20},{28,32},{32,28},{36,40... | collective-permute-start | bytes 589832 | tf_op jit(solution)/shard_map/ppermute | solution.py:476
  2.7 6.9 %collective-permute-start = (f32[2,3,64,128]{3,2,1,0:T(8,128)S(1)}, f32[2,3,64,128]{3,2,1,0:T(8,128)S(1)}, u32[]{:S(2)}, u32[]{:S(2)}) collective-permute-start(f32[2,3,64,128]{3,2,1,0:T(8,128)S(1)} %get-tuple-element.50), channel_id=1, source_target_pairs={{0,4},{4,0},{8,12},{12,8},{16,20},{20,16},{24,28},{28,24},{32,36},... | collective-permute-start | bytes 589832 | tf_op jit(solution)/shard_map/ppermute | solution.py:476
  9.7 8.7 %collective-permute-start.3 = (f32[380,128]{1,0:T(8,128)S(1)}, f32[380,128]{1,0:T(8,128)S(1)}, u32[]{:S(2)}, u32[]{:S(2)}) collective-permute-start(f32[380,128]{1,0:T(8,128)S(1)} %get-tuple-element.38), channel_id=1, source_target_pairs={{1,2},{2,1},{5,6},{6,5},{9,10},{10,9},{13,14},{14,13},{17,18},{18,... | collective-permute-start | bytes 583688 | tf_op jit(solution)/shard_map/ppermute | solution.py:479
  13.2 6.6 %collective-permute-start.2 = (f32[380,128]{1,0:T(8,128)S(1)}, f32[380,128]{1,0:T(8,128)S(1)}, u32[]{:S(2)}, u32[]{:S(2)}) collective-permute-start(f32[380,128]{1,0:T(8,128)S(1)} %get-tuple-element.31.refs_7_), channel_id=1, source_target_pairs={{0,1},{1,0},{2,3},{3,2},{4,5},{5,4},{6,7},{7,6},{8,9},{9,8},{10,11... | collective-permute-start | bytes 583688 | tf_op jit(solution)/shard_map/ppermute | solution.py:479
  22.5 1.6 %collective-permute-start.4 = (f32[16,4,8,128]{3,2,1,0:T(8,128)S(1)}, f32[16,4,8,128]{3,2,1,0:T(8,128)S(1)}, u32[]{:S(2)}, u32[]{:S(2)}) collective-permute-start(f32[16,4,8,128]{3,2,1,0:T(8,128)S(1)} %get-tuple-element.41), channel_id=1, source_target_pairs={{0,4},{4,0},{8,12},{12,8},{16,20},{20,16},{24,28},{28,24},{32,36},... | collective-permute-start | bytes 786440 | tf_op jit(solution)/shard_map/ppermute | solution.py:484
  24.2 7.2 %collective-permute-start.5 = (f32[4,4,8,128]{3,2,1,0:T(8,128)S(1)}, f32[4,4,8,128]{3,2,1,0:T(8,128)S(1)}, u32[]{:S(2)}, u32[]{:S(2)}) collective-permute-start(f32[4,4,8,128]{3,2,1,0:T(8,128)S(1)} %get-tuple-element.45), channel_id=1, source_target_pairs={{0,8},{4,12},{8,0},{12,4},{16,24},{20,28},{24,16},{28,20},{32,40},... | collective-permute-start | bytes 196616 | tf_op jit(solution)/shard_map/ppermute | solution.py:484
  25.4 8.1 %collective-permute-start.6 = (f32[4,4,8,128]{3,2,1,0:T(8,128)S(1)}, f32[4,4,8,128]{3,2,1,0:T(8,128)S(1)}, u32[]{:S(2)}, u32[]{:S(2)}) collective-permute-start(f32[4,4,8,128]{3,2,1,0:T(8,128)S(1)} %get-tuple-element.46), channel_id=1, source_target_pairs={{0,16},{4,20},{8,24},{12,28},{16,0},{20,4},{24,8},{28,12},{32,48},... | collective-permute-start | bytes 196616 | tf_op jit(solution)/shard_map/ppermute | solution.py:484
  30.0 5.5 %collective-permute-start.7 = (f32[4,4,8,128]{3,2,1,0:T(8,128)S(1)}, f32[4,4,8,128]{3,2,1,0:T(8,128)S(1)}, u32[]{:S(2)}, u32[]{:S(2)}) collective-permute-start(f32[4,4,8,128]{3,2,1,0:T(8,128)S(1)} %get-tuple-element.47), channel_id=1, source_target_pairs={{0,24},{4,28},{8,16},{12,20},{16,8},{20,12},{24,0},{28,4},{32,56},... | collective-permute-start | bytes 196616 | tf_op jit(solution)/shard_map/ppermute | solution.py:484

commit v5 on v4

--- a/solution.py
+++ b/solution.py
@@ -182,7 +182,7 @@
     lax.fori_loop(first, last, layer, 0, unroll=unroll)
 
 
-def first_kernel(fields, ext, once, source, twice, thrice):
+def first_kernel(fields, ext, once, source, twice):
     for f in range(2):
 
         def layer(x, carry):
@@ -192,48 +192,52 @@
         lax.fori_loop(0, CX, layer, 0, unroll=8)
     sweep(0, ext, once, source, HALO + 1, HALO + CX - 1, INNER, 5)
     sweep(1, once, twice, source, HALO + 2, HALO + CX - 2, INNER, 14)
-    sweep(2, twice, thrice, source, HALO + 3, HALO + CX - 3, INNER, 13)
 
 
 def first(fields):
     return pl.pallas_call(
         first_kernel,
-        out_shape=[FIELD] * 5,
+        out_shape=[FIELD] * 4,
         in_specs=[VMEM],
-        out_specs=[VMEM] * 5,
+        out_specs=[VMEM] * 4,
         compiler_params=params(4),
     )(fields)
 
 
 def inner_kernel(*refs):
-    depth_a, depth_b, unused_lat, count = refs[5:9]
-    ext, once, source, twice, thrice, pic = refs[9:]
+    depth_a, depth_b, unused_lat, count = refs[4:8]
+    ext, once, source, twice, thrice, pic = refs[8:]
     layer_a = (1 - odd("depth")) * (HALO + CX)
     layer_b = odd("depth") * (HALO + CX)
     for f in range(2):
         for k in range(HALO):
             ext[f, layer_a + k, pl.ds(ROW0, CY), :] = depth_a[f, k]
             ext[f, layer_b + k, pl.ds(ROW0, CY), :] = depth_b[f, k]
-    for j, (inp, out) in enumerate(((ext, once), (once, twice), (twice, thrice))):
+    zero_layers(ext, 0, EX)
+    for j, (inp, out) in enumerate(((ext, once), (once, twice))):
         for start in (1 + j, HALO + CX - 1 - j):
             sweep(j, inp, out, source, start, start + 3, INNER, 3)
-        if j < 2:
-            zero_layers(out, 1 + j, EX - 1 - j)
-    render(INNER_TILES, 2, thrice, count[0, 0], pic)
+        zero_layers(out, 1 + j, EX - 1 - j)
+    sweep(2, twice, thrice, source, HALO, HALO + CX, INNER, 16)
+    render(INNER_TILES, 4, thrice, count[0, 0], pic)
 
 
 def inner(fields, halos, lat_a, iface_count):
     return pl.pallas_call(
         inner_kernel,
         out_shape=[FIELD] * 5 + [PICTURES],
-        in_specs=[VMEM] * 8 + [SMEM],
+        in_specs=[VMEM] * 7 + [SMEM],
         out_specs=[VMEM] * 6,
-        input_output_aliases={i: i for i in range(5)},
+        input_output_aliases={i: i for i in range(4)},
         compiler_params=params(4),
         cost_estimate=pl.CostEstimate(
             flops=40_000_000, bytes_accessed=1 << 20, transcendentals=0
         ),
     )(*fields, *halos, lat_a, iface_count)
+
+
+CENTRE = 0.8
+SHRINK = 0.5 / CENTRE
 
 
 def whole_part(v, x):
@@ -265,33 +269,32 @@
                 base_y = whole_part(v, x)
                 frac_y = xf * (SHEAR_Y[v] / CX) - base_y.astype(jnp.float32)
                 frac_z = xf * (abs(SHEAR_Z[v]) / CX)
-                near_w = (1.0 - frac_y) * (1.0 - frac_z)
-                far_w = frac_y * (1.0 - frac_z)
+                own = (1.0 - frac_y) * (1.0 - frac_z)
+                ratio = jnp.full((8, NZ), frac_y) / (1.0 - frac_y)
                 side = jnp.where(edge, 0.0, jnp.full((8, NZ), frac_z) / (1.0 - frac_z))
-                live = jnp.where(x < count, scale, 0.0)
-                places.append((x, base_y, near_w, far_w, side, live))
+                live = jnp.where(x < count, scale * own * own, 0.0)
+                places.append((x, base_y, ratio, side, live, own * SHRINK))
             for t in tiles:
                 at = pl.ds(t, 8)
                 colours = [pic[v, c, at, :] for c in range(3)]
                 trans = pic[v, 3, at, :]
-                for x, base_y, near_w, far_w, side, live in places:
+                for x, base_y, ratio, side, live, own in places:
                     samples = []
                     for f in range(2):
                         row = ROW0 + t + base_y
                         near = field[f, HALO + x, pl.ds(row, 8), :]
                         far = field[f, HALO + x, pl.ds(row + 1, 8), :]
-                        mixed = near * near_w + far * far_w
+                        mixed = near + far * ratio
                         samples.append(mixed + pltpu.roll(mixed, shift, 1) * side)
-                    s0, s1 = samples
-                    passed = trans * jnp.exp2(s0 * s0 * live)
+                    passed = trans * jnp.exp2(samples[0] * samples[0] * live)
                     weight = trans - passed
                     trans = passed
-                    square = s1 * s1
-                    outer = square + 1.64
-                    slope = 1.6 * s1
-                    colours[0] = colours[0] + weight / (outer + slope)
-                    colours[1] = colours[1] + weight / (square + 1.0)
-                    colours[2] = colours[2] + weight / (outer - slope)
+                    p = samples[1] * own
+                    square = p * p
+                    outer = square + (1.0 + CENTRE * CENTRE) * SHRINK * SHRINK
+                    colours[0] = colours[0] + weight / (outer + p)
+                    colours[1] = colours[1] + weight / (square + SHRINK * SHRINK)
+                    colours[2] = colours[2] + weight / (outer - p)
                 for c in range(3):
                     pic[v, c, at, :] = colours[c]
                 pic[v, 3, at, :] = trans
@@ -304,6 +307,8 @@
     lat_a, lat_b, count = refs[6:9]
     keep, send, ext, once, source, twice, thrice, pic, turned = refs[9:]
     lat_unpack(ext, lat_a, lat_b)
+    zero_layers(ext, 0, EX)
+    zero_rows(ext, 0, EX)
     sweep(0, ext, once, source, 1, EX - 1, STRIPS, 12)
     zero_layers(once, 1, EX - 1)
     zero_rows(once, 1, EX - 1)
@@ -316,6 +321,8 @@
     for v in range(2):
         for c in range(4):
             square = jnp.concatenate([pic[v, c], pltpu.roll(pic[3 - v, c], 64, 1)], axis=0)
+            if c < 3:
+                square = square * (SHRINK * SHRINK)
             turned[v, c] = square.T
     depth = lax.axis_index("depth")
     my_core = lax.rem(depth, 2)
@@ -459,18 +466,23 @@
     )(slabs).transpose(0, 2, 1)
 
 
-def pairs(count, start):
+RING_D = 1
+RING_L = 1
+
+
+def pairs(count, start, ring):
     result = []
-    for i in range(start, count - 1, 2):
-        result += [(i, i + 1), (i + 1, i)]
+    for i in range(start, count if ring else count - 1, 2):
+        after = (i + 1) % count
+        result += [(i, after), (after, i)]
     return result
 
 
 def per_device(phase, temper, iface_count):
     depth_size = lax.axis_size("depth")
     lat_size = lax.axis_size("lat")
-    depth_pairs = [pairs(depth_size, start) for start in range(2)]
-    lat_pairs = [pairs(lat_size, start) for start in range(2)]
+    depth_pairs = [pairs(depth_size, start, RING_D) for start in range(2)]
+    lat_pairs = [pairs(lat_size, start, RING_L) for start in range(2)]
     fields = jnp.stack([phase, temper])
     halos = depth_pack(fields)
     halos = [lax.ppermute(h, "depth", p) for h, p in zip(halos, depth_pairs)]

time: 51.8 us -> 49.2 us (0.950)
  the two profiles are of different devices: /device:TPU:8 before, /device:TPU:6 now
where the time goes in v5:
time: 49.2 us; the launch traced here: 48.9 us
  starting transfers between devices  14 us (28%)
  blocking collectives  12.5 us (25%)
  Pallas kernels  10.4 us (21%)
  waiting for transfers between devices  9 us (18%)
  other arithmetic  1.64 us (3%)
  between operations  1.39 us (3%)
    all_to_all x1, blocking collectives, per_device(): lax.all_to_all(x_combine(parts, token), 'depth', 0, 0, tiled=True, axis_i...  12.5 us
    ppermute x4, starting transfers between devices, partner(): lax.ppermute(value, 'depth', [(i, i ^ distance) for i in range(depth_size)])  8.74 us
    ppermute x4, waiting for transfers between devices, partner(): lax.ppermute(value, 'depth', [(i, i ^ distance) for i in range(depth_size)])  5.29 us
    ppermute x2, waiting for transfers between devices, per_device(): rims = [lax.ppermute(h, 'lat', p) for h, p in zip(packed, lat_pairs)]  3.58 us
    ppermute x2, starting transfers between devices, per_device(): rims = [lax.ppermute(h, 'lat', p) for h, p in zip(packed, lat_pairs)]  3.24 us
    pallas_call x1, Pallas kernels, first(): pl.pallas_call(first_kernel, out_shape=[FIELD] * 4, in_specs=[VMEM], out_...  2.76 us
    pallas_call x1, Pallas kernels, inner(): pl.pallas_call(inner_kernel, out_shape=[FIELD] * 5 + [PICTURES], in_specs...  2.7 us
    pallas_call x1, Pallas kernels, brick(): pl.pallas_call(brick_kernel, out_shape=[pieces, pieces] + [FIELD] * 5 + [...  2.67 us
  transfers between devices with their start and end apart: 8, of which 6 were waited for; matrix products, arithmetic and copies ran while one was open for 0% of the time, Pallas kernels for 14%

profile of v5, /device:TPU:6, one launch (start us, length us, event | category | flops | bytes accessed | tf_op | source)
XLA Modules:
  0.0 48.9 jit_solution(15641403657063205735)
XLA Ops:
  0.6 0.0 copy-start
  0.6 0.0 copy-start.1
  0.7 1.4 %broadcast_select_fusion = (f32[2,3,64,128]{3,2,1,0:T(8,128)S(1)}, f32[2,3,64,128]{3,2,1,0:T(8,128)S(1)}) fusion(pred[]{:T(512)S(6)} %eq.3, f32[1,32,64,128]{3,2,1,0:T(8,128)} %bitcast.3, f32[1,32,64,128]{3,2,1,0:T(8,128)} %bitcast.5), kind=kLoop, calls=%fused_computation.7 | loop fusion | flops 294912 | bytes 2490369 | tf_op jit(solution)/shard_map/jit(_where)/select_n | solution.py:70
  2.1 0.4 collective-permute-start.1
  2.4 1.7 %collective-permute-start = (f32[2,3,64,128]{3,2,1,0:T(8,128)S(1)}, f32[2,3,64,128]{3,2,1,0:T(8,128)S(1)}, u32[]{:S(2)}, u32[]{:S(2)}) collective-permute-start(f32[2,3,64,128]{3,2,1,0:T(8,128)S(1)} %get-tuple-element.48), channel_id=1, source_target_pairs={{0,4},{4,0},{8,12},{12,8},{16,20},{20,16},{24,28},{28,24},{32,36},... | collective-permute-start | bytes 589832 | tf_op jit(solution)/shard_map/ppermute | solution.py:488
  4.1 0.0 copy-done
  4.1 0.0 copy-done.1
  4.1 0.2 pad_maximum_fusion.fields
  4.3 2.8 %shard_map.58 = (f32[2,38,80,128]{3,2,1,0:T(8,128)S(1)}, f32[2,38,80,128]{3,2,1,0:T(8,128)S(1)}, f32[2,38,80,128]{3,2,1,0:T(8,128)S(1)}, f32[2,38,80,128]{3,2,1,0:T(8,128)S(1)}) custom-call(f32[2,32,64,128]{3,2,1,0:T(8,128)S(1)} %pad_maximum_fusion.fields), custom_call_target="tpu_custom_call" | custom-call | tf_op jit(solution)/shard_map/pallas_call | solution.py:198
  7.1 0.1 collective-permute-done.1.depth_b.refs_5_
  7.2 0.0 collective-permute-done.depth_a.refs_4_
  7.2 0.1 shard_map.59
  7.3 3.1 %collective-permute-start.3 = (f32[380,128]{1,0:T(8,128)S(1)}, f32[380,128]{1,0:T(8,128)S(1)}, u32[]{:S(2)}, u32[]{:S(2)}) collective-permute-start(f32[380,128]{1,0:T(8,128)S(1)} %get-tuple-element.36), channel_id=1, source_target_pairs={{1,2},{2,1},{3,0},{0,3},{5,6},{6,5},{7,4},{4,7},{9,10},{10,9},{11,... | collective-permute-start | bytes 583688 | tf_op jit(solution)/shard_map/ppermute | solution.py:491
  10.4 0.1 collective-permute-start.2
  11.2 2.7 %shard_map.60 = (f32[2,38,80,128]{3,2,1,0:T(8,128)S(1)}, f32[2,38,80,128]{3,2,1,0:T(8,128)S(1)}, f32[2,38,80,128]{3,2,1,0:T(8,128)S(1)}, f32[2,38,80,128]{3,2,1,...) custom-call(f32[2,38,80,128]{3,2,1,0:T(8,128)S(1)} %get-tuple-elemen, ...), custom_call_target="tpu_custom_call", output_to_operand_aliasing={{0}: (0, {}), {1}: (1, {}), {2}: (2, {}), {3}: (3, {})} | custom-call | flops 40000000 | bytes 1048576 | tf_op jit(solution)/shard_map/pallas_call | solution.py:226
  13.9 1.4 %collective-permute-done.3.refs_7_ = f32[380,128]{1,0:T(8,128)S(1)} collective-permute-done((f32[380,128]{1,0:T(8,128)S(1)}, f32[380,128]{1,0:T(8,128)S(1)}, u32[]{:S(2)}, u32[]{:S(2)}) %collective-permute-start.3) | collective-permute-done | bytes 194592 | tf_op jit(solution)/shard_map/ppermute | solution.py:491
  15.3 2.1 %collective-permute-done.2.refs_6_ = f32[380,128]{1,0:T(8,128)S(1)} collective-permute-done((f32[380,128]{1,0:T(8,128)S(1)}, f32[380,128]{1,0:T(8,128)S(1)}, u32[]{:S(2)}, u32[]{:S(2)}) %collective-permute-start.2) | collective-permute-done | bytes 194592 | tf_op jit(solution)/shard_map/ppermute | solution.py:491
  17.5 2.7 %shard_map.61 = (f32[16,4,8,128]{3,2,1,0:T(8,128)S(1)}, f32[16,4,8,128]{3,2,1,0:T(8,128)S(1)}, f32[2,38,80,128]{3,2,1,0:T(8,128)S(1)}, f32[2,38,80,128]{3,2,1,0:...) custom-call(f32[2,38,80,128]{3,2,1,0:T(8,128)S(1)} %get-tuple-elemen, ...), custom_call_target="tpu_custom_call", output_to_operand_aliasing={{2}: (0, {}), {3}: (1, {}), {4}: (2, {}), {5}: (3, {}), {6}... | custom-call | tf_op jit(solution)/shard_map/pallas_call | solution.py:341
  20.2 0.8 %collective-permute-start.4 = (f32[16,4,8,128]{3,2,1,0:T(8,128)S(1)}, f32[16,4,8,128]{3,2,1,0:T(8,128)S(1)}, u32[]{:S(2)}, u32[]{:S(2)}) collective-permute-start(f32[16,4,8,128]{3,2,1,0:T(8,128)S(1)} %get-tuple-element.39), channel_id=1, source_target_pairs={{0,4},{4,0},{8,12},{12,8},{16,20},{20,16},{24,28},{28,24},{32,36},... | collective-permute-start | bytes 786440 | tf_op jit(solution)/shard_map/ppermute | solution.py:496
  21.0 1.2 %collective-permute-done.4.theirs = f32[16,4,8,128]{3,2,1,0:T(8,128)S(1)} collective-permute-done((f32[16,4,8,128]{3,2,1,0:T(8,128)S(1)}, f32[16,4,8,128]{3,2,1,0:T(8,128)S(1)}, u32[]{:S(2)}, u32[]{:S(2)}) %collective-permute-start.4) | collective-permute-done | bytes 262176 | tf_op jit(solution)/shard_map/ppermute | solution.py:496
  22.2 0.1 collective-permute-start.5
  22.3 7.8 %collective-permute-start.6 = (f32[4,4,8,128]{3,2,1,0:T(8,128)S(1)}, f32[4,4,8,128]{3,2,1,0:T(8,128)S(1)}, u32[]{:S(2)}, u32[]{:S(2)}) collective-permute-start(f32[4,4,8,128]{3,2,1,0:T(8,128)S(1)} %get-tuple-element.44), channel_id=1, source_target_pairs={{0,16},{4,20},{8,24},{12,28},{16,0},{20,4},{24,8},{28,12},{32,48},... | collective-permute-start | bytes 196616 | tf_op jit(solution)/shard_map/ppermute | solution.py:496
  30.1 0.0 collective-permute-start.7
  30.1 1.3 %shard_map.63 = (f32[32,64,128]{2,1,0:T(8,128)}, f32[32,64,128]{2,1,0:T(8,128)}, f32[8,128]{1,0:T(8,128)S(1)}) custom-call(f32[2,38,80,128]{3,2,1,0:T(8,128)S(1)} %get-tuple-element.37.field, f32[4,4,8,128]{3,2,1,0:T(8,128)S(1)} %get-tuple-element.40.part.refs_0_), custom_call_target="tpu_custom_call" | custom-call | tf_op jit(solution)/shard_map/pallas_call | solution.py:369
  31.5 0.0 collective-permute-done.5.refs_1_
  31.5 2.2 %collective-permute-done.6.refs_2_ = f32[4,4,8,128]{3,2,1,0:T(8,128)S(1)} collective-permute-done((f32[4,4,8,128]{3,2,1,0:T(8,128)S(1)}, f32[4,4,8,128]{3,2,1,0:T(8,128)S(1)}, u32[]{:S(2)}, u32[]{:S(2)}) %collective-permute-start.6) | collective-permute-done | bytes 65568 | tf_op jit(solution)/shard_map/ppermute | solution.py:496
  33.6 2.0 %collective-permute-done.7.refs_3_ = f32[4,4,8,128]{3,2,1,0:T(8,128)S(1)} collective-permute-done((f32[4,4,8,128]{3,2,1,0:T(8,128)S(1)}, f32[4,4,8,128]{3,2,1,0:T(8,128)S(1)}, u32[]{:S(2)}, u32[]{:S(2)}) %collective-permute-start.7) | collective-permute-done | bytes 65568 | tf_op jit(solution)/shard_map/ppermute | solution.py:496
  35.6 0.1 shard_map.64
  35.7 12.5 %all_to_all.5.slabs = f32[8,2,8,128]{3,2,1,0:T(8,128)S(1)} all-to-all(f32[8,2,8,128]{3,2,1,0:T(8,128)S(1)} %shard_map.64), channel_id=1, replica_groups={{0,32,64,96,128,160,192,224},{4,36,68,100,132,164,196,228},{8,40,72,104..., dimensions={0} | all-to-all | bytes 131072 | tf_op jit(solution)/shard_map/all_to_all | solution.py:502
  48.2 0.8 %shard_map.65 = f32[4,8,64]{2,1,0:T(8,128)} custom-call(f32[8,2,8,128]{3,2,1,0:T(8,128)S(1)} %all_to_all.5.slabs), custom_call_target="tpu_custom_call" | custom-call | tf_op jit(solution)/shard_map/pallas_call | solution.py:460
  (1 shorter events, 0.0 us)
Async XLA Ops:
  0.6 3.5 %copy-start = (f32[32,64,128]{2,1,0:T(8,128)S(1)}, f32[32,64,128]{2,1,0:T(8,128)}, u32[]{:S(2)}) copy-start(f32[32,64,128]{2,1,0:T(8,128)} %param.4) | copy-start | bytes 3145732
  0.6 3.5 %copy-start.1 = (f32[32,64,128]{2,1,0:T(8,128)S(1)}, f32[32,64,128]{2,1,0:T(8,128)}, u32[]{:S(2)}) copy-start(f32[32,64,128]{2,1,0:T(8,128)} %param.3) | copy-start | bytes 3145732
  2.1 5.2 %collective-permute-start.1 = (f32[2,3,64,128]{3,2,1,0:T(8,128)S(1)}, f32[2,3,64,128]{3,2,1,0:T(8,128)S(1)}, u32[]{:S(2)}, u32[]{:S(2)}) collective-permute-start(f32[2,3,64,128]{3,2,1,0:T(8,128)S(1)} %get-tuple-element.47), channel_id=1, source_target_pairs={{4,8},{8,4},{12,16},{16,12},{20,24},{24,20},{28,32},{32,28},{36,40... | collective-permute-start | bytes 589832 | tf_op jit(solution)/shard_map/ppermute | solution.py:488
  2.4 4.8 %collective-permute-start = (f32[2,3,64,128]{3,2,1,0:T(8,128)S(1)}, f32[2,3,64,128]{3,2,1,0:T(8,128)S(1)}, u32[]{:S(2)}, u32[]{:S(2)}) collective-permute-start(f32[2,3,64,128]{3,2,1,0:T(8,128)S(1)} %get-tuple-element.48), channel_id=1, source_target_pairs={{0,4},{4,0},{8,12},{12,8},{16,20},{20,16},{24,28},{28,24},{32,36},... | collective-permute-start | bytes 589832 | tf_op jit(solution)/shard_map/ppermute | solution.py:488
  7.3 8.0 %collective-permute-start.3 = (f32[380,128]{1,0:T(8,128)S(1)}, f32[380,128]{1,0:T(8,128)S(1)}, u32[]{:S(2)}, u32[]{:S(2)}) collective-permute-start(f32[380,128]{1,0:T(8,128)S(1)} %get-tuple-element.36), channel_id=1, source_target_pairs={{1,2},{2,1},{3,0},{0,3},{5,6},{6,5},{7,4},{4,7},{9,10},{10,9},{11,... | collective-permute-start | bytes 583688 | tf_op jit(solution)/shard_map/ppermute | solution.py:491
  10.4 7.1 %collective-permute-start.2 = (f32[380,128]{1,0:T(8,128)S(1)}, f32[380,128]{1,0:T(8,128)S(1)}, u32[]{:S(2)}, u32[]{:S(2)}) collective-permute-start(f32[380,128]{1,0:T(8,128)S(1)} %get-tuple-element.29.refs_6_), channel_id=1, source_target_pairs={{0,1},{1,0},{2,3},{3,2},{4,5},{5,4},{6,7},{7,6},{8,9},{9,8},{10,11... | collective-permute-start | bytes 583688 | tf_op jit(solution)/shard_map/ppermute | solution.py:491
  20.2 2.0 %collective-permute-start.4 = (f32[16,4,8,128]{3,2,1,0:T(8,128)S(1)}, f32[16,4,8,128]{3,2,1,0:T(8,128)S(1)}, u32[]{:S(2)}, u32[]{:S(2)}) collective-permute-start(f32[16,4,8,128]{3,2,1,0:T(8,128)S(1)} %get-tuple-element.39), channel_id=1, source_target_pairs={{0,4},{4,0},{8,12},{12,8},{16,20},{20,16},{24,28},{28,24},{32,36},... | collective-permute-start | bytes 786440 | tf_op jit(solution)/shard_map/ppermute | solution.py:496
  22.2 9.3 %collective-permute-start.5 = (f32[4,4,8,128]{3,2,1,0:T(8,128)S(1)}, f32[4,4,8,128]{3,2,1,0:T(8,128)S(1)}, u32[]{:S(2)}, u32[]{:S(2)}) collective-permute-start(f32[4,4,8,128]{3,2,1,0:T(8,128)S(1)} %get-tuple-element.43), channel_id=1, source_target_pairs={{0,8},{4,12},{8,0},{12,4},{16,24},{20,28},{24,16},{28,20},{32,40},... | collective-permute-start | bytes 196616 | tf_op jit(solution)/shard_map/ppermute | solution.py:496
  22.3 11.4 %collective-permute-start.6 = (f32[4,4,8,128]{3,2,1,0:T(8,128)S(1)}, f32[4,4,8,128]{3,2,1,0:T(8,128)S(1)}, u32[]{:S(2)}, u32[]{:S(2)}) collective-permute-start(f32[4,4,8,128]{3,2,1,0:T(8,128)S(1)} %get-tuple-element.44), channel_id=1, source_target_pairs={{0,16},{4,20},{8,24},{12,28},{16,0},{20,4},{24,8},{28,12},{32,48},... | collective-permute-start | bytes 196616 | tf_op jit(solution)/shard_map/ppermute | solution.py:496
  30.1 5.5 %collective-permute-start.7 = (f32[4,4,8,128]{3,2,1,0:T(8,128)S(1)}, f32[4,4,8,128]{3,2,1,0:T(8,128)S(1)}, u32[]{:S(2)}, u32[]{:S(2)}) collective-permute-start(f32[4,4,8,128]{3,2,1,0:T(8,128)S(1)} %get-tuple-element.45), channel_id=1, source_target_pairs={{0,24},{4,28},{8,16},{12,20},{16,8},{20,12},{24,0},{28,4},{32,56},... | collective-permute-start | bytes 196616 | tf_op jit(solution)/shard_map/ppermute | solution.py:496

commit v6 on v5

--- a/solution.py
+++ b/solution.py
@@ -182,7 +182,7 @@
     lax.fori_loop(first, last, layer, 0, unroll=unroll)
 
 
-def first_kernel(fields, ext, once, source, twice):
+def first_kernel(fields, ext, once, source, twice, thrice):
     for f in range(2):
 
         def layer(x, carry):
@@ -192,21 +192,22 @@
         lax.fori_loop(0, CX, layer, 0, unroll=8)
     sweep(0, ext, once, source, HALO + 1, HALO + CX - 1, INNER, 5)
     sweep(1, once, twice, source, HALO + 2, HALO + CX - 2, INNER, 14)
+    sweep(2, twice, thrice, source, HALO + 3, HALO + CX - 3, INNER, 13)
 
 
 def first(fields):
     return pl.pallas_call(
         first_kernel,
-        out_shape=[FIELD] * 4,
+        out_shape=[FIELD] * 5,
         in_specs=[VMEM],
-        out_specs=[VMEM] * 4,
+        out_specs=[VMEM] * 5,
         compiler_params=params(4),
     )(fields)
 
 
 def inner_kernel(*refs):
-    depth_a, depth_b, unused_lat, count = refs[4:8]
-    ext, once, source, twice, thrice, pic = refs[8:]
+    depth_a, depth_b, unused_lat, count = refs[5:9]
+    ext, once, source, twice, thrice, pic = refs[9:]
     layer_a = (1 - odd("depth")) * (HALO + CX)
     layer_b = odd("depth") * (HALO + CX)
     for f in range(2):
@@ -214,11 +215,11 @@
             ext[f, layer_a + k, pl.ds(ROW0, CY), :] = depth_a[f, k]
             ext[f, layer_b + k, pl.ds(ROW0, CY), :] = depth_b[f, k]
     zero_layers(ext, 0, EX)
-    for j, (inp, out) in enumerate(((ext, once), (once, twice))):
+    for j, (inp, out) in enumerate(((ext, once), (once, twice), (twice, thrice))):
         for start in (1 + j, HALO + CX - 1 - j):
             sweep(j, inp, out, source, start, start + 3, INNER, 3)
-        zero_layers(out, 1 + j, EX - 1 - j)
-    sweep(2, twice, thrice, source, HALO, HALO + CX, INNER, 16)
+        if j < 2:
+            zero_layers(out, 1 + j, EX - 1 - j)
     render(INNER_TILES, 4, thrice, count[0, 0], pic)
 
 
@@ -226,9 +227,9 @@
     return pl.pallas_call(
         inner_kernel,
         out_shape=[FIELD] * 5 + [PICTURES],
-        in_specs=[VMEM] * 7 + [SMEM],
+        in_specs=[VMEM] * 8 + [SMEM],
         out_specs=[VMEM] * 6,
-        input_output_aliases={i: i for i in range(4)},
+        input_output_aliases={i: i for i in range(5)},
         compiler_params=params(4),
         cost_estimate=pl.CostEstimate(
             flops=40_000_000, bytes_accessed=1 << 20, transcendentals=0
@@ -317,7 +318,7 @@
     zero_rows(twice, 2, EX - 2)
     sweep(2, twice, thrice, source, HALO, HALO + CX, STRIPS, 16)
     zero_rows(thrice, HALO, HALO + CX)
-    render(OUTER_TILES, 4, thrice, count[0, 0], pic)
+    render(OUTER_TILES, 8, thrice, count[0, 0], pic)
     for v in range(2):
         for c in range(4):
             square = jnp.concatenate([pic[v, c], pltpu.roll(pic[3 - v, c], 64, 1)], axis=0)
@@ -383,7 +384,8 @@
     write(3, clear * back[:, 3])
 
 
-def core_kernel(mine, theirs, *parts):
+def core_kernel(mine, theirs, token, *parts):
+    del token
     in_front = lax.rem(lax.axis_index("depth"), 2) == 0
 
     def write(c, value):
@@ -399,19 +401,19 @@
         blend(theirs, mine, write)
 
 
-def core_combine(mine, theirs):
+def core_combine(mine, theirs, token):
     part = jax.ShapeDtypeStruct((4,) + mine.shape[1:], jnp.float32)
     return pl.pallas_call(
         core_kernel,
         out_shape=[part] * 4,
-        in_specs=[VMEM] * 2,
+        in_specs=[VMEM] * 3,
         out_specs=[VMEM] * 4,
         compiler_params=params(4),
-    )(mine, theirs)
+    )(mine, theirs, token)
 
 
 def x_kernel(*refs):
-    parts, out = refs[:4], refs[5]
+    parts, out = refs[:4], refs[4]
     my_x = lax.rem(lax.div(lax.axis_index("depth"), 2), 4)
     low = lax.broadcasted_iota(jnp.int32, (8, NZ), 1) < CY
 
@@ -432,14 +434,14 @@
         pl.when(my_x == place)(functools.partial(ordered, place))
 
 
-def x_combine(parts, token):
+def x_combine(parts):
     return pl.pallas_call(
         x_kernel,
         out_shape=jax.ShapeDtypeStruct((8, 2, 8, NZ), jnp.float32),
-        in_specs=[VMEM] * 5,
+        in_specs=[VMEM] * 4,
         out_specs=VMEM,
         compiler_params=params(4),
-    )(*parts, token)
+    )(*parts)
 
 
 def z_kernel(slabs, out):
@@ -466,13 +468,9 @@
     )(slabs).transpose(0, 2, 1)
 
 
-RING_D = 1
-RING_L = 1
-
-
-def pairs(count, start, ring):
+def pairs(count, start):
     result = []
-    for i in range(start, count if ring else count - 1, 2):
+    for i in range(start, count, 2):
         after = (i + 1) % count
         result += [(i, after), (after, i)]
     return result
@@ -481,8 +479,8 @@
 def per_device(phase, temper, iface_count):
     depth_size = lax.axis_size("depth")
     lat_size = lax.axis_size("lat")
-    depth_pairs = [pairs(depth_size, start, RING_D) for start in range(2)]
-    lat_pairs = [pairs(lat_size, start, RING_L) for start in range(2)]
+    depth_pairs = [pairs(depth_size, start) for start in range(2)]
+    lat_pairs = [pairs(lat_size, start) for start in range(2)]
     fields = jnp.stack([phase, temper])
     halos = depth_pack(fields)
     halos = [lax.ppermute(h, "depth", p) for h, p in zip(halos, depth_pairs)]
@@ -495,12 +493,13 @@
     def partner(value, distance):
         return lax.ppermute(value, "depth", [(i, i ^ distance) for i in range(depth_size)])
 
-    parts = core_combine(mine, partner(outgoing, 1))
-    phase_next, heat_next, token = emit(solved, parts[0])
+    theirs = partner(outgoing, 1)
+    phase_next, heat_next, token = emit(solved, mine)
+    parts = core_combine(mine, theirs, token)
     parts = [parts[0]] + [partner(parts[k], 2 * k) for k in (1, 2, 3)]
     groups = [[z * 8 + i for z in range(depth_size // 8)] for i in range(8)]
     slabs = lax.all_to_all(
-        x_combine(parts, token), "depth", 0, 0, tiled=True, axis_index_groups=groups
+        x_combine(parts), "depth", 0, 0, tiled=True, axis_index_groups=groups
     )
     return phase_next, heat_next, z_combine(slabs)
 

time: 49.2 us -> 49.3 us (level)
  the two profiles are of different devices: /device:TPU:6 before, /device:TPU:8 now
where the time goes in v6:
time: 49.3 us; the launch traced here: 49.1 us
  starting transfers between devices  16 us (32%)
  blocking collectives  14.4 us (29%)
  Pallas kernels  9.69 us (20%)
  waiting for transfers between devices  6.13 us (12%)
  other arithmetic  1.54 us (3%)
  between operations  1.42 us (3%)
    all_to_all x1, blocking collectives, per_device(): lax.all_to_all(x_combine(parts), 'depth', 0, 0, tiled=True, axis_index_gr...  14.4 us
    ppermute x2, starting transfers between devices, per_device(): halos = [lax.ppermute(h, 'depth', p) for h, p in zip(halos, depth_pairs)]  7.58 us
    ppermute x4, starting transfers between devices, partner(): lax.ppermute(value, 'depth', [(i, i ^ distance) for i in range(depth_size)])  4.86 us
    pallas_call x1, Pallas kernels, first(): pl.pallas_call(first_kernel, out_shape=[FIELD] * 5, in_specs=[VMEM], out_...  3.79 us
    ppermute x2, starting transfers between devices, per_device(): rims = [lax.ppermute(h, 'lat', p) for h, p in zip(packed, lat_pairs)]  3.55 us
    ppermute x2, waiting for transfers between devices, per_device(): rims = [lax.ppermute(h, 'lat', p) for h, p in zip(packed, lat_pairs)]  3.29 us
    ppermute x4, waiting for transfers between devices, partner(): lax.ppermute(value, 'depth', [(i, i ^ distance) for i in range(depth_size)])  2.83 us
    pallas_call x1, Pallas kernels, brick(): pl.pallas_call(brick_kernel, out_shape=[pieces, pieces] + [FIELD] * 5 + [...  2.28 us
  transfers between devices with their start and end apart: 8, of which 6 were waited for; matrix products, arithmetic and copies ran while one was open for 0% of the time, Pallas kernels for 13%

profile of v6, /device:TPU:8, one launch (start us, length us, event | category | flops | bytes accessed | tf_op | source)
XLA Modules:
  0.0 49.1 jit_solution(17744503544193426411)
XLA Ops:
  0.6 0.0 copy-start
  0.6 0.0 copy-start.1
  0.7 1.4 %broadcast_select_fusion = (f32[2,3,64,128]{3,2,1,0:T(8,128)S(1)}, f32[2,3,64,128]{3,2,1,0:T(8,128)S(1)}) fusion(pred[]{:T(512)S(6)} %eq.3, f32[1,32,64,128]{3,2,1,0:T(8,128)} %bitcast.3, f32[1,32,64,128]{3,2,1,0:T(8,128)} %bitcast.5), kind=kLoop, calls=%fused_computation.7 | loop fusion | flops 294912 | bytes 2490369 | tf_op jit(solution)/shard_map/jit(_where)/select_n | solution.py:70
  2.1 7.6 %collective-permute-start.1 = (f32[2,3,64,128]{3,2,1,0:T(8,128)S(1)}, f32[2,3,64,128]{3,2,1,0:T(8,128)S(1)}, u32[]{:S(2)}, u32[]{:S(2)}) collective-permute-start(f32[2,3,64,128]{3,2,1,0:T(8,128)S(1)} %get-tuple-element.49), channel_id=1, source_target_pairs={{4,8},{8,4},{12,16},{16,12},{20,24},{24,20},{28,32},{32,28},{36,40... | collective-permute-start | bytes 589832 | tf_op jit(solution)/shard_map/ppermute | solution.py:486
  9.6 0.0 collective-permute-start
  9.6 0.0 copy-done
  9.6 0.0 copy-done.1
  9.6 0.1 pad_maximum_fusion.fields
  9.8 3.8 %shard_map.58 = (f32[2,38,80,128]{3,2,1,0:T(8,128)S(1)}, f32[2,38,80,128]{3,2,1,0:T(8,128)S(1)}, f32[2,38,80,128]{3,2,1,0:T(8,128)S(1)}, f32[2,38,80,128]{3,2,1,0:T(8,128)S(1)}, f32[2,38,80,128]{3,2,1,0:T(8,128)S(1)}) custom-call(f32[2,32,64,128]{3,2,1,0:T(8,128)S(1)} %pad_maximum_fusion.fields), custom_call_target="tpu_custom_call" | custom-call | tf_op jit(solution)/shard_map/pallas_call | solution.py:199
  13.6 0.0 collective-permute-done.1.depth_b.refs_6_
  13.6 0.0 collective-permute-done.depth_a.refs_5_
  13.6 0.1 shard_map.59
  13.7 1.7 %collective-permute-start.3 = (f32[380,128]{1,0:T(8,128)S(1)}, f32[380,128]{1,0:T(8,128)S(1)}, u32[]{:S(2)}, u32[]{:S(2)}) collective-permute-start(f32[380,128]{1,0:T(8,128)S(1)} %get-tuple-element.38), channel_id=1, source_target_pairs={{1,2},{2,1},{3,0},{0,3},{5,6},{6,5},{7,4},{4,7},{9,10},{10,9},{11,... | collective-permute-start | bytes 583688 | tf_op jit(solution)/shard_map/ppermute | solution.py:489
  15.3 1.9 %collective-permute-start.2 = (f32[380,128]{1,0:T(8,128)S(1)}, f32[380,128]{1,0:T(8,128)S(1)}, u32[]{:S(2)}, u32[]{:S(2)}) collective-permute-start(f32[380,128]{1,0:T(8,128)S(1)} %get-tuple-element.31.refs_7_), channel_id=1, source_target_pairs={{0,1},{1,0},{2,3},{3,2},{4,5},{5,4},{6,7},{7,6},{8,9},{9,8},{10,11... | collective-permute-start | bytes 583688 | tf_op jit(solution)/shard_map/ppermute | solution.py:489
  17.9 1.3 %shard_map.60 = (f32[2,38,80,128]{3,2,1,0:T(8,128)S(1)}, f32[2,38,80,128]{3,2,1,0:T(8,128)S(1)}, f32[2,38,80,128]{3,2,1,0:T(8,128)S(1)}, f32[2,38,80,128]{3,2,1,...) custom-call(f32[2,38,80,128]{3,2,1,0:T(8,128)S(1)} %get-tuple-elemen, ...), custom_call_target="tpu_custom_call", output_to_operand_aliasing={{0}: (0, {}), {1}: (1, {}), {2}: (2, {}), {3}: (3, {}), {4}... | custom-call | flops 40000000 | bytes 1048576 | tf_op jit(solution)/shard_map/pallas_call | solution.py:227
  19.2 1.9 %collective-permute-done.3.refs_7_ = f32[380,128]{1,0:T(8,128)S(1)} collective-permute-done((f32[380,128]{1,0:T(8,128)S(1)}, f32[380,128]{1,0:T(8,128)S(1)}, u32[]{:S(2)}, u32[]{:S(2)}) %collective-permute-start.3) | collective-permute-done | bytes 194592 | tf_op jit(solution)/shard_map/ppermute | solution.py:489
  21.1 1.4 %collective-permute-done.2.refs_6_ = f32[380,128]{1,0:T(8,128)S(1)} collective-permute-done((f32[380,128]{1,0:T(8,128)S(1)}, f32[380,128]{1,0:T(8,128)S(1)}, u32[]{:S(2)}, u32[]{:S(2)}) %collective-permute-start.2) | collective-permute-done | bytes 194592 | tf_op jit(solution)/shard_map/ppermute | solution.py:489
  22.5 2.3 %shard_map.61 = (f32[16,4,8,128]{3,2,1,0:T(8,128)S(1)}, f32[16,4,8,128]{3,2,1,0:T(8,128)S(1)}, f32[2,38,80,128]{3,2,1,0:T(8,128)S(1)}, f32[2,38,80,128]{3,2,1,0:...) custom-call(f32[2,38,80,128]{3,2,1,0:T(8,128)S(1)} %get-tuple-elemen, ...), custom_call_target="tpu_custom_call", output_to_operand_aliasing={{2}: (0, {}), {3}: (1, {}), {4}: (2, {}), {5}: (3, {}), {6}... | custom-call | tf_op jit(solution)/shard_map/pallas_call | solution.py:342
  24.8 0.1 collective-permute-start.4
  24.9 1.3 %shard_map.62 = (f32[32,64,128]{2,1,0:T(8,128)}, f32[32,64,128]{2,1,0:T(8,128)}, f32[8,128]{1,0:T(8,128)S(1)}) custom-call(f32[2,38,80,128]{3,2,1,0:T(8,128)S(1)} %get-tuple-element.39.field, f32[16,4,8,128]{3,2,1,0:T(8,128)S(1)} %get-tuple-element.40.part.mine), custom_call_target="tpu_custom_call" | custom-call | tf_op jit(solution)/shard_map/pallas_call | solution.py:370
  26.2 0.2 collective-permute-done.4.theirs
  26.5 0.1 collective-permute-start.5
  26.6 0.1 collective-permute-start.6
  26.7 4.6 %collective-permute-start.7 = (f32[4,4,8,128]{3,2,1,0:T(8,128)S(1)}, f32[4,4,8,128]{3,2,1,0:T(8,128)S(1)}, u32[]{:S(2)}, u32[]{:S(2)}) collective-permute-start(f32[4,4,8,128]{3,2,1,0:T(8,128)S(1)} %get-tuple-element.48), channel_id=1, source_target_pairs={{0,24},{4,28},{8,16},{12,20},{16,8},{20,12},{24,0},{28,4},{32,56},... | collective-permute-start | bytes 196616 | tf_op jit(solution)/shard_map/ppermute | solution.py:494
  31.3 0.3 collective-permute-done.5.refs_1_
  31.5 1.0 %collective-permute-done.6.refs_2_ = f32[4,4,8,128]{3,2,1,0:T(8,128)S(1)} collective-permute-done((f32[4,4,8,128]{3,2,1,0:T(8,128)S(1)}, f32[4,4,8,128]{3,2,1,0:T(8,128)S(1)}, u32[]{:S(2)}, u32[]{:S(2)}) %collective-permute-start.6) | collective-permute-done | bytes 65568 | tf_op jit(solution)/shard_map/ppermute | solution.py:494
  32.6 1.3 %collective-permute-done.7.refs_3_ = f32[4,4,8,128]{3,2,1,0:T(8,128)S(1)} collective-permute-done((f32[4,4,8,128]{3,2,1,0:T(8,128)S(1)}, f32[4,4,8,128]{3,2,1,0:T(8,128)S(1)}, u32[]{:S(2)}, u32[]{:S(2)}) %collective-permute-start.7) | collective-permute-done | bytes 65568 | tf_op jit(solution)/shard_map/ppermute | solution.py:494
  33.9 0.1 shard_map.64
  34.0 14.4 %all_to_all.5.slabs = f32[8,2,8,128]{3,2,1,0:T(8,128)S(1)} all-to-all(f32[8,2,8,128]{3,2,1,0:T(8,128)S(1)} %shard_map.64), channel_id=1, replica_groups={{0,32,64,96,128,160,192,224},{4,36,68,100,132,164,196,228},{8,40,72,104..., dimensions={0} | all-to-all | bytes 131072 | tf_op jit(solution)/shard_map/all_to_all | solution.py:501
  48.4 0.8 %shard_map.65 = f32[4,8,64]{2,1,0:T(8,128)} custom-call(f32[8,2,8,128]{3,2,1,0:T(8,128)S(1)} %all_to_all.5.slabs), custom_call_target="tpu_custom_call" | custom-call | tf_op jit(solution)/shard_map/pallas_call | solution.py:462
  (1 shorter events, 0.0 us)
Async XLA Ops:
  0.6 9.0 %copy-start = (f32[32,64,128]{2,1,0:T(8,128)S(1)}, f32[32,64,128]{2,1,0:T(8,128)}, u32[]{:S(2)}) copy-start(f32[32,64,128]{2,1,0:T(8,128)} %param.4) | copy-start | bytes 3145732
  0.6 9.0 %copy-start.1 = (f32[32,64,128]{2,1,0:T(8,128)S(1)}, f32[32,64,128]{2,1,0:T(8,128)}, u32[]{:S(2)}) copy-start(f32[32,64,128]{2,1,0:T(8,128)} %param.3) | copy-start | bytes 3145732
  2.1 11.5 %collective-permute-start.1 = (f32[2,3,64,128]{3,2,1,0:T(8,128)S(1)}, f32[2,3,64,128]{3,2,1,0:T(8,128)S(1)}, u32[]{:S(2)}, u32[]{:S(2)}) collective-permute-start(f32[2,3,64,128]{3,2,1,0:T(8,128)S(1)} %get-tuple-element.49), channel_id=1, source_target_pairs={{4,8},{8,4},{12,16},{16,12},{20,24},{24,20},{28,32},{32,28},{36,40... | collective-permute-start | bytes 589832 | tf_op jit(solution)/shard_map/ppermute | solution.py:486
  9.6 4.0 %collective-permute-start = (f32[2,3,64,128]{3,2,1,0:T(8,128)S(1)}, f32[2,3,64,128]{3,2,1,0:T(8,128)S(1)}, u32[]{:S(2)}, u32[]{:S(2)}) collective-permute-start(f32[2,3,64,128]{3,2,1,0:T(8,128)S(1)} %get-tuple-element.50), channel_id=1, source_target_pairs={{0,4},{4,0},{8,12},{12,8},{16,20},{20,16},{24,28},{28,24},{32,36},... | collective-permute-start | bytes 589832 | tf_op jit(solution)/shard_map/ppermute | solution.py:486
  13.7 7.4 %collective-permute-start.3 = (f32[380,128]{1,0:T(8,128)S(1)}, f32[380,128]{1,0:T(8,128)S(1)}, u32[]{:S(2)}, u32[]{:S(2)}) collective-permute-start(f32[380,128]{1,0:T(8,128)S(1)} %get-tuple-element.38), channel_id=1, source_target_pairs={{1,2},{2,1},{3,0},{0,3},{5,6},{6,5},{7,4},{4,7},{9,10},{10,9},{11,... | collective-permute-start | bytes 583688 | tf_op jit(solution)/shard_map/ppermute | solution.py:489
  15.3 7.2 %collective-permute-start.2 = (f32[380,128]{1,0:T(8,128)S(1)}, f32[380,128]{1,0:T(8,128)S(1)}, u32[]{:S(2)}, u32[]{:S(2)}) collective-permute-start(f32[380,128]{1,0:T(8,128)S(1)} %get-tuple-element.31.refs_7_), channel_id=1, source_target_pairs={{0,1},{1,0},{2,3},{3,2},{4,5},{5,4},{6,7},{7,6},{8,9},{9,8},{10,11... | collective-permute-start | bytes 583688 | tf_op jit(solution)/shard_map/ppermute | solution.py:489
  24.8 1.6 %collective-permute-start.4 = (f32[16,4,8,128]{3,2,1,0:T(8,128)S(1)}, f32[16,4,8,128]{3,2,1,0:T(8,128)S(1)}, u32[]{:S(2)}, u32[]{:S(2)}) collective-permute-start(f32[16,4,8,128]{3,2,1,0:T(8,128)S(1)} %get-tuple-element.43), channel_id=1, source_target_pairs={{0,4},{4,0},{8,12},{12,8},{16,20},{20,16},{24,28},{28,24},{32,36},... | collective-permute-start | bytes 786440 | tf_op jit(solution)/shard_map/ppermute | solution.py:494
  26.5 5.1 %collective-permute-start.5 = (f32[4,4,8,128]{3,2,1,0:T(8,128)S(1)}, f32[4,4,8,128]{3,2,1,0:T(8,128)S(1)}, u32[]{:S(2)}, u32[]{:S(2)}) collective-permute-start(f32[4,4,8,128]{3,2,1,0:T(8,128)S(1)} %get-tuple-element.46), channel_id=1, source_target_pairs={{0,8},{4,12},{8,0},{12,4},{16,24},{20,28},{24,16},{28,20},{32,40},... | collective-permute-start | bytes 196616 | tf_op jit(solution)/shard_map/ppermute | solution.py:494
  26.6 6.0 %collective-permute-start.6 = (f32[4,4,8,128]{3,2,1,0:T(8,128)S(1)}, f32[4,4,8,128]{3,2,1,0:T(8,128)S(1)}, u32[]{:S(2)}, u32[]{:S(2)}) collective-permute-start(f32[4,4,8,128]{3,2,1,0:T(8,128)S(1)} %get-tuple-element.47), channel_id=1, source_target_pairs={{0,16},{4,20},{8,24},{12,28},{16,0},{20,4},{24,8},{28,12},{32,48},... | collective-permute-start | bytes 196616 | tf_op jit(solution)/shard_map/ppermute | solution.py:494
  26.7 7.2 %collective-permute-start.7 = (f32[4,4,8,128]{3,2,1,0:T(8,128)S(1)}, f32[4,4,8,128]{3,2,1,0:T(8,128)S(1)}, u32[]{:S(2)}, u32[]{:S(2)}) collective-permute-start(f32[4,4,8,128]{3,2,1,0:T(8,128)S(1)} %get-tuple-element.48), channel_id=1, source_target_pairs={{0,24},{4,28},{8,16},{12,20},{16,8},{20,12},{24,0},{28,4},{32,56},... | collective-permute-start | bytes 196616 | tf_op jit(solution)/shard_map/ppermute | solution.py:494

commit v7 on v6

--- a/solution.py
+++ b/solution.py
@@ -70,41 +70,67 @@
     return jnp.where(is_odd, low, high), jnp.where(is_odd, high, low)
 
 
-def lat_pack_kernel(ext, depth_a, depth_b, lat_a, lat_b):
-    layer_a = (1 - odd("depth")) * (HALO + CX)
-    layer_b = odd("depth") * (HALO + CX)
+def lat_pack_kernel(fields, lat_a, lat_b):
     row_a = (1 - odd("lat")) * (CY - RIM)
     row_b = odd("lat") * (CY - RIM)
     for f in range(2):
-        for row, target in ((row_a, lat_a), (row_b, lat_b)):
-            for x in range(CX):
-                at = pl.ds((f * EX + HALO + x) * RIM, RIM)
-                target[at, :] = ext[f, HALO + x, pl.ds(ROW0 + row, RIM), :]
-            for k in range(HALO):
-                for layer, halo in ((layer_a, depth_a), (layer_b, depth_b)):
-                    at = pl.ds((f * EX + layer + k) * RIM, RIM)
-                    target[at, :] = halo[f, k, pl.ds(row, RIM), :]
-
-
-def lat_pack(ext, depth_a, depth_b):
-    rows = jax.ShapeDtypeStruct((2 * EX * RIM, NZ), jnp.float32)
+        for x in range(CX):
+            at = pl.ds((f * CX + x) * RIM, RIM)
+            lat_a[at, :] = fields[f, x, pl.ds(row_a, RIM), :]
+            lat_b[at, :] = fields[f, x, pl.ds(row_b, RIM), :]
+
+
+def lat_pack(fields):
+    rows = jax.ShapeDtypeStruct((2 * CX * RIM, NZ), jnp.float32)
     return pl.pallas_call(
         lat_pack_kernel,
+        out_shape=[rows, rows],
+        in_specs=[VMEM],
+        out_specs=[VMEM] * 2,
+        compiler_params=params(4),
+    )(fields)
+
+
+def corner_at(f, side, k):
+    return pl.ds(((f * 2 + side) * HALO + k) * RIM, RIM)
+
+
+def corner_pack_kernel(depth_a, depth_b, swept, corner_a, corner_b):
+    del swept
+    side_a = 1 - odd("depth")
+    side_b = odd("depth")
+    row_a = (1 - odd("lat")) * (CY - RIM)
+    row_b = odd("lat") * (CY - RIM)
+    for f in range(2):
+        for k in range(HALO):
+            for side, halo in ((side_a, depth_a), (side_b, depth_b)):
+                corner_a[corner_at(f, side, k), :] = halo[f, k, pl.ds(row_a, RIM), :]
+                corner_b[corner_at(f, side, k), :] = halo[f, k, pl.ds(row_b, RIM), :]
+
+
+def corner_pack(depth_a, depth_b, swept):
+    rows = jax.ShapeDtypeStruct((2 * 2 * HALO * RIM, NZ), jnp.float32)
+    return pl.pallas_call(
+        corner_pack_kernel,
         out_shape=[rows, rows],
         in_specs=[VMEM] * 3,
         out_specs=[VMEM] * 2,
         compiler_params=params(4),
-    )(ext, depth_a, depth_b)
-
-
-def lat_unpack(ext, lat_a, lat_b):
+    )(depth_a, depth_b, swept)
+
+
+def lat_unpack(ext, lat_a, lat_b, corner_a, corner_b):
     row_a = ROW0 - RIM + (1 - odd("lat")) * (RIM + CY)
     row_b = ROW0 - RIM + odd("lat") * (RIM + CY)
     for f in range(2):
-        for x in range(EX):
-            at = pl.ds((f * EX + x) * RIM, RIM)
-            ext[f, x, pl.ds(row_a, RIM), :] = lat_a[at, :]
-            ext[f, x, pl.ds(row_b, RIM), :] = lat_b[at, :]
+        for row, lat, corner in ((row_a, lat_a, corner_a), (row_b, lat_b, corner_b)):
+            for x in range(CX):
+                at = pl.ds((f * CX + x) * RIM, RIM)
+                ext[f, HALO + x, pl.ds(row, RIM), :] = lat[at, :]
+            for side in range(2):
+                for k in range(HALO):
+                    layer = side * (HALO + CX) + k
+                    ext[f, layer, pl.ds(row, RIM), :] = corner[corner_at(f, side, k), :]
 
 
 def zero_layers(ref, first, last):
@@ -182,7 +208,8 @@
     lax.fori_loop(first, last, layer, 0, unroll=unroll)
 
 
-def first_kernel(fields, ext, once, source, twice, thrice):
+def first_kernel(fields, packed, ext, once, source, twice, thrice):
+    del packed
     for f in range(2):
 
         def layer(x, carry):
@@ -195,18 +222,18 @@
     sweep(2, twice, thrice, source, HALO + 3, HALO + CX - 3, INNER, 13)
 
 
-def first(fields):
+def first(fields, packed):
     return pl.pallas_call(
         first_kernel,
         out_shape=[FIELD] * 5,
-        in_specs=[VMEM],
+        in_specs=[VMEM] * 2,
         out_specs=[VMEM] * 5,
         compiler_params=params(4),
-    )(fields)
+    )(fields, packed)
 
 
 def inner_kernel(*refs):
-    depth_a, depth_b, unused_lat, count = refs[5:9]
+    depth_a, depth_b, unused_corner, count = refs[5:9]
     ext, once, source, twice, thrice, pic = refs[9:]
     layer_a = (1 - odd("depth")) * (HALO + CX)
     layer_b = odd("depth") * (HALO + CX)
@@ -223,7 +250,7 @@
     render(INNER_TILES, 4, thrice, count[0, 0], pic)
 
 
-def inner(fields, halos, lat_a, iface_count):
+def inner(fields, halos, corner_a, iface_count):
     return pl.pallas_call(
         inner_kernel,
         out_shape=[FIELD] * 5 + [PICTURES],
@@ -234,7 +261,7 @@
         cost_estimate=pl.CostEstimate(
             flops=40_000_000, bytes_accessed=1 << 20, transcendentals=0
         ),
-    )(*fields, *halos, lat_a, iface_count)
+    )(*fields, *halos, corner_a, iface_count)
 
 
 CENTRE = 0.8
@@ -305,9 +332,9 @@
 
 
 def brick_kernel(*refs):
-    lat_a, lat_b, count = refs[6:9]
-    keep, send, ext, once, source, twice, thrice, pic, turned = refs[9:]
-    lat_unpack(ext, lat_a, lat_b)
+    count = refs[10]
+    keep, send, ext, once, source, twice, thrice, pic, turned = refs[11:]
+    lat_unpack(ext, *refs[6:10])
     zero_layers(ext, 0, EX)
     zero_rows(ext, 0, EX)
     sweep(0, ext, once, source, 1, EX - 1, STRIPS, 12)
@@ -337,17 +364,17 @@
                     target[x_rel * 4 + z, c] = turned[z >> 1, c, at, :]
 
 
-def brick(fields, lat_a, lat_b, iface_count):
+def brick(fields, rims, iface_count):
     pieces = jax.ShapeDtypeStruct((16, 4, 8, NZ), jnp.float32)
     results = pl.pallas_call(
         brick_kernel,
         out_shape=[pieces, pieces] + [FIELD] * 5 + [PICTURES],
-        in_specs=[VMEM] * 8 + [SMEM],
+        in_specs=[VMEM] * 10 + [SMEM],
         out_specs=[VMEM] * 8,
         input_output_aliases={i: 2 + i for i in range(6)},
         scratch_shapes=[pltpu.VMEM((2, 4, NZ, 2 * CY), jnp.float32)],
         compiler_params=params(4),
-    )(*fields, lat_a, lat_b, iface_count)
+    )(*fields, *rims, iface_count)
     return results[0], results[1], results[6]
 
 
@@ -484,11 +511,13 @@
     fields = jnp.stack([phase, temper])
     halos = depth_pack(fields)
     halos = [lax.ppermute(h, "depth", p) for h, p in zip(halos, depth_pairs)]
-    fields = first(fields)
-    packed = lat_pack(fields[0], *halos)
+    packed = lat_pack(fields)
     rims = [lax.ppermute(h, "lat", p) for h, p in zip(packed, lat_pairs)]
+    fields = first(fields, packed[0])
+    packed = corner_pack(*halos, fields[1])
+    corners = [lax.ppermute(h, "lat", p) for h, p in zip(packed, lat_pairs)]
     fields = inner(fields, halos, packed[0], iface_count)
-    mine, outgoing, solved = brick(fields, *rims, iface_count)
+    mine, outgoing, solved = brick(fields, (*rims, *corners), iface_count)
 
     def partner(value, distance):
         return lax.ppermute(value, "depth", [(i, i ^ distance) for i in range(depth_size)])

time: 49.3 us -> 49.1 us (level)
  waiting for transfers between devices: 6.13 us -> 2.84 us
  starting transfers between devices: 16 us -> 17.3 us
  Pallas kernels: 9.69 us -> 10.9 us
  blocking collectives: 14.4 us -> 14.9 us
    ppermute x2, waiting for transfers between devices: 3.29 us -> 0.01 us  [per_device(): rims = [lax.ppermute(h, 'lat', p) for h, p in zip(packed, lat_pairs)]]
    ppermute x0 -> x2, starting transfers between devices: none -> 1.27 us  [per_device(): corners = [lax.ppermute(h, 'lat', p) for h, p in zip(packed, lat_pairs)]]
    pallas_call x1, Pallas kernels: 1.33 us -> 2.18 us  [inner(): pl.pallas_call(inner_kernel, out_shape=[FIELD] * 5 + [PICTURES], in_specs...]
    all_to_all x1, blocking collectives: 14.4 us -> 14.9 us  [per_device(): lax.all_to_all(x_combine(parts), 'depth', 0, 0, tiled=True, axis_index_gr...]
    pallas_call x2 -> x3, Pallas kernels: 3.86 us -> 3.89 us  [the longest x1 3.78 us: first(): pl.pallas_call(first_kernel, out_shape=[FIELD] * 5, in_specs=[VMEM] * 2,...]
  transfers between devices with their start and end apart: 8 -> 10, of which waited for: 6 -> 4; matrix products, arithmetic and copies ran while one was open for 0% -> 0% of each run, Pallas kernels for 13% -> 15%
where the time goes in v7:
time: 49.1 us
  starting transfers between devices  17.3 us (35%)
  blocking collectives  14.9 us (30%)
  Pallas kernels  10.9 us (22%)
  waiting for transfers between devices  2.84 us (6%)
  other arithmetic  1.64 us (3%)
  between operations  1.47 us (3%)
    all_to_all x1, blocking collectives, per_device(): lax.all_to_all(x_combine(parts), 'depth', 0, 0, tiled=True, axis_index_gr...  14.9 us
    ppermute x2, starting transfers between devices, per_device(): halos = [lax.ppermute(h, 'depth', p) for h, p in zip(halos, depth_pairs)]  7.58 us
    ppermute x4, starting transfers between devices, partner(): lax.ppermute(value, 'depth', [(i, i ^ distance) for i in range(depth_size)])  4.86 us
    pallas_call x1, Pallas kernels, first(): pl.pallas_call(first_kernel, out_shape=[FIELD] * 5, in_specs=[VMEM] * 2,...  3.78 us
    ppermute x2, starting transfers between devices, per_device(): rims = [lax.ppermute(h, 'lat', p) for h, p in zip(packed, lat_pairs)]  3.55 us
    ppermute x4, waiting for transfers between devices, partner(): lax.ppermute(value, 'depth', [(i, i ^ distance) for i in range(depth_size)])  2.83 us
    pallas_call x1, Pallas kernels, brick(): pl.pallas_call(brick_kernel, out_shape=[pieces, pieces] + [FIELD] * 5 + [...  2.64 us
    pallas_call x1, Pallas kernels, inner(): pl.pallas_call(inner_kernel, out_shape=[FIELD] * 5 + [PICTURES], in_specs...  2.18 us
  transfers between devices with their start and end apart: 10, of which 4 were waited for; matrix products, arithmetic and copies ran while one was open for 0% of the time, Pallas kernels for 15%

profile of v7, /device:TPU:8, one launch (start us, length us, event | category | flops | bytes accessed | tf_op | source)
XLA Modules:
  0.0 49.1 jit_solution(8276922407586771086)
XLA Ops:
  0.6 0.0 copy-start
  0.6 0.0 copy-start.1
  0.7 1.4 %broadcast_select_fusion = (f32[2,3,64,128]{3,2,1,0:T(8,128)S(1)}, f32[2,3,64,128]{3,2,1,0:T(8,128)S(1)}) fusion(pred[]{:T(512)S(6)} %eq.3, f32[1,32,64,128]{3,2,1,0:T(8,128)} %bitcast.3, f32[1,32,64,128]{3,2,1,0:T(8,128)} %bitcast.5), kind=kLoop, calls=%fused_computation.7 | loop fusion | flops 294912 | bytes 2490369 | tf_op jit(solution)/shard_map/jit(_where)/select_n | solution.py:70
  2.1 7.6 %collective-permute-start.1 = (f32[2,3,64,128]{3,2,1,0:T(8,128)S(1)}, f32[2,3,64,128]{3,2,1,0:T(8,128)S(1)}, u32[]{:S(2)}, u32[]{:S(2)}) collective-permute-start(f32[2,3,64,128]{3,2,1,0:T(8,128)S(1)} %get-tuple-element.53), channel_id=1, source_target_pairs={{4,8},{8,4},{12,16},{16,12},{20,24},{24,20},{28,32},{32,28},{36,40... | collective-permute-start | bytes 589832 | tf_op jit(solution)/shard_map/ppermute | solution.py:513
  9.6 0.0 collective-permute-start
  9.6 0.0 copy-done
  9.6 0.0 copy-done.1
  9.6 0.2 pad_maximum_fusion.fields
  9.9 0.1 shard_map.58
  10.0 1.7 %collective-permute-start.3 = (f32[320,128]{1,0:T(8,128)S(1)}, f32[320,128]{1,0:T(8,128)S(1)}, u32[]{:S(2)}, u32[]{:S(2)}) collective-permute-start(f32[320,128]{1,0:T(8,128)S(1)} %get-tuple-element.41), channel_id=1, source_target_pairs={{1,2},{2,1},{3,0},{0,3},{5,6},{6,5},{7,4},{4,7},{9,10},{10,9},{11,... | collective-permute-start | bytes 491528 | tf_op jit(solution)/shard_map/ppermute | solution.py:515
  11.6 1.9 %collective-permute-start.2 = (f32[320,128]{1,0:T(8,128)S(1)}, f32[320,128]{1,0:T(8,128)S(1)}, u32[]{:S(2)}, u32[]{:S(2)}) collective-permute-start(f32[320,128]{1,0:T(8,128)S(1)} %get-tuple-element.28.packed), channel_id=1, source_target_pairs={{0,1},{1,0},{2,3},{3,2},{4,5},{5,4},{6,7},{7,6},{8,9},{9,8},{10,11... | collective-permute-start | bytes 491528 | tf_op jit(solution)/shard_map/ppermute | solution.py:515
  13.5 3.8 %shard_map.59 = (f32[2,38,80,128]{3,2,1,0:T(8,128)S(1)}, f32[2,38,80,128]{3,2,1,0:T(8,128)S(1)}, f32[2,38,80,128]{3,2,1,0:T(8,128)S(1)}, f32[2,38,80,128]{3,2,1,0:T(8,128)S(1)}, f32[2,38,80,128]{3,2,1,0:T(8,128)S(1)}) custom-call(f32[2,32,64,128]{3,2,1,0:T(8,128)S(1)} %pad_maximum_fusion.fields, f32[320,128]{1,0:T(8,128)S(1)} %get-tuple-element.28.packed), custom_call_target="tpu_custom_call" | custom-call | tf_op jit(solution)/shard_map/pallas_call | solution.py:226
  17.3 0.0 collective-permute-done.1.depth_b.refs_6_
  17.3 0.0 collective-permute-done.depth_a.refs_5_
  17.4 0.1 collective-permute-start.5
  17.5 1.2 %collective-permute-start.4 = (f32[60,128]{1,0:T(8,128)S(1)}, f32[60,128]{1,0:T(8,128)S(1)}, u32[]{:S(2)}, u32[]{:S(2)}) collective-permute-start(f32[60,128]{1,0:T(8,128)S(1)} %get-tuple-element.34.refs_7_), channel_id=1, source_target_pairs={{0,1},{1,0},{2,3},{3,2},{4,5},{5,4},{6,7},{7,6},{8,9},{9,8},{10,11... | collective-permute-start | bytes 92168 | tf_op jit(solution)/shard_map/ppermute | solution.py:518
  19.3 2.2 %shard_map.61 = (f32[2,38,80,128]{3,2,1,0:T(8,128)S(1)}, f32[2,38,80,128]{3,2,1,0:T(8,128)S(1)}, f32[2,38,80,128]{3,2,1,0:T(8,128)S(1)}, f32[2,38,80,128]{3,2,1,...) custom-call(f32[2,38,80,128]{3,2,1,0:T(8,128)S(1)} %get-tuple-elemen, ...), custom_call_target="tpu_custom_call", output_to_operand_aliasing={{0}: (0, {}), {1}: (1, {}), {2}: (2, {}), {3}: (3, {}), {4}... | custom-call | flops 40000000 | bytes 1048576 | tf_op jit(solution)/shard_map/pallas_call | solution.py:254
  21.5 0.0 collective-permute-done.3.refs_7_
  21.5 0.0 collective-permute-done.2.refs_6_
  21.5 0.0 collective-permute-done.5.refs_9_
  21.5 0.0 collective-permute-done.4.refs_8_
  21.5 2.6 %shard_map.62 = (f32[16,4,8,128]{3,2,1,0:T(8,128)S(1)}, f32[16,4,8,128]{3,2,1,0:T(8,128)S(1)}, f32[2,38,80,128]{3,2,1,0:T(8,128)S(1)}, f32[2,38,80,128]{3,2,1,0:...) custom-call(f32[2,38,80,128]{3,2,1,0:T(8,128)S(1)} %get-tuple-elemen, ...), custom_call_target="tpu_custom_call", output_to_operand_aliasing={{2}: (0, {}), {3}: (1, {}), {4}: (2, {}), {5}: (3, {}), {6}... | custom-call | tf_op jit(solution)/shard_map/pallas_call | solution.py:369
  24.2 0.1 collective-permute-start.6
  24.3 1.3 %shard_map.63 = (f32[32,64,128]{2,1,0:T(8,128)}, f32[32,64,128]{2,1,0:T(8,128)}, f32[8,128]{1,0:T(8,128)S(1)}) custom-call(f32[2,38,80,128]{3,2,1,0:T(8,128)S(1)} %get-tuple-element.43.field, f32[16,4,8,128]{3,2,1,0:T(8,128)S(1)} %get-tuple-element.44.part.mine), custom_call_target="tpu_custom_call" | custom-call | tf_op jit(solution)/shard_map/pallas_call | solution.py:397
  25.6 0.2 collective-permute-done.6.theirs
  25.9 0.1 collective-permute-start.7
  26.0 0.1 collective-permute-start.8
  26.1 4.6 %collective-permute-start.9 = (f32[4,4,8,128]{3,2,1,0:T(8,128)S(1)}, f32[4,4,8,128]{3,2,1,0:T(8,128)S(1)}, u32[]{:S(2)}, u32[]{:S(2)}) collective-permute-start(f32[4,4,8,128]{3,2,1,0:T(8,128)S(1)} %get-tuple-element.52), channel_id=1, source_target_pairs={{0,24},{4,28},{8,16},{12,20},{16,8},{20,12},{24,0},{28,4},{32,56},... | collective-permute-start | bytes 196616 | tf_op jit(solution)/shard_map/ppermute | solution.py:523
  30.6 0.3 collective-permute-done.7.refs_1_
  30.9 1.0 %collective-permute-done.8.refs_2_ = f32[4,4,8,128]{3,2,1,0:T(8,128)S(1)} collective-permute-done((f32[4,4,8,128]{3,2,1,0:T(8,128)S(1)}, f32[4,4,8,128]{3,2,1,0:T(8,128)S(1)}, u32[]{:S(2)}, u32[]{:S(2)}) %collective-permute-start.8) | collective-permute-done | bytes 65568 | tf_op jit(solution)/shard_map/ppermute | solution.py:523
  32.0 1.3 %collective-permute-done.9.refs_3_ = f32[4,4,8,128]{3,2,1,0:T(8,128)S(1)} collective-permute-done((f32[4,4,8,128]{3,2,1,0:T(8,128)S(1)}, f32[4,4,8,128]{3,2,1,0:T(8,128)S(1)}, u32[]{:S(2)}, u32[]{:S(2)}) %collective-permute-start.9) | collective-permute-done | bytes 65568 | tf_op jit(solution)/shard_map/ppermute | solution.py:523
  33.3 0.1 shard_map.65
  33.4 14.9 %all_to_all.5.slabs = f32[8,2,8,128]{3,2,1,0:T(8,128)S(1)} all-to-all(f32[8,2,8,128]{3,2,1,0:T(8,128)S(1)} %shard_map.65), channel_id=1, replica_groups={{0,32,64,96,128,160,192,224},{4,36,68,100,132,164,196,228},{8,40,72,104..., dimensions={0} | all-to-all | bytes 131072 | tf_op jit(solution)/shard_map/all_to_all | solution.py:530
  48.4 0.8 %shard_map.66 = f32[4,8,64]{2,1,0:T(8,128)} custom-call(f32[8,2,8,128]{3,2,1,0:T(8,128)S(1)} %all_to_all.5.slabs), custom_call_target="tpu_custom_call" | custom-call | tf_op jit(solution)/shard_map/pallas_call | solution.py:489
  (2 shorter events, 0.1 us)
Async XLA Ops:
  0.6 9.0 %copy-start = (f32[32,64,128]{2,1,0:T(8,128)S(1)}, f32[32,64,128]{2,1,0:T(8,128)}, u32[]{:S(2)}) copy-start(f32[32,64,128]{2,1,0:T(8,128)} %param.4) | copy-start | bytes 3145732
  0.6 9.0 %copy-start.1 = (f32[32,64,128]{2,1,0:T(8,128)S(1)}, f32[32,64,128]{2,1,0:T(8,128)}, u32[]{:S(2)}) copy-start(f32[32,64,128]{2,1,0:T(8,128)} %param.3) | copy-start | bytes 3145732
  2.1 15.3 %collective-permute-start.1 = (f32[2,3,64,128]{3,2,1,0:T(8,128)S(1)}, f32[2,3,64,128]{3,2,1,0:T(8,128)S(1)}, u32[]{:S(2)}, u32[]{:S(2)}) collective-permute-start(f32[2,3,64,128]{3,2,1,0:T(8,128)S(1)} %get-tuple-element.53), channel_id=1, source_target_pairs={{4,8},{8,4},{12,16},{16,12},{20,24},{24,20},{28,32},{32,28},{36,40... | collective-permute-start | bytes 589832 | tf_op jit(solution)/shard_map/ppermute | solution.py:513
  9.6 7.7 %collective-permute-start = (f32[2,3,64,128]{3,2,1,0:T(8,128)S(1)}, f32[2,3,64,128]{3,2,1,0:T(8,128)S(1)}, u32[]{:S(2)}, u32[]{:S(2)}) collective-permute-start(f32[2,3,64,128]{3,2,1,0:T(8,128)S(1)} %get-tuple-element.54), channel_id=1, source_target_pairs={{0,4},{4,0},{8,12},{12,8},{16,20},{20,16},{24,28},{28,24},{32,36},... | collective-permute-start | bytes 589832 | tf_op jit(solution)/shard_map/ppermute | solution.py:513
  10.0 11.5 %collective-permute-start.3 = (f32[320,128]{1,0:T(8,128)S(1)}, f32[320,128]{1,0:T(8,128)S(1)}, u32[]{:S(2)}, u32[]{:S(2)}) collective-permute-start(f32[320,128]{1,0:T(8,128)S(1)} %get-tuple-element.41), channel_id=1, source_target_pairs={{1,2},{2,1},{3,0},{0,3},{5,6},{6,5},{7,4},{4,7},{9,10},{10,9},{11,... | collective-permute-start | bytes 491528 | tf_op jit(solution)/shard_map/ppermute | solution.py:515
  11.6 9.9 %collective-permute-start.2 = (f32[320,128]{1,0:T(8,128)S(1)}, f32[320,128]{1,0:T(8,128)S(1)}, u32[]{:S(2)}, u32[]{:S(2)}) collective-permute-start(f32[320,128]{1,0:T(8,128)S(1)} %get-tuple-element.28.packed), channel_id=1, source_target_pairs={{0,1},{1,0},{2,3},{3,2},{4,5},{5,4},{6,7},{7,6},{8,9},{9,8},{10,11... | collective-permute-start | bytes 491528 | tf_op jit(solution)/shard_map/ppermute | solution.py:515
  17.4 4.1 %collective-permute-start.5 = (f32[60,128]{1,0:T(8,128)S(1)}, f32[60,128]{1,0:T(8,128)S(1)}, u32[]{:S(2)}, u32[]{:S(2)}) collective-permute-start(f32[60,128]{1,0:T(8,128)S(1)} %get-tuple-element.42), channel_id=1, source_target_pairs={{1,2},{2,1},{3,0},{0,3},{5,6},{6,5},{7,4},{4,7},{9,10},{10,9},{11,... | collective-permute-start | bytes 92168 | tf_op jit(solution)/shard_map/ppermute | solution.py:518
  17.5 4.1 %collective-permute-start.4 = (f32[60,128]{1,0:T(8,128)S(1)}, f32[60,128]{1,0:T(8,128)S(1)}, u32[]{:S(2)}, u32[]{:S(2)}) collective-permute-start(f32[60,128]{1,0:T(8,128)S(1)} %get-tuple-element.34.refs_7_), channel_id=1, source_target_pairs={{0,1},{1,0},{2,3},{3,2},{4,5},{5,4},{6,7},{7,6},{8,9},{9,8},{10,11... | collective-permute-start | bytes 92168 | tf_op jit(solution)/shard_map/ppermute | solution.py:518
  24.2 1.6 %collective-permute-start.6 = (f32[16,4,8,128]{3,2,1,0:T(8,128)S(1)}, f32[16,4,8,128]{3,2,1,0:T(8,128)S(1)}, u32[]{:S(2)}, u32[]{:S(2)}) collective-permute-start(f32[16,4,8,128]{3,2,1,0:T(8,128)S(1)} %get-tuple-element.47), channel_id=1, source_target_pairs={{0,4},{4,0},{8,12},{12,8},{16,20},{20,16},{24,28},{28,24},{32,36},... | collective-permute-start | bytes 786440 | tf_op jit(solution)/shard_map/ppermute | solution.py:523
  25.9 5.1 %collective-permute-start.7 = (f32[4,4,8,128]{3,2,1,0:T(8,128)S(1)}, f32[4,4,8,128]{3,2,1,0:T(8,128)S(1)}, u32[]{:S(2)}, u32[]{:S(2)}) collective-permute-start(f32[4,4,8,128]{3,2,1,0:T(8,128)S(1)} %get-tuple-element.50), channel_id=1, source_target_pairs={{0,8},{4,12},{8,0},{12,4},{16,24},{20,28},{24,16},{28,20},{32,40},... | collective-permute-start | bytes 196616 | tf_op jit(solution)/shard_map/ppermute | solution.py:523
  26.0 6.0 %collective-permute-start.8 = (f32[4,4,8,128]{3,2,1,0:T(8,128)S(1)}, f32[4,4,8,128]{3,2,1,0:T(8,128)S(1)}, u32[]{:S(2)}, u32[]{:S(2)}) collective-permute-start(f32[4,4,8,128]{3,2,1,0:T(8,128)S(1)} %get-tuple-element.51), channel_id=1, source_target_pairs={{0,16},{4,20},{8,24},{12,28},{16,0},{20,4},{24,8},{28,12},{32,48},... | collective-permute-start | bytes 196616 | tf_op jit(solution)/shard_map/ppermute | solution.py:523
  26.1 7.2 %collective-permute-start.9 = (f32[4,4,8,128]{3,2,1,0:T(8,128)S(1)}, f32[4,4,8,128]{3,2,1,0:T(8,128)S(1)}, u32[]{:S(2)}, u32[]{:S(2)}) collective-permute-start(f32[4,4,8,128]{3,2,1,0:T(8,128)S(1)} %get-tuple-element.52), channel_id=1, source_target_pairs={{0,24},{4,28},{8,16},{12,20},{16,8},{20,12},{24,0},{28,4},{32,56},... | collective-permute-start | bytes 196616 | tf_op jit(solution)/shard_map/ppermute | solution.py:523
